TPU v7x, 32 devices: a whole 2x2x4 slice. The times are simulated.
32 devices in a mesh: fsdp: 8 (over z, core), solve: 4 (over y, x).
Axes of the slice: x: 2, y: 2, z: 4, core: 2. Of those that a mesh axis runs over, the one named last changes fastest.
Arguments:
- inputs: bfloat16 [6144, 8192], P('fsdp', 'solve'), may hold values from -6 to 6
- cotangent: bfloat16 [6144, 8192], P('fsdp', 'solve'), may hold values from -6 to 6
- gate_pre: bfloat16 [6144, 14336], P('fsdp', 'solve'), may hold values from -6 to 6
- up_pre: bfloat16 [6144, 14336], P('fsdp', 'solve'), may hold values from -6 to 6
- down_weight: bfloat16 [14336, 8192], P('solve', 'fsdp'), may hold values from -0.046875 to 0.046875
- proj_model: bfloat16 [8192, 128], P('solve'), may hold values from -0.0625 to 0.0625
- proj_hidden: bfloat16 [14336, 128], P('solve'), may hold values from -0.046875 to 0.046875
- lengths: int32 [24], P('fsdp'), may hold values from 64 to 256
- gram: float32 [8192, 8192], P('fsdp', 'solve'), may hold values from -6 to 6
- inverse_factor: float32 [8192, 8192], P('fsdp', 'solve'), as said below
- queries: float32 [8192, 256], P('solve', 'fsdp'), may hold values from -6 to 6
Outputs:
- new_gram: float32 [8192, 8192], P('fsdp', 'solve')
- whitened: float32 [8192, 256], P(('fsdp', 'solve'))
- scores: float32 [24, 256], replicated
Inputs may be any that keep to these rules, and one draw needn't show every extreme that they name: `inverse_factor`: zero above the diagonal; diagonal entries between 0.5 and 3.
All inputs are finite; a program needn't handle non-finite values.
Results may differ from a plain program's by a relative error of at most 0.0032.
Values may be sent and summed in bfloat16 or wider, within the bound.
No kernel may reach another device: no remote copies, remote signals or barrier semaphores. Data moves between devices by JAX's collectives and lax.ppermute only.
A program may use at most 192 MiB of HBM per device.

v0:
```python
import functools

import jax
import jax.numpy as jnp
from jax import lax
from jax.experimental import pallas as pl
from jax.experimental.pallas import tpu as pltpu
from jax.sharding import PartitionSpec as P


SEQ_LEN = 256
TILE = 256


def tokens_kernel(count, gates, chained, idx, *refs):
    del idx
    cots, refs = refs[:count], refs[count:]
    weights, refs = refs[:count], refs[count:]
    gate_refs, refs = refs[:gates], refs[gates:]
    if chained:
        start, refs = refs[0], refs[1:]
    proj, out = refs

    @pl.when(pl.program_id(0) == 0)
    def _():
        out[...] = start[...] if chained else jnp.zeros_like(out)

    grad = None
    for cot, weight in zip(cots, weights):
        term = lax.dot_general(
            cot[...], weight[...], (((1,), (1,)), ((), ())), preferred_element_type=jnp.float32
        )
        grad = term if grad is None else grad + term
    gate = gate_refs[0][...].astype(jnp.float32)
    for other in gate_refs[1:]:
        gate = gate + other[...].astype(jnp.float32)
    smooth = gate * jax.nn.sigmoid(gate)
    grad_up = (grad * smooth).astype(jnp.bfloat16)
    out[...] += jnp.dot(grad_up, proj[...], preferred_element_type=jnp.float32)


def tokens(idx, cot, weights, gate_parts, start, proj, first, tiles):
    count = len(weights)
    rows = cot.shape[0]
    width = weights[0].shape[1]
    in_specs = [
        pl.BlockSpec(
            (rows, width), functools.partial(lambda k, i, ix: (0, ix[k]), k), pipeline_mode=pl.Buffered(1)
        )
        for k in range(count)
    ]
    in_specs += [pl.BlockSpec((TILE, width), lambda i, ix: (first + i, 0)) for _ in weights]
    for _, shift in gate_parts:
        in_specs.append(pl.BlockSpec((rows, TILE), functools.partial(lambda a, i, ix: (0, a + i), shift)))
    operands = [cot] * count + list(weights) + [part for part, _ in gate_parts]
    whole = pl.BlockSpec((rows, proj.shape[1]), lambda i, ix: (0, 0))
    if start is not None:
        in_specs.append(whole)
        operands.append(start)
    in_specs.append(pl.BlockSpec((TILE, proj.shape[1]), lambda i, ix: (first + i, 0)))
    operands.append(proj)
    return pl.pallas_call(
        functools.partial(tokens_kernel, count, len(gate_parts), start is not None),
        out_shape=jax.ShapeDtypeStruct((rows, proj.shape[1]), jnp.float32),
        grid_spec=pltpu.PrefetchScalarGridSpec(
            num_scalar_prefetch=1,
            grid=(tiles,),
            in_specs=in_specs,
            out_specs=whole,
        ),
        compiler_params=pltpu.CompilerParams(dimension_semantics=("arbitrary",)),
        cost_estimate=pl.CostEstimate(
            flops=2 * rows * TILE * tiles * (count * width + 256),
            bytes_accessed=TILE * tiles * (count * width + 2 * rows) * 2 + rows * count * width * 2,
            transcendentals=rows * TILE * tiles,
        ),
    )(idx, *operands)


def features_kernel(examples, seqs, mirror_of, idx, up, down, other, left_out, right_out, scores):
    f32 = jnp.float32
    pick = lax.broadcasted_iota(jnp.int32, (examples, up.shape[0]), 1)
    row = lax.broadcasted_iota(jnp.int32, (examples, up.shape[0]), 0)
    sel = jnp.zeros(pick.shape, f32)
    for i, j in enumerate(mirror_of):
        for e in range(seqs):
            hit = (pick == 2 * seqs * i + e) | (pick == 2 * seqs * j + seqs + e)
            sel = jnp.where(hit & (row == seqs * i + e), 1.0, sel)
    sel = sel.astype(jnp.bfloat16)

    def split(x):
        high = x.astype(jnp.bfloat16)
        return high, (x - high.astype(f32)).astype(jnp.bfloat16)

    def part(offset, width):
        size = down.shape[1]

        def from_up():
            at = pl.multiple_of(offset - size, 128)
            high, low = split(up[:, pl.ds(at, width)])
            return jnp.dot(sel, high, preferred_element_type=f32) + jnp.dot(
                sel, low, preferred_element_type=f32
            )

        def from_down():
            return down[:, pl.ds(pl.multiple_of(offset, 128), width)]

        return lax.cond(offset >= size, from_up, from_down)

    high, low = split(part(idx[0], left_out.shape[1]))
    left_out[...] = jnp.concatenate([high, low, high], axis=0)
    right = part(idx[1], right_out.shape[1])
    high, low = split(right)
    right_out[...] = jnp.concatenate([high, high, low], axis=0)
    scores[...] = jnp.dot(right, other[...], precision=lax.Precision.HIGHEST, preferred_element_type=f32)


def gram_kernel(scale, gram, left, right, out):
    term = lax.dot_general(
        left[...], right[...], (((0,), (0,)), ((), ())), preferred_element_type=jnp.float32
    )
    out[...] = gram[...] + term * scale


def local(
    n,
    m,
    inputs,
    cotangent,
    gate_pre,
    up_pre,
    down_weight,
    proj_model,
    proj_hidden,
    lengths,
    gram,
    inverse_factor,
    queries,
):
    top = lax.Precision.HIGHEST
    f32 = jnp.float32
    f = lax.axis_index("fsdp")
    s = lax.axis_index("solve")
    rows = inputs.shape[0]
    local_seqs = lengths.shape[0]
    half = proj_model.shape[1] // 2
    h = n // 2
    chips = n // 2
    side = f // h

    def swap(x, axis, size, bit):
        return lax.ppermute(x, axis, [(i, i ^ bit) for i in range(size)])

    mirror_of = [(chips - 1 - i // 2) * 2 + i % 2 for i in range(n)]

    def mirror(x, keep=lambda chip: True):
        pairs = [(i, mirror_of[i]) for i in range(n) if keep(i // 2)]
        return lax.ppermute(x, "fsdp", pairs)

    def inner(chip):
        return chips // 4 <= chip < chips - chips // 4

    blocks = {0: down_weight}
    step = 2
    while step < h:
        blocks.update({k ^ step: swap(v, "fsdp", n, step) for k, v in list(blocks.items())})
        step *= 2
    gate_inner = mirror(gate_pre, inner)
    blocks.update({k ^ 1: swap(v, "fsdp", n, 1) for k, v in list(blocks.items())})
    order = sorted(blocks)
    weights = [blocks[k] for k in order]
    cot_full = lax.all_gather(cotangent, "solve", axis=1, tiled=True)
    part = rows // m
    near = cot_full.shape[1] // 2
    quarter = lax.dynamic_slice(cot_full, (s * part, (1 - side) * near), (part, near))
    quarter = mirror(quarter)
    cot_far = lax.all_gather(quarter, "solve", axis=0, tiled=True)
    tiles = gate_pre.shape[1] // TILE
    share = -(-tiles // 4)
    cuts = list(range(0, tiles, share)) + [tiles]
    gate_outer = []
    for a, b in zip(cuts[:-1], cuts[1:]):
        gate_outer.append(mirror(gate_pre[:, a * TILE : b * TILE], lambda chip: not inner(chip)))

    gate = gate_pre.astype(f32)
    hidden = (gate * jax.nn.sigmoid(gate) * up_pre.astype(f32)).astype(jnp.bfloat16)
    early = jnp.concatenate(
        [
            jnp.dot(hidden, proj_hidden[:, :half], preferred_element_type=f32),
            jnp.dot(cotangent, proj_model[:, :half], preferred_element_type=f32),
            jnp.dot(inputs, proj_model[:, half:], preferred_element_type=f32),
        ],
        axis=1,
    )
    early = lax.psum(early, "solve")

    query_block = lax.all_gather(queries, "fsdp", axis=1, tiled=True)
    partial = jnp.dot(inverse_factor, query_block, precision=top)
    whitened = partial
    bit = m // 2
    while bit:
        size = whitened.shape[0] // 2
        mine = s // bit % 2
        moved = swap(lax.dynamic_slice_in_dim(whitened, (1 - mine) * size, size, 0), "solve", m, bit)
        whitened = lax.dynamic_slice_in_dim(whitened, mine * size, size, 0) + moved
        bit //= 2
    whitened_rows = whitened
    bit = 1
    while bit < m:
        mine = s // bit % 2
        moved = swap(whitened_rows, "solve", m, bit)
        whitened_rows = jnp.where(
            mine == 0,
            jnp.concatenate([whitened_rows, moved], axis=0),
            jnp.concatenate([moved, whitened_rows], axis=0),
        )
        bit *= 2
    query_side = lax.dot_general(
        inverse_factor, whitened_rows, (((0,), (0,)), ((), ())), precision=top
    )

    own_idx = jnp.stack([f ^ k for k in order]).astype(jnp.int32)
    far_idx = own_idx - side * h
    own = tokens(own_idx, cot_full, weights, [(gate_pre, 0)], None, proj_hidden, 0, tiles)
    token_index = lax.broadcasted_iota(jnp.int32, (rows, 1), 0)
    slots = lax.broadcasted_iota(jnp.int32, (1, local_seqs), 1)
    length_of = jnp.sum(
        jnp.where(token_index // SEQ_LEN == slots, lengths[None, :], 0), axis=1, keepdims=True
    )
    weight_of = jnp.where(
        token_index % SEQ_LEN < length_of, 1.0 / jnp.sqrt(length_of.astype(f32)), 0.0
    )
    in_down = early[:, :half]
    out_down = early[:, half : 2 * half] * weight_of
    in_up = early[:, 2 * half :] * weight_of
    in_up_far = mirror(in_up)

    def pair(outs, ins):
        shape = (local_seqs, SEQ_LEN, half)
        feat = jnp.einsum("eto,eti->eoi", outs.reshape(shape), ins.reshape(shape), precision=top)
        return feat.reshape(local_seqs, half * half)

    down_all = lax.all_gather(pair(out_down, in_down), "fsdp", axis=0, tiled=True)
    up_own = pair(own[:, half:], in_up)

    far = None
    for j, (a, b, outer) in enumerate(zip(cuts[:-1], cuts[1:], gate_outer)):
        if j == len(gate_outer) // 2:
            far_idx, query_side = lax.optimization_barrier((far_idx, query_side))
        far = tokens(far_idx, cot_far, weights, [(gate_inner, a), (outer, 0)], far, proj_hidden, a, b - a)
    up_far = pair(far[:, half:], in_up_far)
    up = jnp.concatenate([up_own, up_far], axis=0)
    bit = 1
    while bit < m:
        up = up + swap(up, "solve", m, bit)
        bit *= 2
    up_all = lax.all_gather(up, "fsdp", axis=0, tiled=True)

    examples = n * local_seqs
    row_width = gram.shape[0]
    col_width = gram.shape[1]
    count = queries.shape[1] * n
    at = jnp.stack([f * row_width, s * col_width]).astype(jnp.int32)
    left, right, scores = pl.pallas_call(
        functools.partial(features_kernel, examples, local_seqs, mirror_of),
        out_shape=(
            jax.ShapeDtypeStruct((3 * examples, row_width), jnp.bfloat16),
            jax.ShapeDtypeStruct((3 * examples, col_width), jnp.bfloat16),
            jax.ShapeDtypeStruct((examples, count), f32),
        ),
        in_specs=[pl.BlockSpec(memory_space=pltpu.SMEM)] + [pl.BlockSpec(memory_space=pltpu.VMEM)] * 3,
    )(at, up_all, down_all, query_side)
    total = 2 * half * half
    scores = scores / jnp.sqrt(f32(total))
    for axis, size in (("fsdp", n), ("solve", m)):
        bit = 1
        while bit < size:
            scores = scores + swap(scores, axis, size, bit)
            bit *= 2
    block = 128
    new_gram = pl.pallas_call(
        functools.partial(gram_kernel, 1.0 / examples),
        out_shape=jax.ShapeDtypeStruct(gram.shape, f32),
        grid=(row_width // block,),
        in_specs=[
            pl.BlockSpec((block, col_width), lambda i: (i, 0)),
            pl.BlockSpec((3 * examples, block), lambda i: (0, i)),
            pl.BlockSpec((3 * examples, col_width), lambda i: (0, 0)),
        ],
        out_specs=pl.BlockSpec((block, col_width), lambda i: (i, 0)),
    )(gram, left, right)
    return (new_gram, whitened, scores)


def solution(mesh):
    in_specs = (
        P("fsdp", "solve"),
        P("fsdp", "solve"),
        P("fsdp", "solve"),
        P("fsdp", "solve"),
        P("solve", "fsdp"),
        P("solve", None),
        P("solve", None),
        P("fsdp"),
        P("fsdp", "solve"),
        P("fsdp", "solve"),
        P("solve", "fsdp"),
    )
    out_specs = (P("fsdp", "solve"), P(("fsdp", "solve"), None), P())

    def body(*args):
        return local(mesh.shape["fsdp"], mesh.shape["solve"], *args)

    return jax.shard_map(body, mesh=mesh, in_specs=in_specs, out_specs=out_specs, check_vma=False)
```

profile of v0, /device:TPU:0, one launch (start us, length us, event | category | flops | bytes accessed | tf_op | source)
XLA Modules:
  0.0 614.5 jit_solution(6697453166689645880)
XLA Ops:
  8.0 3.1 collective-permute-start.1
  11.2 123.8 %all-gather.6.cloned.1.call-done.refs_0_.refs_1_.refs_2_.refs_3_ = bf16[768,8192]{1,0:T(8,128)(2,1)} async-done(((bf16[768,2048]{1,0:T(8,128)(2,1)}), bf16[768,8192]{1,0:T(8,128)(2,1)}) %all-gather.6.cloned.1.call-update) | async-done | bytes 12582928 | tf_op jit(solution)/shard_map/all_gather | solution.py:172
  135.0 2.7 dynamic_slice.19
  137.7 3.3 collective-permute-start.7
  141.0 6.7 %fusion.5 = f32[768,64]{0,1:T(8,128)S(1)} fusion(bf16[768,3584]{1,0:T(8,128)(2,1)} %param.14, bf16[768,3584]{1,0:T(8,128)(2,1)} %refs_8_.1, bf16[3584,128]{1,0:T(8,128)(2,1)} %refs_11_.5), kind=kOutput, calls=%fused_computation.7 | convolution fusion | flops 374341632 | bytes 12124160 | tf_op jit(solution)/shard_map/dot_general | solution.py:189
  147.8 1.1 fusion.15
  148.9 1.2 fusion.13
  151.1 35.5 %collective-permute-done.1.refs_6_ = bf16[3584,1024]{1,0:T(8,128)(2,1)} collective-permute-done((bf16[3584,1024]{1,0:T(8,128)(2,1)}, bf16[3584,1024]{1,0:T(8,128)(2,1)}, u32[]{:S(2)}, u32[]{:S(2)}) %collective-permute-start.1) | collective-permute-done | bytes 7340064 | tf_op jit(solution)/shard_map/ppermute | solution.py:152
  186.6 35.6 %collective-permute-done.7 = bf16[192,4096]{1,0:T(8,128)(2,1)} collective-permute-done((bf16[192,4096]{1,0:T(8,128)(2,1)}, bf16[192,4096]{1,0:T(8,128)(2,1)}, u32[]{:S(2)}, u32[]{:S(2)}) %collective-permute-start.7) | collective-permute-done | bytes 1572896 | tf_op jit(solution)/shard_map/ppermute | solution.py:158
  222.3 9.5 %fusion.40 = f32[1024,256]{1,0:T(8,128)S(1)} fusion(f32[1024,2048]{1,0:T(8,128)} %param.20, f32[2048,256]{0,1:T(8,128)} %all-gather.8.cloned.1.call-done), kind=kOutput, calls=%fused_computation.65 | convolution fusion | flops 6442450944 | bytes 11534336 | tf_op jit(solution)/shard_map/dot_general | solution.py:198
  231.8 1.6 collective-permute-start.3
  233.4 3.1 collective-permute-start.8
  236.5 9.7 %collective-permute-done.3 = f32[512,256]{1,0:T(8,128)S(1)} collective-permute-done((f32[512,256]{1,0:T(8,128)S(1)}, f32[512,256]{1,0:T(8,128)S(1)}, u32[]{:S(2)}, u32[]{:S(2)}) %collective-permute-start.3) | collective-permute-done | bytes 524320 | tf_op jit(solution)/shard_map/ppermute | solution.py:152
  246.3 1.1 collective-permute-start.4
  247.4 4.5 fusion.39
  251.9 4.1 collective-permute-start.12
  256.1 4.1 collective-permute-done.4
  260.2 1.1 collective-permute-start.5
  262.1 10.0 %collective-permute-done.5 = f32[256,256]{1,0:T(8,128)S(1)} collective-permute-done((f32[256,256]{1,0:T(8,128)S(1)}, f32[256,256]{1,0:T(8,128)S(1)}, u32[]{:S(2)}, u32[]{:S(2)}) %collective-permute-start.5) | collective-permute-done | bytes 262176 | tf_op jit(solution)/shard_map/ppermute | solution.py:152
  272.1 1.5 collective-permute-start.6
  274.3 2.1 slice.41
  276.4 2.1 slice_multiply_fusion
  278.5 11.6 %collective-permute-done.6 = f32[512,256]{1,0:T(8,128)S(1)} collective-permute-done((f32[512,256]{1,0:T(8,128)S(1)}, f32[512,256]{1,0:T(8,128)S(1)}, u32[]{:S(2)}, u32[]{:S(2)}) %collective-permute-start.6) | collective-permute-done | bytes 524320 | tf_op jit(solution)/shard_map/ppermute | solution.py:152
  290.1 8.6 %collective-permute-start.11 = (bf16[768,1024]{1,0:T(8,128)(2,1)}, bf16[768,1024]{1,0:T(8,128)(2,1)}, u32[]{:S(2)}, u32[]{:S(2)}) collective-permute-start(bf16[768,1024]{1,0:T(8,128)(2,1)} %get-tuple-element.17), channel_id=1, source_target_pairs={{0,24},{4,28},{24,0},{28,4},{1,25},{5,29},{25,1},{29,5},{2,26},{6,... | collective-permute-start | bytes 4718600 | tf_op jit(solution)/shard_map/ppermute | solution.py:158
  298.7 16.6 %convolution_bitcast_fusion.other = f32[2048,256]{1,0:T(8,128)} fusion(f32[1024,2048]{1,0:T(8,128)} %param.20, f32[512,256]{1,0:T(8,128)S(1)} %collective-permute-done.6, f32[512,256]{1,0:T(8,128)S(1)} %maximum_select_fusion.2, pred[]{:T(512)S(6)} %eq.29), kind=kOutput, calls=%fused_computation.8 | convolution fusion | flops 6443237376 | bytes 11534337 | tf_op jit(solution)/shard_map/dot_general | solution.py:218
  315.3 1.9 collective-permute-start.10
  317.2 5.9 collective-permute-start.9
  323.2 34.8 %shard_map.130 = f32[768,128]{1,0:T(8,128)} custom-call(s32[4]{0:T(128)} %get-tuple-element.14.idx, bf16[768,8192]{1,0:T(8,128)(2,1)} %all-gather.6.cloned.1.call-done.refs_0_.refs_1_.refs_2_.refs_3_, bf16[768,8192]{1,0:T(8,128)(2,1)} %all-gather.6.cloned.1.call-done.refs_0_.refs_1_.refs_2_.refs_3_, ...), custom_call_target="tpu_custom_call" | custom-call | flops 23957864448 | bytes 46661632 | tf_op jit(solution)/shard_map/pallas_call | solution.py:62
  358.0 1.2 slice.48
  360.2 14.0 %shard_map.131.refs_10_ = f32[768,128]{1,0:T(8,128)} custom-call(s32[4]{0:T(128)} %get-tuple-element.8.idx, bf16[768,4096]{1,0:T(8,128)(2,1)} %all-gather.10.cloned.1.call-done.refs_0_.refs_1_.refs_2_.refs_3_, bf16[768,4096]{1,0:T(8,128)(2,1)} %all-gather.10.cloned.1.call-done.refs_0_.refs_1_.refs_2_.refs_3_, ...), custom_call_target="tpu_custom_call" | custom-call | flops 6845104128 | bytes 17825792 | tf_op jit(solution)/shard_map/pallas_call | solution.py:62
  374.2 14.1 %shard_map.132.refs_10_ = f32[768,128]{1,0:T(8,128)} custom-call(s32[4]{0:T(128)} %get-tuple-element.8.idx, bf16[768,4096]{1,0:T(8,128)(2,1)} %all-gather.10.cloned.1.call-done.refs_0_.refs_1_.refs_2_.refs_3_, bf16[768,4096]{1,0:T(8,128)(2,1)} %all-gather.10.cloned.1.call-done.refs_0_.refs_1_.refs_2_.refs_3_, ...), custom_call_target="tpu_custom_call" | custom-call | flops 6845104128 | bytes 17825792 | tf_op jit(solution)/shard_map/pallas_call | solution.py:62
  388.2 14.0 %shard_map.133.refs_10_ = f32[768,128]{1,0:T(8,128)} custom-call(s32[4]{0:T(128)} %get-tuple-element.8.idx, bf16[768,4096]{1,0:T(8,128)(2,1)} %all-gather.10.cloned.1.call-done.refs_0_.refs_1_.refs_2_.refs_3_, bf16[768,4096]{1,0:T(8,128)(2,1)} %all-gather.10.cloned.1.call-done.refs_0_.refs_1_.refs_2_.refs_3_, ...), custom_call_target="tpu_custom_call" | custom-call | flops 6845104128 | bytes 17825792 | tf_op jit(solution)/shard_map/pallas_call | solution.py:62
  403.1 9.8 %shard_map.134 = f32[768,128]{1,0:T(8,128)} custom-call(s32[4]{0:T(128)} %get-tuple-element.8.idx, bf16[768,4096]{1,0:T(8,128)(2,1)} %all-gather.10.cloned.1.call-done.refs_0_.refs_1_.refs_2_.refs_3_, bf16[768,4096]{1,0:T(8,128)(2,1)} %all-gather.10.cloned.1.call-done.refs_0_.refs_1_.refs_2_.refs_3_, ...), custom_call_target="tpu_custom_call" | custom-call | flops 3422552064 | bytes 12058624 | tf_op jit(solution)/shard_map/pallas_call | solution.py:62
  412.9 1.2 slice.50
  414.1 1.7 fusion.23
  416.5 4.5 collective-permute-done.14
  421.0 2.4 collective-permute-start.15
  423.5 134.3 %all-gather.1 = f32[8,3,4096]{2,1,0:T(4,128)S(1)} all-gather(f32[1,3,4096]{2,1,0:T(4,128)S(1)} %reshape.108), channel_id=1, replica_groups=mesh['fsdp'=8,'solve'=4] {'fsdp'}, dimensions={0}, use_global_device_ids=true | all-gather | bytes 442368 | tf_op jit(solution)/shard_map/all_gather | solution.py:243
  557.7 1.0 reshape.109.down
  558.7 17.0 %all-gather = f32[8,6,4096]{2,1,0:T(8,128)S(1)} all-gather(f32[1,6,4096]{2,1,0:T(8,128)S(1)} %add_bitcast_fusion), channel_id=1, replica_groups=mesh['fsdp'=8,'solve'=4] {'fsdp'}, dimensions={0}, use_global_device_ids=true | all-gather | bytes 884736 | tf_op jit(solution)/shard_map/all_gather | solution.py:257
  575.7 1.0 reshape.107.up
  576.7 3.7 shard_map.135
  583.1 3.8 collective-permute-done.17
  587.8 3.8 collective-permute-done.18
  591.7 1.5 collective-permute-start.19
  593.1 2.4 collective-permute-done.19
  595.5 1.7 collective-permute-start.20
  597.2 10.1 %shard_map.136 = f32[1024,2048]{1,0:T(8,128)} custom-call(f32[1024,2048]{1,0:T(8,128)} %gram.1, bf16[72,1024]{1,0:T(8,128)(2,1)} %get-tuple-element.10.left, bf16[72,2048]{1,0:T(8,128)(2,1)} %get-tuple-element.11.right), custom_call_target="tpu_custom_call" | custom-call | tf_op jit(solution)/shard_map/pallas_call | solution.py:281
  (70 shorter events, 10.3 us)
Async XLA Ops:
  7.2 141.7 %copy-start = (bf16[768,2048]{1,0:T(8,128)(2,1)S(1)}, bf16[768,2048]{1,0:T(8,128)(2,1)}, u32[]{:S(2)}) copy-start(bf16[768,2048]{1,0:T(8,128)(2,1)} %param.11) | copy-start | bytes 9437188
  7.2 127.8 %all-gather.6.cloned.1.call-start = ((), (), s32[]{:S(2)}) async-start(), calls=%async_computation | async-start | bytes 15728640 | tf_op jit(solution)/shard_map/all_gather | solution.py:172
  7.9 214.4 %all-gather.8.cloned.1.call-start = ((), (), s32[]{:S(2)}) async-start(), calls=%async_computation.2 | async-start | bytes 2359296 | tf_op jit(solution)/shard_map/all_gather | solution.py:197
  8.0 178.7 %collective-permute-start.1 = (bf16[3584,1024]{1,0:T(8,128)(2,1)}, bf16[3584,1024]{1,0:T(8,128)(2,1)}, u32[]{:S(2)}, u32[]{:S(2)}) collective-permute-start(bf16[3584,1024]{1,0:T(8,128)(2,1)} %refs_4_.9), channel_id=1, source_target_pairs={{0,8},{4,12},{8,0},{12,4},{16,24},{20,28},{24,16},{28,20},{1,9},{5... | collective-permute-start | bytes 22020104 | tf_op jit(solution)/shard_map/ppermute | solution.py:152
  11.1 265.3 %all-reduce.2.cloned.1.call-start = ((), (), s32[]{:S(2)}) async-start(), calls=%async_computation.1 | async-start | bytes 1179648 | tf_op jit(solution)/shard_map/psum | solution.py:195
  137.7 10.1 %copy-start.2 = (bf16[768,2048]{1,0:T(8,128)(2,1)S(1)}, bf16[768,2048]{1,0:T(8,128)(2,1)}, u32[]{:S(2)}) copy-start(bf16[768,2048]{1,0:T(8,128)(2,1)} %param.12) | copy-start | bytes 9437188
  137.7 10.1 %copy-start.3 = (bf16[2048,128]{1,0:T(8,128)(2,1)S(1)}, bf16[2048,128]{1,0:T(8,128)(2,1)}, u32[]{:S(2)}) copy-start(bf16[2048,128]{1,0:T(8,128)(2,1)} %param.16) | copy-start | bytes 1572868
  137.7 84.5 %collective-permute-start.7 = (bf16[192,4096]{1,0:T(8,128)(2,1)}, bf16[192,4096]{1,0:T(8,128)(2,1)}, u32[]{:S(2)}, u32[]{:S(2)}) collective-permute-start(bf16[192,4096]{1,0:T(8,128)(2,1)} %dynamic_slice.19), channel_id=1, source_target_pairs={{0,24},{4,28},{8,16},{12,20},{16,8},{20,12},{24,0},{28,4},{1,25},{... | collective-permute-start | bytes 4718600 | tf_op jit(solution)/shard_map/ppermute | solution.py:158
  150.9 209.3 %all-gather.10.cloned.1.call-start = ((), (), s32[]{:S(2)}) async-start(), calls=%async_computation.3 | async-start | bytes 7864320 | tf_op jit(solution)/shard_map/all_gather | solution.py:177
  151.0 164.3 %collective-permute-start = (bf16[3584,1024]{1,0:T(8,128)(2,1)}, bf16[3584,1024]{1,0:T(8,128)(2,1)}, u32[]{:S(2)}, u32[]{:S(2)}) collective-permute-start(bf16[3584,1024]{1,0:T(8,128)(2,1)} %refs_4_.9), channel_id=1, source_target_pairs={{0,4},{4,0},{8,12},{12,8},{16,20},{20,16},{24,28},{28,24},{1,5},{5... | collective-permute-start | bytes 22020104 | tf_op jit(solution)/shard_map/ppermute | solution.py:152
  186.6 130.6 %collective-permute-start.2 = (bf16[3584,1024]{1,0:T(8,128)(2,1)}, bf16[3584,1024]{1,0:T(8,128)(2,1)}, u32[]{:S(2)}, u32[]{:S(2)}) collective-permute-start(bf16[3584,1024]{1,0:T(8,128)(2,1)} %collective-permute-done.1.refs_6_), channel_id=1, source_target_pairs={{0,4},{4,0},{8,12},{12,8},{16,20},{20,16},{24,28},{28,24},{1,5},{5... | collective-permute-start | bytes 22020104 | tf_op jit(solution)/shard_map/ppermute | solution.py:152
  231.8 14.3 %collective-permute-start.3 = (f32[512,256]{1,0:T(8,128)S(1)}, f32[512,256]{1,0:T(8,128)S(1)}, u32[]{:S(2)}, u32[]{:S(2)}) collective-permute-start(f32[512,256]{1,0:T(8,128)S(1)} %constant_dynamic-slice_fusion.1), channel_id=1, source_target_pairs={{0,2},{1,3},{2,0},{3,1},{4,6},{5,7},{6,4},{7,5},{8,10},{9,11},{10,... | collective-permute-start | bytes 1572872 | tf_op jit(solution)/shard_map/ppermute | solution.py:152
  233.4 126.8 %collective-permute-start.8 = (bf16[768,3584]{1,0:T(8,128)(2,1)}, bf16[768,3584]{1,0:T(8,128)(2,1)}, u32[]{:S(2)}, u32[]{:S(2)}) collective-permute-start(bf16[768,3584]{1,0:T(8,128)(2,1)} %refs_8_.1), channel_id=1, source_target_pairs={{8,16},{12,20},{16,8},{20,12},{9,17},{13,21},{17,9},{21,13},{10,18... | collective-permute-start | bytes 16515080 | tf_op jit(solution)/shard_map/ppermute | solution.py:158
  246.2 15.7 %copy-start.7 = (s32[3]{0:T(128)S(1)}, s32[3]{0:T(128)}, u32[]{:S(2)}) copy-start(s32[3]{0:T(128)} %param.18) | copy-start | bytes 40
  246.3 13.8 %collective-permute-start.4 = (f32[256,256]{1,0:T(8,128)S(1)}, f32[256,256]{1,0:T(8,128)S(1)}, u32[]{:S(2)}, u32[]{:S(2)}) collective-permute-start(f32[256,256]{1,0:T(8,128)S(1)} %constant_dynamic-slice_fusion), channel_id=1, source_target_pairs={{0,1},{1,0},{2,3},{3,2},{4,5},{5,4},{6,7},{7,6},{8,9},{9,8},{10,11... | collective-permute-start | bytes 786440 | tf_op jit(solution)/shard_map/ppermute | solution.py:152
  251.9 108.2 %collective-permute-start.12 = (bf16[768,1024]{1,0:T(8,128)(2,1)}, bf16[768,1024]{1,0:T(8,128)(2,1)}, u32[]{:S(2)}, u32[]{:S(2)}) collective-permute-start(bf16[768,1024]{1,0:T(8,128)(2,1)} %get-tuple-element.15), channel_id=1, source_target_pairs={{0,24},{4,28},{24,0},{28,4},{1,25},{5,29},{25,1},{29,5},{2,26},{6,... | collective-permute-start | bytes 4718600 | tf_op jit(solution)/shard_map/ppermute | solution.py:158
  260.2 55.1 %copy-start.4 = (f32[256,256]{1,0:T(8,128)}, f32[256,256]{1,0:T(8,128)S(1)}, u32[]{:S(2)}) copy-start(f32[256,256]{1,0:T(8,128)S(1)} %dynamic-slice_add_fusion.1) | copy-start | bytes 786436
  260.2 11.9 %collective-permute-start.5 = (f32[256,256]{1,0:T(8,128)S(1)}, f32[256,256]{1,0:T(8,128)S(1)}, u32[]{:S(2)}, u32[]{:S(2)}) collective-permute-start(f32[256,256]{1,0:T(8,128)S(1)} %dynamic-slice_add_fusion.1), channel_id=1, source_target_pairs={{0,1},{1,0},{2,3},{3,2},{4,5},{5,4},{6,7},{7,6},{8,9},{9,8},{10,11... | collective-permute-start | bytes 786440 | tf_op jit(solution)/shard_map/ppermute | solution.py:152
  272.1 18.0 %collective-permute-start.6 = (f32[512,256]{1,0:T(8,128)S(1)}, f32[512,256]{1,0:T(8,128)S(1)}, u32[]{:S(2)}, u32[]{:S(2)}) collective-permute-start(f32[512,256]{1,0:T(8,128)S(1)} %maximum_select_fusion.2), channel_id=1, source_target_pairs={{0,2},{1,3},{2,0},{3,1},{4,6},{5,7},{6,4},{7,5},{8,10},{9,11},{10,... | collective-permute-start | bytes 1572872 | tf_op jit(solution)/shard_map/ppermute | solution.py:152
  290.1 84.1 %collective-permute-start.11 = (bf16[768,1024]{1,0:T(8,128)(2,1)}, bf16[768,1024]{1,0:T(8,128)(2,1)}, u32[]{:S(2)}, u32[]{:S(2)}) collective-permute-start(bf16[768,1024]{1,0:T(8,128)(2,1)} %get-tuple-element.17), channel_id=1, source_target_pairs={{0,24},{4,28},{24,0},{28,4},{1,25},{5,29},{25,1},{29,5},{2,26},{6,... | collective-permute-start | bytes 4718600 | tf_op jit(solution)/shard_map/ppermute | solution.py:158
  315.3 72.9 %collective-permute-start.10 = (bf16[768,1024]{1,0:T(8,128)(2,1)S(1)}, bf16[768,1024]{1,0:T(8,128)(2,1)}, u32[]{:S(2)}, u32[]{:S(2)}) collective-permute-start(bf16[768,1024]{1,0:T(8,128)(2,1)S(1)} %get-tuple-element.16), channel_id=1, source_target_pairs={{0,24},{4,28},{24,0},{28,4},{1,25},{5,29},{25,1},{29,5},{2,26},{6,... | collective-permute-start | bytes 4718600 | tf_op jit(solution)/shard_map/ppermute | solution.py:158
  317.2 85.0 %collective-permute-start.9 = (bf16[768,512]{1,0:T(8,128)(2,1)}, bf16[768,512]{1,0:T(8,128)(2,1)S(1)}, u32[]{:S(2)}, u32[]{:S(2)}) collective-permute-start(bf16[768,512]{1,0:T(8,128)(2,1)} %slice.41), channel_id=1, source_target_pairs={{0,24},{4,28},{24,0},{28,4},{1,25},{5,29},{25,1},{29,5},{2,26},{6,... | collective-permute-start | bytes 2359304 | tf_op jit(solution)/shard_map/ppermute | solution.py:158
  323.2 36.0 %copy-start.6 = (f32[768,64]{0,1:T(8,128)S(1)}, f32[768,64]{0,1:T(8,128)}, u32[]{:S(2)}) copy-start(f32[768,64]{0,1:T(8,128)} %get-tuple-element.19) | copy-start | bytes 589828
  360.1 54.0 %collective-permute-start.13 = (f32[768,64]{0,1:T(8,128)S(1)}, f32[768,64]{0,1:T(8,128)}, u32[]{:S(2)}, u32[]{:S(2)}) collective-permute-start(f32[768,64]{0,1:T(8,128)S(1)} %copy-done.6), channel_id=1, source_target_pairs={{0,24},{4,28},{8,16},{12,20},{16,8},{20,12},{24,0},{28,4},{1,25},{... | collective-permute-start | bytes 589832 | tf_op jit(solution)/shard_map/ppermute | solution.py:158
  402.3 0.9 copy-start.5
  416.0 5.0 collective-permute-start.14
  421.0 137.6 %collective-permute-start.15 = (f32[6,4096]{1,0:T(8,128)S(1)}, f32[6,4096]{1,0:T(8,128)S(1)}, u32[]{:S(2)}, u32[]{:S(2)}) collective-permute-start(f32[6,4096]{1,0:T(8,128)S(1)} %fusion.38), channel_id=1, source_target_pairs={{0,2},{1,3},{2,0},{3,1},{4,6},{5,7},{6,4},{7,5},{8,10},{9,11},{10,... | collective-permute-start | bytes 294920 | tf_op jit(solution)/shard_map/ppermute | solution.py:152
  581.2 1.2 collective-permute-start.16
  583.1 3.8 collective-permute-start.17
  586.9 4.7 collective-permute-start.18
  591.7 3.8 collective-permute-start.19
  595.5 11.8 %collective-permute-start.20 = (f32[24,256]{1,0:T(8,128)S(1)}, f32[24,256]{1,0:T(8,128)S(1)}, u32[]{:S(2)}, u32[]{:S(2)}) collective-permute-start(f32[24,256]{1,0:T(8,128)S(1)} %add.96), channel_id=1, source_target_pairs={{0,2},{1,3},{2,0},{3,1},{4,6},{5,7},{6,4},{7,5},{8,10},{9,11},{10,... | collective-permute-start | bytes 73736 | tf_op jit(solution)/shard_map/ppermute | solution.py:152
  597.2 10.7 %copy-start.1 = (bf16[768,2048]{1,0:T(8,128)(2,1)S(1)}, bf16[768,2048]{1,0:T(8,128)(2,1)}, u32[]{:S(2)}) copy-start(bf16[768,2048]{1,0:T(8,128)(2,1)} %param.11) | copy-start | bytes 9437188
Sparse Core Ops, SparseCore 0:
  9.8 125.0 all-gather.5
  136.6 41.8 all-gather.7
  181.5 49.5 all-reduce.1
  232.8 83.4 all-gather.9
where the time goes:
time: 615 us; the launch traced here: 614 us
  waiting for transfers between devices  246 us (40%)
  blocking collectives  151 us (25%)
  Pallas kernels  100 us (16%)
  starting transfers between devices  42.7 us (7%)
  matrix products  37.8 us (6%)
  local copies, waits for them, and re-layouts  14.9 us (2%)
  between operations  14.1 us (2%)
  other arithmetic  6.74 us (1%)
    all_gather x1, blocking collectives, local(): lax.all_gather(pair(out_down, in_down), 'fsdp', axis=0, tiled=True)  134 us
    all_gather x1, waiting for transfers between devices, local(): cot_full = lax.all_gather(cotangent, 'solve', axis=1, tiled=True)  124 us
    pallas_call x5, Pallas kernels, tokens(): pl.pallas_call(functools.partial(tokens_kernel, count, len(gate_parts), s...  86.6 us
    ppermute x14, waiting for transfers between devices, swap(): return lax.ppermute(x, axis, [(i, i ^ bit) for i in range(size)])  86.3 us
    ppermute x7, waiting for transfers between devices, mirror(): return lax.ppermute(x, 'fsdp', pairs)  35.6 us
    ppermute x7, starting transfers between devices, mirror(): return lax.ppermute(x, 'fsdp', pairs)  27 us
    all_gather x1, blocking collectives, local(): up_all = lax.all_gather(up, 'fsdp', axis=0, tiled=True)  17 us
    dot_general x1, matrix products, local(): lax.dot_general(inverse_factor, whitened_rows, (((0,), (0,)), ((), ())),...  16.6 us
  transfers between devices with their start and end apart: 25, of which 12 were waited for; matrix products, arithmetic and copies ran while one was open for 9% of the time, Pallas kernels for 16%

commit v1 on v0

--- a/solution.py
+++ b/solution.py
@@ -42,17 +42,18 @@
 def tokens(idx, cot, weights, gate_parts, start, proj, first, tiles):
     count = len(weights)
     rows = cot.shape[0]
-    width = weights[0].shape[1]
+    width = weights[0][0].shape[1]
     in_specs = [
         pl.BlockSpec(
             (rows, width), functools.partial(lambda k, i, ix: (0, ix[k]), k), pipeline_mode=pl.Buffered(1)
         )
         for k in range(count)
     ]
-    in_specs += [pl.BlockSpec((TILE, width), lambda i, ix: (first + i, 0)) for _ in weights]
+    for _, shift in weights:
+        in_specs.append(pl.BlockSpec((TILE, width), functools.partial(lambda a, i, ix: (a + i, 0), shift)))
     for _, shift in gate_parts:
         in_specs.append(pl.BlockSpec((rows, TILE), functools.partial(lambda a, i, ix: (0, a + i), shift)))
-    operands = [cot] * count + list(weights) + [part for part, _ in gate_parts]
+    operands = [cot] * count + [part for part, _ in weights] + [part for part, _ in gate_parts]
     whole = pl.BlockSpec((rows, proj.shape[1]), lambda i, ix: (0, 0))
     if start is not None:
         in_specs.append(whole)
@@ -115,7 +116,8 @@
     scores[...] = jnp.dot(right, other[...], precision=lax.Precision.HIGHEST, preferred_element_type=f32)
 
 
-def gram_kernel(scale, gram, left, right, out):
+def gram_kernel(scale, gram, left, right, *refs):
+    out = refs[-1]
     term = lax.dot_general(
         left[...], right[...], (((0,), (0,)), ((), ())), preferred_element_type=jnp.float32
     )
@@ -160,15 +162,7 @@
     def inner(chip):
         return chips // 4 <= chip < chips - chips // 4
 
-    blocks = {0: down_weight}
-    step = 2
-    while step < h:
-        blocks.update({k ^ step: swap(v, "fsdp", n, step) for k, v in list(blocks.items())})
-        step *= 2
-    gate_inner = mirror(gate_pre, inner)
-    blocks.update({k ^ 1: swap(v, "fsdp", n, 1) for k, v in list(blocks.items())})
-    order = sorted(blocks)
-    weights = [blocks[k] for k in order]
+    gate_outer = mirror(gate_pre, lambda chip: not inner(chip))
     cot_full = lax.all_gather(cotangent, "solve", axis=1, tiled=True)
     part = rows // m
     near = cot_full.shape[1] // 2
@@ -176,11 +170,24 @@
     quarter = mirror(quarter)
     cot_far = lax.all_gather(quarter, "solve", axis=0, tiled=True)
     tiles = gate_pre.shape[1] // TILE
-    share = -(-tiles // 4)
-    cuts = list(range(0, tiles, share)) + [tiles]
-    gate_outer = []
-    for a, b in zip(cuts[:-1], cuts[1:]):
-        gate_outer.append(mirror(gate_pre[:, a * TILE : b * TILE], lambda chip: not inner(chip)))
+    share = max(1, tiles // 7)
+    cuts = [0, tiles - 3 * share, tiles - share, tiles]
+    sibling = swap(down_weight, "fsdp", n, 1) if h > 1 else None
+    chunks = []
+    for j, (a, b) in enumerate(zip(cuts[:-1], cuts[1:])):
+        blocks = {0: down_weight[a * TILE : b * TILE]}
+        step = 2
+        while step < h:
+            blocks.update({k ^ step: swap(v, "fsdp", n, step) for k, v in list(blocks.items())})
+            step *= 2
+        gate_inner = mirror(gate_pre[:, a * TILE : b * TILE], inner)
+        blocks.update({k ^ 1: swap(v, "fsdp", n, 1) for k, v in list(blocks.items()) if k})
+        parts = {k: (v, 0) for k, v in blocks.items()}
+        parts[0] = (down_weight, a)
+        if h > 1:
+            parts[1] = (sibling, a)
+        order = sorted(parts)
+        chunks.append((j, a, b, [parts[k] for k in order], gate_inner))
 
     gate = gate_pre.astype(f32)
     hidden = (gate * jax.nn.sigmoid(gate) * up_pre.astype(f32)).astype(jnp.bfloat16)
@@ -192,7 +199,10 @@
         ],
         axis=1,
     )
-    early = lax.psum(early, "solve")
+    bit = 1
+    while bit < m:
+        early = early + swap(early, "solve", m, bit)
+        bit *= 2
 
     query_block = lax.all_gather(queries, "fsdp", axis=1, tiled=True)
     partial = jnp.dot(inverse_factor, query_block, precision=top)
@@ -221,7 +231,9 @@
 
     own_idx = jnp.stack([f ^ k for k in order]).astype(jnp.int32)
     far_idx = own_idx - side * h
-    own = tokens(own_idx, cot_full, weights, [(gate_pre, 0)], None, proj_hidden, 0, tiles)
+    own = None
+    for j, a, b, weights, _ in chunks:
+        own = tokens(own_idx, cot_full, weights, [(gate_pre, a)], own, proj_hidden, a, b - a)
     token_index = lax.broadcasted_iota(jnp.int32, (rows, 1), 0)
     slots = lax.broadcasted_iota(jnp.int32, (1, local_seqs), 1)
     length_of = jnp.sum(
@@ -244,10 +256,11 @@
     up_own = pair(own[:, half:], in_up)
 
     far = None
-    for j, (a, b, outer) in enumerate(zip(cuts[:-1], cuts[1:], gate_outer)):
-        if j == len(gate_outer) // 2:
+    for j, a, b, weights, gate_inner in chunks:
+        if j == len(chunks) - 2:
             far_idx, query_side = lax.optimization_barrier((far_idx, query_side))
-        far = tokens(far_idx, cot_far, weights, [(gate_inner, a), (outer, 0)], far, proj_hidden, a, b - a)
+        gates = [(gate_outer, a), (gate_inner, 0)]
+        far = tokens(far_idx, cot_far, weights, gates, far, proj_hidden, a, b - a)
     up_far = pair(far[:, half:], in_up_far)
     up = jnp.concatenate([up_own, up_far], axis=0)
     bit = 1
@@ -278,17 +291,27 @@
             scores = scores + swap(scores, axis, size, bit)
             bit *= 2
     block = 128
-    new_gram = pl.pallas_call(
-        functools.partial(gram_kernel, 1.0 / examples),
-        out_shape=jax.ShapeDtypeStruct(gram.shape, f32),
-        grid=(row_width // block,),
-        in_specs=[
-            pl.BlockSpec((block, col_width), lambda i: (i, 0)),
-            pl.BlockSpec((3 * examples, block), lambda i: (0, i)),
+    steps = row_width // block
+    ends = [0, steps // 2, steps]
+    new_gram = None
+    for a, b in zip(ends[:-1], ends[1:]):
+        in_specs = [
+            pl.BlockSpec((block, col_width), functools.partial(lambda z, i: (z + i, 0), a)),
+            pl.BlockSpec((3 * examples, block), functools.partial(lambda z, i: (0, z + i), a)),
             pl.BlockSpec((3 * examples, col_width), lambda i: (0, 0)),
-        ],
-        out_specs=pl.BlockSpec((block, col_width), lambda i: (i, 0)),
-    )(gram, left, right)
+        ]
+        operands = [gram, left, right]
+        if new_gram is not None:
+            in_specs.append(pl.BlockSpec(memory_space=pl.ANY))
+            operands.append(new_gram)
+        new_gram = pl.pallas_call(
+            functools.partial(gram_kernel, 1.0 / examples),
+            out_shape=jax.ShapeDtypeStruct(gram.shape, f32),
+            grid=(b - a,),
+            in_specs=in_specs,
+            out_specs=pl.BlockSpec((block, col_width), functools.partial(lambda z, i: (z + i, 0), a)),
+            input_output_aliases={} if new_gram is None else {3: 0},
+        )(*operands)
     return (new_gram, whitened, scores)
 
 

time: 615 us -> 677 us (1.10)
  waiting for transfers between devices: 246 us -> 355 us
  blocking collectives: 151 us -> 50.3 us
  starting transfers between devices: 42.7 us -> 71.8 us
  local copies, waits for them, and re-layouts: 14.9 us -> 28.2 us
    all_gather x1, blocking collectives: 134 us -> 33.3 us  [local(): lax.all_gather(pair(out_down, in_down), 'fsdp', axis=0, tiled=True)]
    ppermute x14 -> x20, waiting for transfers between devices: 86.3 us -> 182 us  [swap(): return lax.ppermute(x, axis, [(i, i ^ bit) for i in range(size)])]
    ppermute x14 -> x20, starting transfers between devices: 15.5 us -> 56.2 us  [swap(): return lax.ppermute(x, axis, [(i, i ^ bit) for i in range(size)])]
    slice x2 -> x6, local copies, waits for them, and re-layouts: 6.63 us -> 18.9 us  [the longest x3 10.2 us: local(): blocks = {0: down_weight[a * TILE:b * TILE]}]
    ppermute x7 -> x6, starting transfers between devices: 27 us -> 15.5 us  [mirror(): return lax.ppermute(x, 'fsdp', pairs)]
    all_gather x1, waiting for transfers between devices: 0.02 us -> 8.55 us  [local(): query_block = lax.all_gather(queries, 'fsdp', axis=1, tiled=True)]
    ppermute x7 -> x6, waiting for transfers between devices: 35.6 us -> 43.8 us  [mirror(): return lax.ppermute(x, 'fsdp', pairs)]
    pallas_call x5 -> x6, Pallas kernels: 86.6 us -> 91.8 us  [tokens(): pl.pallas_call(functools.partial(tokens_kernel, count, len(gate_parts), s...]
  transfers between devices with their start and end apart: 25 -> 29, of which waited for: 12 -> 13; matrix products, arithmetic and copies ran while one was open for 9% -> 11% of each run, Pallas kernels for 16% -> 15%
where the time goes in v1:
time: 677 us; the launch traced here: 676 us
  waiting for transfers between devices  355 us (52%)
  Pallas kernels  106 us (16%)
  starting transfers between devices  71.8 us (11%)
  blocking collectives  50.3 us (7%)
  matrix products  39.2 us (6%)
  local copies, waits for them, and re-layouts  28.2 us (4%)
  between operations  14.1 us (2%)
  other arithmetic  11.1 us (2%)
    ppermute x20, waiting for transfers between devices, swap(): return lax.ppermute(x, axis, [(i, i ^ bit) for i in range(size)])  182 us
    all_gather x1, waiting for transfers between devices, local(): cot_full = lax.all_gather(cotangent, 'solve', axis=1, tiled=True)  119 us
    pallas_call x6, Pallas kernels, tokens(): pl.pallas_call(functools.partial(tokens_kernel, count, len(gate_parts), s...  91.8 us
    ppermute x20, starting transfers between devices, swap(): return lax.ppermute(x, axis, [(i, i ^ bit) for i in range(size)])  56.2 us
    ppermute x6, waiting for transfers between devices, mirror(): return lax.ppermute(x, 'fsdp', pairs)  43.8 us
    all_gather x1, blocking collectives, local(): lax.all_gather(pair(out_down, in_down), 'fsdp', axis=0, tiled=True)  33.3 us
    all_gather x1, blocking collectives, local(): up_all = lax.all_gather(up, 'fsdp', axis=0, tiled=True)  17 us
    dot_general x1, matrix products, local(): lax.dot_general(inverse_factor, whitened_rows, (((0,), (0,)), ((), ())),...  16.5 us
  transfers between devices with their start and end apart: 29, of which 13 were waited for; matrix products, arithmetic and copies ran while one was open for 11% of the time, Pallas kernels for 15%

profile of v1, /device:TPU:0, one launch (start us, length us, event | category | flops | bytes accessed | tf_op | source)
XLA Modules:
  0.0 675.8 jit_solution(8644208705078781794)
XLA Ops:
  8.7 4.6 slice.44
  13.4 3.1 collective-permute-start.5
  16.4 118.6 %all-gather.6.cloned.1.call-done.refs_0_.refs_1_.refs_2_.refs_3_ = bf16[768,8192]{1,0:T(8,128)(2,1)} async-done(((bf16[768,2048]{1,0:T(8,128)(2,1)}), bf16[768,8192]{1,0:T(8,128)(2,1)}) %all-gather.6.cloned.1.call-update) | async-done | bytes 12582928 | tf_op jit(solution)/shard_map/all_gather | solution.py:166
  135.0 1.5 dynamic_slice.19
  136.5 3.4 collective-permute-start.13
  139.9 43.8 %collective-permute-done.13 = bf16[192,4096]{1,0:T(8,128)(2,1)} collective-permute-done((bf16[192,4096]{1,0:T(8,128)(2,1)S(1)}, bf16[192,4096]{1,0:T(8,128)(2,1)}, u32[]{:S(2)}, u32[]{:S(2)}) %collective-permute-start.13) | collective-permute-done | bytes 1572896 | tf_op jit(solution)/shard_map/ppermute | solution.py:160
  183.7 9.0 %fusion.5 = f32[768,64]{0,1:T(8,128)} fusion(bf16[768,3584]{1,0:T(8,128)(2,1)} %param.14, bf16[768,3584]{1,0:T(8,128)(2,1)} %refs_8_.5, bf16[3584,128]{1,0:T(8,128)(2,1)} %refs_11_.3), kind=kOutput, calls=%fused_computation.7 | convolution fusion | flops 374341632 | bytes 12124160 | tf_op jit(solution)/shard_map/dot_general | solution.py:196
  192.7 8.5 %all-gather.8.cloned.1.call-done = f32[2048,256]{0,1:T(8,128)} async-done(((f32[2048,32]{0,1:T(8,128)}), f32[2048,256]{0,1:T(8,128)}) %all-gather.8.cloned.1.call-update) | async-done | bytes 2097168 | tf_op jit(solution)/shard_map/all_gather | solution.py:207
  201.2 9.6 %fusion.40 = f32[1024,256]{1,0:T(8,128)S(1)} fusion(f32[1024,2048]{1,0:T(8,128)} %param.20, f32[2048,256]{0,1:T(8,128)} %all-gather.8.cloned.1.call-done), kind=kOutput, calls=%fused_computation.65 | convolution fusion | flops 6442450944 | bytes 11534336 | tf_op jit(solution)/shard_map/dot_general | solution.py:208
  211.7 1.5 collective-permute-start.9
  216.1 10.0 %collective-permute-done.9 = f32[512,256]{1,0:T(8,128)} collective-permute-done((f32[512,256]{1,0:T(8,128)}, f32[512,256]{1,0:T(8,128)}, u32[]{:S(2)}, u32[]{:S(2)}) %collective-permute-start.9) | collective-permute-done | bytes 524320 | tf_op jit(solution)/shard_map/ppermute | solution.py:154
  226.0 1.3 dynamic-slice_add_fusion
  227.4 1.5 collective-permute-start.10
  228.9 2.4 slice.42
  231.3 37.8 %collective-permute-start.1 = (bf16[512,1024]{1,0:T(8,128)(2,1)}, bf16[512,1024]{1,0:T(8,128)(2,1)S(1)}, u32[]{:S(2)}, u32[]{:S(2)}) collective-permute-start(bf16[512,1024]{1,0:T(8,128)(2,1)} %slice.42), channel_id=1, source_target_pairs={{0,8},{4,12},{8,0},{12,4},{16,24},{20,28},{24,16},{28,20},{1,9},{5... | collective-permute-start | bytes 3145736 | tf_op jit(solution)/shard_map/ppermute | solution.py:154
  269.2 4.5 collective-permute-start.14
  273.6 3.1 slice.43
  277.5 3.0 collective-permute-start.3
  281.6 12.8 %collective-permute-done.1.refs_6_ = bf16[512,1024]{1,0:T(8,128)(2,1)S(1)} collective-permute-done((bf16[512,1024]{1,0:T(8,128)(2,1)}, bf16[512,1024]{1,0:T(8,128)(2,1)S(1)}, u32[]{:S(2)}, u32[]{:S(2)}) %collective-permute-start.1) | collective-permute-done | bytes 1048608 | tf_op jit(solution)/shard_map/ppermute | solution.py:154
  295.0 2.0 fusion.39
  296.9 5.6 collective-permute-done.11
  303.3 1.5 collective-permute-start.8
  304.8 4.0 slice.52
  308.8 2.7 slice.51
  311.5 2.1 slice.50
  314.6 3.0 collective-permute-done.8
  319.6 135.4 %collective-permute-done.3.refs_6_ = bf16[1024,1024]{1,0:T(8,128)(2,1)S(1)} collective-permute-done((bf16[1024,1024]{1,0:T(8,128)(2,1)}, bf16[1024,1024]{1,0:T(8,128)(2,1)S(1)}, u32[]{:S(2)}, u32[]{:S(2)}) %collective-permute-start.3) | collective-permute-done | bytes 2097184 | tf_op jit(solution)/shard_map/ppermute | solution.py:154
  455.6 1.4 add.85
  457.0 2.3 collective-permute-start.17
  460.0 16.5 %convolution_bitcast_fusion.other = f32[2048,256]{1,0:T(8,128)} fusion(f32[1024,2048]{1,0:T(8,128)} %param.20, f32[512,256]{1,0:T(8,128)S(1)} %collective-permute-done.12, f32[512,256]{1,0:T(8,128)S(1)} %maximum_select_fusion.2, pred[]{:T(512)S(6)} %eq.29), kind=kOutput, calls=%fused_computation.8 | convolution fusion | flops 6443237376 | bytes 11534337 | tf_op jit(solution)/shard_map/dot_general | solution.py:228
  476.6 1.8 collective-permute-start.16
  478.8 22.1 %shard_map.130.refs_9_ = f32[768,128]{1,0:T(8,128)} custom-call(s32[4]{0:T(128)} %get-tuple-element.14.idx, bf16[768,8192]{1,0:T(8,128)(2,1)} %all-gather.6.cloned.1.call-done.refs_0_.refs_1_.refs_2_.refs_3_, bf16[768,8192]{1,0:T(8,128)(2,1)} %all-gather.6.cloned.1.call-done.refs_0_.refs_1_.refs_2_.refs_3_, ...), custom_call_target="tpu_custom_call" | custom-call | flops 13690208256 | bytes 29360128 | tf_op jit(solution)/shard_map/pallas_call | solution.py:63
  502.0 13.8 %shard_map.131.refs_9_ = f32[768,128]{1,0:T(8,128)} custom-call(s32[4]{0:T(128)} %get-tuple-element.14.idx, bf16[768,8192]{1,0:T(8,128)(2,1)} %all-gather.6.cloned.1.call-done.refs_0_.refs_1_.refs_2_.refs_3_, bf16[768,8192]{1,0:T(8,128)(2,1)} %all-gather.6.cloned.1.call-done.refs_0_.refs_1_.refs_2_.refs_3_, ...), custom_call_target="tpu_custom_call" | custom-call | flops 6845104128 | bytes 17825792 | tf_op jit(solution)/shard_map/pallas_call | solution.py:63
  515.8 2.4 collective-permute-start.18
  518.2 9.6 %shard_map.132 = f32[768,128]{1,0:T(8,128)} custom-call(s32[4]{0:T(128)} %get-tuple-element.14.idx, bf16[768,8192]{1,0:T(8,128)(2,1)} %all-gather.6.cloned.1.call-done.refs_0_.refs_1_.refs_2_.refs_3_, bf16[768,8192]{1,0:T(8,128)(2,1)} %all-gather.6.cloned.1.call-done.refs_0_.refs_1_.refs_2_.refs_3_, ...), custom_call_target="tpu_custom_call" | custom-call | flops 3422552064 | bytes 12058624 | tf_op jit(solution)/shard_map/pallas_call | solution.py:63
  529.9 22.4 %shard_map.133.refs_10_ = f32[768,128]{1,0:T(8,128)} custom-call(s32[4]{0:T(128)} %get-tuple-element.8.idx, bf16[768,4096]{1,0:T(8,128)(2,1)} %all-gather.10.cloned.1.call-done.refs_0_.refs_1_.refs_2_.refs_3_, bf16[768,4096]{1,0:T(8,128)(2,1)} %all-gather.10.cloned.1.call-done.refs_0_.refs_1_.refs_2_.refs_3_, ...), custom_call_target="tpu_custom_call" | custom-call | flops 13690208256 | bytes 29360128 | tf_op jit(solution)/shard_map/pallas_call | solution.py:63
  552.3 14.1 %shard_map.134.refs_10_ = f32[768,128]{1,0:T(8,128)} custom-call(s32[4]{0:T(128)} %get-tuple-element.8.idx, bf16[768,4096]{1,0:T(8,128)(2,1)} %all-gather.10.cloned.1.call-done.refs_0_.refs_1_.refs_2_.refs_3_, bf16[768,4096]{1,0:T(8,128)(2,1)} %all-gather.10.cloned.1.call-done.refs_0_.refs_1_.refs_2_.refs_3_, ...), custom_call_target="tpu_custom_call" | custom-call | flops 6845104128 | bytes 17825792 | tf_op jit(solution)/shard_map/pallas_call | solution.py:63
  567.3 9.8 %shard_map.135 = f32[768,128]{1,0:T(8,128)} custom-call(s32[4]{0:T(128)} %get-tuple-element.8.idx, bf16[768,4096]{1,0:T(8,128)(2,1)} %all-gather.10.cloned.1.call-done.refs_0_.refs_1_.refs_2_.refs_3_, bf16[768,4096]{1,0:T(8,128)(2,1)} %all-gather.10.cloned.1.call-done.refs_0_.refs_1_.refs_2_.refs_3_, ...), custom_call_target="tpu_custom_call" | custom-call | flops 3422552064 | bytes 12058624 | tf_op jit(solution)/shard_map/pallas_call | solution.py:63
  580.2 4.3 collective-permute-done.19
  584.9 33.3 %all-gather.1 = f32[8,3,4096]{2,1,0:T(4,128)S(1)} all-gather(f32[1,3,4096]{2,1,0:T(4,128)S(1)} %reshape.108), channel_id=1, replica_groups=mesh['fsdp'=8,'solve'=4] {'fsdp'}, dimensions={0}, use_global_device_ids=true | all-gather | bytes 442368 | tf_op jit(solution)/shard_map/all_gather | solution.py:255
  619.1 17.0 %all-gather = f32[8,6,4096]{2,1,0:T(8,128)S(1)} all-gather(f32[1,6,4096]{2,1,0:T(8,128)S(1)} %add_bitcast_fusion), channel_id=1, replica_groups=mesh['fsdp'=8,'solve'=4] {'fsdp'}, dimensions={0}, use_global_device_ids=true | all-gather | bytes 884736 | tf_op jit(solution)/shard_map/all_gather | solution.py:270
  637.2 3.7 shard_map.136
  643.6 3.8 collective-permute-done.22
  648.3 3.8 collective-permute-done.23
  653.0 2.9 collective-permute-done.24
  656.0 2.0 collective-permute-start.25
  657.9 5.3 shard_map.137.refs_0_
  663.2 5.4 shard_map.138
  (103 shorter events, 27.8 us)
Async XLA Ops:
  7.2 207.1 %copy-start = (bf16[768,2048]{1,0:T(8,128)(2,1)S(1)}, bf16[768,2048]{1,0:T(8,128)(2,1)}, u32[]{:S(2)}) copy-start(bf16[768,2048]{1,0:T(8,128)(2,1)} %param.11) | copy-start | bytes 9437188
  7.2 127.8 %all-gather.6.cloned.1.call-start = ((), (), s32[]{:S(2)}) async-start(), calls=%async_computation | async-start | bytes 15728640 | tf_op jit(solution)/shard_map/all_gather | solution.py:166
  7.9 193.3 %all-gather.8.cloned.1.call-start = ((), (), s32[]{:S(2)}) async-start(), calls=%async_computation.1 | async-start | bytes 2359296 | tf_op jit(solution)/shard_map/all_gather | solution.py:207
  8.7 521.2 %all-gather.10.cloned.1.call-start = ((), (), s32[]{:S(2)}) async-start(), calls=%async_computation.2 | async-start | bytes 7864320 | tf_op jit(solution)/shard_map/all_gather | solution.py:171
  13.4 199.8 %collective-permute-start.5 = (bf16[2048,1024]{1,0:T(8,128)(2,1)}, bf16[2048,1024]{1,0:T(8,128)(2,1)}, u32[]{:S(2)}, u32[]{:S(2)}) collective-permute-start(bf16[2048,1024]{1,0:T(8,128)(2,1)} %slice.44), channel_id=1, source_target_pairs={{0,8},{4,12},{8,0},{12,4},{16,24},{20,28},{24,16},{28,20},{1,9},{5... | collective-permute-start | bytes 12582920 | tf_op jit(solution)/shard_map/ppermute | solution.py:154
  136.5 47.2 %collective-permute-start.13 = (bf16[192,4096]{1,0:T(8,128)(2,1)S(1)}, bf16[192,4096]{1,0:T(8,128)(2,1)}, u32[]{:S(2)}, u32[]{:S(2)}) collective-permute-start(bf16[192,4096]{1,0:T(8,128)(2,1)S(1)} %dynamic_slice.19), channel_id=1, source_target_pairs={{0,24},{4,28},{8,16},{12,20},{16,8},{20,12},{24,0},{28,4},{1,25},{... | collective-permute-start | bytes 4718600 | tf_op jit(solution)/shard_map/ppermute | solution.py:160
  139.9 336.7 %collective-permute-start = (bf16[3584,1024]{1,0:T(8,128)(2,1)}, bf16[3584,1024]{1,0:T(8,128)(2,1)}, u32[]{:S(2)}, u32[]{:S(2)}) collective-permute-start(bf16[3584,1024]{1,0:T(8,128)(2,1)} %refs_4_.11), channel_id=1, source_target_pairs={{0,4},{4,0},{8,12},{12,8},{16,20},{20,16},{24,28},{28,24},{1,5},{5... | collective-permute-start | bytes 22020104 | tf_op jit(solution)/shard_map/ppermute | solution.py:154
  201.2 11.9 %copy-start.2 = (bf16[768,2048]{1,0:T(8,128)(2,1)S(1)}, bf16[768,2048]{1,0:T(8,128)(2,1)}, u32[]{:S(2)}) copy-start(bf16[768,2048]{1,0:T(8,128)(2,1)} %param.12) | copy-start | bytes 9437188
  201.2 11.9 %copy-start.7 = (bf16[2048,128]{1,0:T(8,128)(2,1)S(1)}, bf16[2048,128]{1,0:T(8,128)(2,1)}, u32[]{:S(2)}) copy-start(bf16[2048,128]{1,0:T(8,128)(2,1)} %param.16) | copy-start | bytes 1572868
  210.8 3.4 copy-start.4
  210.8 4.6 copy-start.10
  211.7 14.4 %collective-permute-start.9 = (f32[512,256]{1,0:T(8,128)}, f32[512,256]{1,0:T(8,128)}, u32[]{:S(2)}, u32[]{:S(2)}) collective-permute-start(f32[512,256]{1,0:T(8,128)} %constant_dynamic-slice_fusion.1), channel_id=1, source_target_pairs={{0,2},{1,3},{2,0},{3,1},{4,6},{5,7},{6,4},{7,5},{8,10},{9,11},{10,... | collective-permute-start | bytes 1572872 | tf_op jit(solution)/shard_map/ppermute | solution.py:154
  213.1 265.3 %collective-permute-start.6 = (bf16[2048,1024]{1,0:T(8,128)(2,1)}, bf16[2048,1024]{1,0:T(8,128)(2,1)}, u32[]{:S(2)}, u32[]{:S(2)}) collective-permute-start(bf16[2048,1024]{1,0:T(8,128)(2,1)} %collective-permute-done.5.refs_6_), channel_id=1, source_target_pairs={{0,4},{4,0},{8,12},{12,8},{16,20},{20,16},{24,28},{28,24},{1,5},{5... | collective-permute-start | bytes 12582920 | tf_op jit(solution)/shard_map/ppermute | solution.py:154
  215.5 53.7 %collective-permute-start.7 = (f32[768,192]{0,1:T(8,128)S(1)}, f32[768,192]{0,1:T(8,128)S(1)}, u32[]{:S(2)}, u32[]{:S(2)}) collective-permute-start(f32[768,192]{0,1:T(8,128)S(1)} %pad_maximum_fusion), channel_id=1, source_target_pairs={{0,1},{1,0},{2,3},{3,2},{4,5},{5,4},{6,7},{7,6},{8,9},{9,8},{10,11... | collective-permute-start | bytes 1769480 | tf_op jit(solution)/shard_map/ppermute | solution.py:154
  227.3 49.4 %copy-start.6 = (f32[512,256]{1,0:T(8,128)}, f32[512,256]{1,0:T(8,128)S(1)}, u32[]{:S(2)}) copy-start(f32[512,256]{1,0:T(8,128)S(1)} %dynamic-slice_add_fusion) | copy-start | bytes 1572868
  227.4 49.4 %collective-permute-start.10 = (f32[256,256]{1,0:T(8,128)S(1)}, f32[256,256]{1,0:T(8,128)S(1)}, u32[]{:S(2)}, u32[]{:S(2)}) collective-permute-start(f32[256,256]{1,0:T(8,128)S(1)} %constant_dynamic-slice_fusion), channel_id=1, source_target_pairs={{0,1},{1,0},{2,3},{3,2},{4,5},{5,4},{6,7},{7,6},{8,9},{9,8},{10,11... | collective-permute-start | bytes 786440 | tf_op jit(solution)/shard_map/ppermute | solution.py:154
  231.3 63.1 %collective-permute-start.1 = (bf16[512,1024]{1,0:T(8,128)(2,1)}, bf16[512,1024]{1,0:T(8,128)(2,1)S(1)}, u32[]{:S(2)}, u32[]{:S(2)}) collective-permute-start(bf16[512,1024]{1,0:T(8,128)(2,1)} %slice.42), channel_id=1, source_target_pairs={{0,8},{4,12},{8,0},{12,4},{16,24},{20,28},{24,16},{28,20},{1,9},{5... | collective-permute-start | bytes 3145736 | tf_op jit(solution)/shard_map/ppermute | solution.py:154
  269.1 7.6 %copy-start.13 = (f32[768,192]{0,1:T(8,128)}, f32[768,192]{0,1:T(8,128)S(1)}, u32[]{:S(2)}) copy-start(f32[768,192]{0,1:T(8,128)S(1)} %collective-permute-done.7) | copy-start | bytes 1769476
  269.2 260.7 %collective-permute-start.14 = (bf16[768,3584]{1,0:T(8,128)(2,1)}, bf16[768,3584]{1,0:T(8,128)(2,1)}, u32[]{:S(2)}, u32[]{:S(2)}) collective-permute-start(bf16[768,3584]{1,0:T(8,128)(2,1)} %refs_8_.5), channel_id=1, source_target_pairs={{0,24},{4,28},{24,0},{28,4},{1,25},{5,29},{25,1},{29,5},{2,26},{6,... | collective-permute-start | bytes 16515080 | tf_op jit(solution)/shard_map/ppermute | solution.py:160
  276.8 0.7 copy-start.15
  277.5 177.5 %collective-permute-start.3 = (bf16[1024,1024]{1,0:T(8,128)(2,1)}, bf16[1024,1024]{1,0:T(8,128)(2,1)S(1)}, u32[]{:S(2)}, u32[]{:S(2)}) collective-permute-start(bf16[1024,1024]{1,0:T(8,128)(2,1)} %slice.43), channel_id=1, source_target_pairs={{0,8},{4,12},{8,0},{12,4},{16,24},{20,28},{24,16},{28,20},{1,9},{5... | collective-permute-start | bytes 6291464 | tf_op jit(solution)/shard_map/ppermute | solution.py:154
  281.6 15.4 %copy-start.8 = (f32[256,256]{1,0:T(8,128)}, f32[256,256]{1,0:T(8,128)S(1)}, u32[]{:S(2)}) copy-start(f32[256,256]{1,0:T(8,128)S(1)} %dynamic-slice_add_fusion.1) | copy-start | bytes 786436
  294.4 184.0 %copy-start.5 = (bf16[512,1024]{1,0:T(8,128)(2,1)}, bf16[512,1024]{1,0:T(8,128)(2,1)S(1)}, u32[]{:S(2)}) copy-start(bf16[512,1024]{1,0:T(8,128)(2,1)S(1)} %collective-permute-done.1.refs_6_) | copy-start | bytes 3145732
  294.4 8.2 %collective-permute-start.11 = (f32[256,256]{1,0:T(8,128)S(1)}, f32[256,256]{1,0:T(8,128)S(1)}, u32[]{:S(2)}, u32[]{:S(2)}) collective-permute-start(f32[256,256]{1,0:T(8,128)S(1)} %dynamic-slice_add_fusion.1), channel_id=1, source_target_pairs={{0,1},{1,0},{2,3},{3,2},{4,5},{5,4},{6,7},{7,6},{8,9},{9,8},{10,11... | collective-permute-start | bytes 786440 | tf_op jit(solution)/shard_map/ppermute | solution.py:154
  302.6 0.7 copy-start.14
  303.3 14.3 %collective-permute-start.8 = (f32[768,192]{0,1:T(8,128)}, f32[768,192]{0,1:T(8,128)}, u32[]{:S(2)}, u32[]{:S(2)}) collective-permute-start(f32[768,192]{0,1:T(8,128)} %fusion.39), channel_id=1, source_target_pairs={{0,2},{1,3},{2,0},{3,1},{4,6},{5,7},{6,4},{7,5},{8,10},{9,11},{10,... | collective-permute-start | bytes 1769480 | tf_op jit(solution)/shard_map/ppermute | solution.py:154
  304.8 8.8 %copy-start.9 = (f32[256,256]{1,0:T(8,128)S(1)}, f32[256,256]{1,0:T(8,128)}, u32[]{:S(2)}) copy-start(f32[256,256]{1,0:T(8,128)} %copy-done.8) | copy-start | bytes 786436
  304.8 14.7 %copy-start.16 = (s32[3]{0:T(128)S(1)}, s32[3]{0:T(128)}, u32[]{:S(2)}) copy-start(s32[3]{0:T(128)} %param.18) | copy-start | bytes 40
  317.6 139.3 %collective-permute-start.12 = (f32[512,256]{1,0:T(8,128)S(1)}, f32[512,256]{1,0:T(8,128)S(1)}, u32[]{:S(2)}, u32[]{:S(2)}) collective-permute-start(f32[512,256]{1,0:T(8,128)S(1)} %maximum_select_fusion.2), channel_id=1, source_target_pairs={{0,2},{1,3},{2,0},{3,1},{4,6},{5,7},{6,4},{7,5},{8,10},{9,11},{10,... | collective-permute-start | bytes 1572872 | tf_op jit(solution)/shard_map/ppermute | solution.py:154
  454.9 21.7 %copy-start.3 = (bf16[1024,1024]{1,0:T(8,128)(2,1)}, bf16[1024,1024]{1,0:T(8,128)(2,1)S(1)}, u32[]{:S(2)}) copy-start(bf16[1024,1024]{1,0:T(8,128)(2,1)S(1)} %collective-permute-done.3.refs_6_) | copy-start | bytes 6291460
  454.9 46.0 %collective-permute-start.4 = (bf16[1024,1024]{1,0:T(8,128)(2,1)S(1)}, bf16[1024,1024]{1,0:T(8,128)(2,1)}, u32[]{:S(2)}, u32[]{:S(2)}) collective-permute-start(bf16[1024,1024]{1,0:T(8,128)(2,1)S(1)} %collective-permute-done.3.refs_6_), channel_id=1, source_target_pairs={{0,4},{4,0},{8,12},{12,8},{16,20},{20,16},{24,28},{28,24},{1,5},{5... | collective-permute-start | bytes 6291464 | tf_op jit(solution)/shard_map/ppermute | solution.py:154
  457.0 72.9 %collective-permute-start.17 = (bf16[768,2048]{1,0:T(8,128)(2,1)}, bf16[768,2048]{1,0:T(8,128)(2,1)}, u32[]{:S(2)}, u32[]{:S(2)}) collective-permute-start(bf16[768,2048]{1,0:T(8,128)(2,1)} %slice.52), channel_id=1, source_target_pairs={{8,16},{12,20},{16,8},{20,12},{9,17},{13,21},{17,9},{21,13},{10,18... | collective-permute-start | bytes 9437192 | tf_op jit(solution)/shard_map/ppermute | solution.py:160
  476.6 75.7 %collective-permute-start.16 = (bf16[768,1024]{1,0:T(8,128)(2,1)}, bf16[768,1024]{1,0:T(8,128)(2,1)}, u32[]{:S(2)}, u32[]{:S(2)}) collective-permute-start(bf16[768,1024]{1,0:T(8,128)(2,1)} %slice.51), channel_id=1, source_target_pairs={{8,16},{12,20},{16,8},{20,12},{9,17},{13,21},{17,9},{21,13},{10,18... | collective-permute-start | bytes 4718600 | tf_op jit(solution)/shard_map/ppermute | solution.py:160
  478.4 37.4 %collective-permute-start.2 = (bf16[512,1024]{1,0:T(8,128)(2,1)S(1)}, bf16[512,1024]{1,0:T(8,128)(2,1)}, u32[]{:S(2)}, u32[]{:S(2)}) collective-permute-start(bf16[512,1024]{1,0:T(8,128)(2,1)S(1)} %collective-permute-done.1.refs_6_), channel_id=1, source_target_pairs={{0,4},{4,0},{8,12},{12,8},{16,20},{20,16},{24,28},{28,24},{1,5},{5... | collective-permute-start | bytes 3145736 | tf_op jit(solution)/shard_map/ppermute | solution.py:154
  500.9 14.9 %copy-start.11 = (f32[768,64]{0,1:T(8,128)S(1)}, f32[768,64]{0,1:T(8,128)}, u32[]{:S(2)}) copy-start(f32[768,64]{0,1:T(8,128)} %get-tuple-element.16) | copy-start | bytes 589828
  500.9 65.5 %collective-permute-start.15 = (bf16[768,512]{1,0:T(8,128)(2,1)}, bf16[768,512]{1,0:T(8,128)(2,1)S(1)}, u32[]{:S(2)}, u32[]{:S(2)}) collective-permute-start(bf16[768,512]{1,0:T(8,128)(2,1)} %slice.50), channel_id=1, source_target_pairs={{8,16},{12,20},{16,8},{20,12},{9,17},{13,21},{17,9},{21,13},{10,18... | collective-permute-start | bytes 2359304 | tf_op jit(solution)/shard_map/ppermute | solution.py:160
  515.8 62.4 %collective-permute-start.18 = (f32[768,64]{0,1:T(8,128)S(1)}, f32[768,64]{0,1:T(8,128)S(1)}, u32[]{:S(2)}, u32[]{:S(2)}) collective-permute-start(f32[768,64]{0,1:T(8,128)S(1)} %copy-done.11), channel_id=1, source_target_pairs={{0,24},{4,28},{8,16},{12,20},{16,8},{20,12},{24,0},{28,4},{1,25},{... | collective-permute-start | bytes 589832 | tf_op jit(solution)/shard_map/ppermute | solution.py:160
  566.4 0.9 copy-start.12
  579.2 5.3 collective-permute-start.19
  584.6 34.6 %collective-permute-start.20 = (f32[6,4096]{1,0:T(8,128)S(1)}, f32[6,4096]{1,0:T(8,128)S(1)}, u32[]{:S(2)}, u32[]{:S(2)}) collective-permute-start(f32[6,4096]{1,0:T(8,128)S(1)} %fusion.38), channel_id=1, source_target_pairs={{0,2},{1,3},{2,0},{3,1},{4,6},{5,7},{6,4},{7,5},{8,10},{9,11},{10,... | collective-permute-start | bytes 294920 | tf_op jit(solution)/shard_map/ppermute | solution.py:154
  641.6 1.2 collective-permute-start.21
  643.6 3.8 collective-permute-start.22
  647.4 4.7 collective-permute-start.23
  652.1 3.8 collective-permute-start.24
  656.0 12.7 %collective-permute-start.25 = (f32[24,256]{1,0:T(8,128)S(1)}, f32[24,256]{1,0:T(8,128)S(1)}, u32[]{:S(2)}, u32[]{:S(2)}) collective-permute-start(f32[24,256]{1,0:T(8,128)S(1)} %add.102), channel_id=1, source_target_pairs={{0,2},{1,3},{2,0},{3,1},{4,6},{5,7},{6,4},{7,5},{8,10},{9,11},{10,... | collective-permute-start | bytes 73736 | tf_op jit(solution)/shard_map/ppermute | solution.py:154
  663.2 6.1 copy-start.1
Sparse Core Ops, SparseCore 0:
  9.8 125.0 all-gather.5
  136.6 64.6 all-gather.7
  203.1 96.3 all-gather.9

commit v2 on v1

--- a/solution.py
+++ b/solution.py
@@ -78,35 +78,30 @@
     )(idx, *operands)
 
 
-def features_kernel(examples, seqs, mirror_of, idx, up, down, other, left_out, right_out, scores):
+def features_kernel(examples, seqs, idx, both, other, left_out, right_out, scores):
     f32 = jnp.float32
-    pick = lax.broadcasted_iota(jnp.int32, (examples, up.shape[0]), 1)
-    row = lax.broadcasted_iota(jnp.int32, (examples, up.shape[0]), 0)
-    sel = jnp.zeros(pick.shape, f32)
-    for i, j in enumerate(mirror_of):
+    shape = (examples, both.shape[0])
+    pick = lax.broadcasted_iota(jnp.int32, shape, 1)
+    row = lax.broadcasted_iota(jnp.int32, shape, 0)
+    up = jnp.zeros(shape, f32)
+    down = jnp.zeros(shape, f32)
+    for i in range(examples // seqs):
         for e in range(seqs):
-            hit = (pick == 2 * seqs * i + e) | (pick == 2 * seqs * j + seqs + e)
-            sel = jnp.where(hit & (row == seqs * i + e), 1.0, sel)
-    sel = sel.astype(jnp.bfloat16)
+            here = row == seqs * i + e
+            up = jnp.where((pick == 2 * seqs * i + e) & here, 1.0, up)
+            down = jnp.where((pick == 2 * seqs * i + seqs + e) & here, 1.0, down)
 
     def split(x):
         high = x.astype(jnp.bfloat16)
         return high, (x - high.astype(f32)).astype(jnp.bfloat16)
 
     def part(offset, width):
-        size = down.shape[1]
-
-        def from_up():
-            at = pl.multiple_of(offset - size, 128)
-            high, low = split(up[:, pl.ds(at, width)])
-            return jnp.dot(sel, high, preferred_element_type=f32) + jnp.dot(
-                sel, low, preferred_element_type=f32
-            )
-
-        def from_down():
-            return down[:, pl.ds(pl.multiple_of(offset, 128), width)]
-
-        return lax.cond(offset >= size, from_up, from_down)
+        size = both.shape[1]
+        is_up = offset >= size
+        at = pl.multiple_of(offset - jnp.where(is_up, size, 0), 128)
+        high, low = split(both[:, pl.ds(at, width)])
+        sel = jnp.where(is_up, up, down).astype(jnp.bfloat16)
+        return jnp.dot(sel, high, preferred_element_type=f32) + jnp.dot(sel, low, preferred_element_type=f32)
 
     high, low = split(part(idx[0], left_out.shape[1]))
     left_out[...] = jnp.concatenate([high, low, high], axis=0)
@@ -162,32 +157,38 @@
     def inner(chip):
         return chips // 4 <= chip < chips - chips // 4
 
-    gate_outer = mirror(gate_pre, lambda chip: not inner(chip))
+    tiles = gate_pre.shape[1] // TILE
+    first = tiles * 5 // 7 * TILE
+    blocks = {0: down_weight}
+    if h > 2:
+        from_inner = lax.ppermute(down_weight, "fsdp", [(i, i ^ 2) for i in range(n) if inner(i // 2)])
+        outer_pairs = [(i, i ^ 2) for i in range(n) if not inner(i // 2)]
+        part_a = lax.ppermute(down_weight[:first], "fsdp", outer_pairs)
+    gate_inner = mirror(gate_pre, inner)
     cot_full = lax.all_gather(cotangent, "solve", axis=1, tiled=True)
     part = rows // m
     near = cot_full.shape[1] // 2
     quarter = lax.dynamic_slice(cot_full, (s * part, (1 - side) * near), (part, near))
     quarter = mirror(quarter)
     cot_far = lax.all_gather(quarter, "solve", axis=0, tiled=True)
-    tiles = gate_pre.shape[1] // TILE
+    if h > 2:
+        part_b = lax.ppermute(down_weight[first:], "fsdp", outer_pairs)
+        part_b, _ = lax.optimization_barrier((part_b, quarter))
+        blocks[2] = from_inner + jnp.concatenate([part_a, part_b], axis=0)
+    step = 4
+    while step < h:
+        blocks.update({k ^ step: swap(v, "fsdp", n, step) for k, v in list(blocks.items())})
+        step *= 2
+    if h > 1:
+        blocks.update({k ^ 1: swap(v, "fsdp", n, 1) for k, v in list(blocks.items())})
+    order = sorted(blocks)
+    weights = [blocks[k] for k in order]
     share = max(1, tiles // 7)
     cuts = [0, tiles - 3 * share, tiles - share, tiles]
-    sibling = swap(down_weight, "fsdp", n, 1) if h > 1 else None
     chunks = []
     for j, (a, b) in enumerate(zip(cuts[:-1], cuts[1:])):
-        blocks = {0: down_weight[a * TILE : b * TILE]}
-        step = 2
-        while step < h:
-            blocks.update({k ^ step: swap(v, "fsdp", n, step) for k, v in list(blocks.items())})
-            step *= 2
-        gate_inner = mirror(gate_pre[:, a * TILE : b * TILE], inner)
-        blocks.update({k ^ 1: swap(v, "fsdp", n, 1) for k, v in list(blocks.items()) if k})
-        parts = {k: (v, 0) for k, v in blocks.items()}
-        parts[0] = (down_weight, a)
-        if h > 1:
-            parts[1] = (sibling, a)
-        order = sorted(parts)
-        chunks.append((j, a, b, [parts[k] for k in order], gate_inner))
+        gate_outer = mirror(gate_pre[:, a * TILE : b * TILE], lambda chip: not inner(chip))
+        chunks.append((j, a, b, gate_outer))
 
     gate = gate_pre.astype(f32)
     hidden = (gate * jax.nn.sigmoid(gate) * up_pre.astype(f32)).astype(jnp.bfloat16)
@@ -231,9 +232,9 @@
 
     own_idx = jnp.stack([f ^ k for k in order]).astype(jnp.int32)
     far_idx = own_idx - side * h
-    own = None
-    for j, a, b, weights, _ in chunks:
-        own = tokens(own_idx, cot_full, weights, [(gate_pre, a)], own, proj_hidden, a, b - a)
+    own = tokens(
+        own_idx, cot_full, [(v, 0) for v in weights], [(gate_pre, 0)], None, proj_hidden, 0, tiles
+    )
     token_index = lax.broadcasted_iota(jnp.int32, (rows, 1), 0)
     slots = lax.broadcasted_iota(jnp.int32, (1, local_seqs), 1)
     length_of = jnp.sum(
@@ -252,22 +253,22 @@
         feat = jnp.einsum("eto,eti->eoi", outs.reshape(shape), ins.reshape(shape), precision=top)
         return feat.reshape(local_seqs, half * half)
 
-    down_all = lax.all_gather(pair(out_down, in_down), "fsdp", axis=0, tiled=True)
+    down = pair(out_down, in_down)
     up_own = pair(own[:, half:], in_up)
 
     far = None
-    for j, a, b, weights, gate_inner in chunks:
-        if j == len(chunks) - 2:
+    for j, a, b, gate_outer in chunks:
+        if j == len(chunks) - 1:
             far_idx, query_side = lax.optimization_barrier((far_idx, query_side))
-        gates = [(gate_outer, a), (gate_inner, 0)]
-        far = tokens(far_idx, cot_far, weights, gates, far, proj_hidden, a, b - a)
+        gates = [(gate_inner, a), (gate_outer, 0)]
+        far = tokens(far_idx, cot_far, [(v, a) for v in weights], gates, far, proj_hidden, a, b - a)
     up_far = pair(far[:, half:], in_up_far)
-    up = jnp.concatenate([up_own, up_far], axis=0)
+    up = up_own + mirror(up_far)
     bit = 1
     while bit < m:
         up = up + swap(up, "solve", m, bit)
         bit *= 2
-    up_all = lax.all_gather(up, "fsdp", axis=0, tiled=True)
+    both = lax.all_gather(jnp.concatenate([up, down], axis=0), "fsdp", axis=0, tiled=True)
 
     examples = n * local_seqs
     row_width = gram.shape[0]
@@ -275,14 +276,14 @@
     count = queries.shape[1] * n
     at = jnp.stack([f * row_width, s * col_width]).astype(jnp.int32)
     left, right, scores = pl.pallas_call(
-        functools.partial(features_kernel, examples, local_seqs, mirror_of),
+        functools.partial(features_kernel, examples, local_seqs),
         out_shape=(
             jax.ShapeDtypeStruct((3 * examples, row_width), jnp.bfloat16),
             jax.ShapeDtypeStruct((3 * examples, col_width), jnp.bfloat16),
             jax.ShapeDtypeStruct((examples, count), f32),
         ),
-        in_specs=[pl.BlockSpec(memory_space=pltpu.SMEM)] + [pl.BlockSpec(memory_space=pltpu.VMEM)] * 3,
-    )(at, up_all, down_all, query_side)
+        in_specs=[pl.BlockSpec(memory_space=pltpu.SMEM)] + [pl.BlockSpec(memory_space=pltpu.VMEM)] * 2,
+    )(at, both, query_side)
     total = 2 * half * half
     scores = scores / jnp.sqrt(f32(total))
     for axis, size in (("fsdp", n), ("solve", m)):

time: 677 us -> 595 us (0.88)
  waiting for transfers between devices: 355 us -> 272 us
  starting transfers between devices: 71.8 us -> 50.5 us
  blocking collectives: 50.3 us -> 70.8 us
  Pallas kernels: 106 us -> 95.5 us
  other arithmetic: 11.1 us -> 19.5 us
    ppermute x20 -> x15, waiting for transfers between devices: 182 us -> 61.5 us  [swap(): return lax.ppermute(x, axis, [(i, i ^ bit) for i in range(size)])]
    ppermute x0 -> x3, waiting for transfers between devices: none -> 58.4 us  [the longest x1 58.4 us: local(): part_b = lax.ppermute(down_weight[first:], 'fsdp', outer_pairs)]
    ppermute x20 -> x15, starting transfers between devices: 56.2 us -> 16 us  [swap(): return lax.ppermute(x, axis, [(i, i ^ bit) for i in range(size)])]
    all_gather x2 -> x1, blocking collectives: 50.3 us -> 70.8 us  [local(): lax.all_gather(jnp.concatenate([up, down], axis=0), 'fsdp', axis=0, tiled...]
    all_gather x1, waiting for transfers between devices: 119 us -> 104 us  [local(): cot_full = lax.all_gather(cotangent, 'solve', axis=1, tiled=True)]
    ppermute x0 -> x3, starting transfers between devices: none -> 14.5 us  [the longest x1 10.5 us: local(): part_a = lax.ppermute(down_weight[:first], 'fsdp', outer_pairs)]
    pallas_call x6 -> x4, Pallas kernels: 91.8 us -> 81.1 us  [tokens(): pl.pallas_call(functools.partial(tokens_kernel, count, len(gate_parts), s...]
    add x0 -> x2, other arithmetic: none -> 8.75 us  [the longest x1 8.73 us: local(): blocks[2] = from_inner + jnp.concatenate([part_a, part_b], axis=0)]
  transfers between devices with their start and end apart: 29 -> 28, of which waited for: 13 -> 17; matrix products, arithmetic and copies ran while one was open for 11% -> 14% of each run, Pallas kernels for 15% -> 15%
where the time goes in v2:
time: 595 us; the launch traced here: 594 us
  waiting for transfers between devices  272 us (46%)
  Pallas kernels  95.5 us (16%)
  blocking collectives  70.8 us (12%)
  starting transfers between devices  50.5 us (8%)
  matrix products  45.5 us (8%)
  local copies, waits for them, and re-layouts  26.3 us (4%)
  other arithmetic  19.5 us (3%)
  between operations  14 us (2%)
    all_gather x1, waiting for transfers between devices, local(): cot_full = lax.all_gather(cotangent, 'solve', axis=1, tiled=True)  104 us
    pallas_call x4, Pallas kernels, tokens(): pl.pallas_call(functools.partial(tokens_kernel, count, len(gate_parts), s...  81.1 us
    all_gather x1, blocking collectives, local(): lax.all_gather(jnp.concatenate([up, down], axis=0), 'fsdp', axis=0, tiled...  70.8 us
    ppermute x15, waiting for transfers between devices, swap(): return lax.ppermute(x, axis, [(i, i ^ bit) for i in range(size)])  61.5 us
    ppermute x1, waiting for transfers between devices, local(): part_b = lax.ppermute(down_weight[first:], 'fsdp', outer_pairs)  58.4 us
    ppermute x7, waiting for transfers between devices, mirror(): return lax.ppermute(x, 'fsdp', pairs)  47.7 us
    ppermute x7, starting transfers between devices, mirror(): return lax.ppermute(x, 'fsdp', pairs)  19.8 us
    dot_general x1, matrix products, local(): lax.dot_general(inverse_factor, whitened_rows, (((0,), (0,)), ((), ())),...  18.3 us
  transfers between devices with their start and end apart: 28, of which 17 were waited for; matrix products, arithmetic and copies ran while one was open for 14% of the time, Pallas kernels for 15%

profile of v2, /device:TPU:0, one launch (start us, length us, event | category | flops | bytes accessed | tf_op | source)
XLA Modules:
  0.0 593.9 jit_solution(15871253477392804412)
XLA Ops:
  9.4 5.4 slice.39
  14.8 10.5 %collective-permute-start.2 = (bf16[2560,1024]{1,0:T(8,128)(2,1)}, bf16[2560,1024]{1,0:T(8,128)(2,1)}, u32[]{:S(2)}, u32[]{:S(2)}) collective-permute-start(bf16[2560,1024]{1,0:T(8,128)(2,1)} %slice.39), channel_id=1, source_target_pairs={{0,8},{4,12},{24,16},{28,20},{1,9},{5,13},{25,17},{29,21},{2,10},{... | collective-permute-start | bytes 15728648 | tf_op jit(solution)/shard_map/ppermute | solution.py:166
  25.4 3.5 slice.40
  28.9 2.6 collective-permute-start.3
  31.5 103.5 %all-gather.5.cloned.1.call-done.refs_0_.refs_1_.refs_2_.refs_3_ = bf16[768,8192]{1,0:T(8,128)(2,1)} async-done(((bf16[768,2048]{1,0:T(8,128)(2,1)}), bf16[768,8192]{1,0:T(8,128)(2,1)}) %all-gather.5.cloned.1.call-update) | async-done | bytes 12582928 | tf_op jit(solution)/shard_map/all_gather | solution.py:168
  136.5 3.4 collective-permute-start.4
  139.9 58.4 %collective-permute-done.3 = bf16[1024,1024]{1,0:T(8,128)(2,1)} collective-permute-done((bf16[1024,1024]{1,0:T(8,128)(2,1)}, bf16[1024,1024]{1,0:T(8,128)(2,1)}, u32[]{:S(2)}, u32[]{:S(2)}) %collective-permute-start.3) | collective-permute-done | bytes 2097184 | tf_op jit(solution)/shard_map/ppermute | solution.py:175
  198.3 38.2 %collective-permute-done.4 = bf16[192,4096]{1,0:T(8,128)(2,1)} collective-permute-done((bf16[192,4096]{1,0:T(8,128)(2,1)S(1)}, bf16[192,4096]{1,0:T(8,128)(2,1)}, u32[]{:S(2)}, u32[]{:S(2)}) %collective-permute-start.4) | collective-permute-done | bytes 1572896 | tf_op jit(solution)/shard_map/ppermute | solution.py:155
  236.5 8.7 %maximum_add_fusion.refs_6_ = bf16[3584,1024]{1,0:T(8,128)(2,1)} fusion(bf16[3584,1024]{1,0:T(8,128)(2,1)} %collective-permute-done.1, bf16[1024,1024]{1,0:T(8,128)(2,1)} %collective-permute-done.3, bf16[2560,1024]{1,0:T(8,128)(2,1)} %collective-permute-done.2), kind=kLoop, calls=%fused_computation.7 | loop fusion | flops 22020096 | bytes 22020096 | tf_op jit(solution)/shard_map/add | solution.py:177
  245.2 3.0 collective-permute-start.12
  248.3 3.2 fusion.15
  251.5 9.7 %fusion.5 = f32[768,64]{0,1:T(8,128)} fusion(bf16[768,3584]{1,0:T(8,128)(2,1)} %param.14, bf16[768,3584]{1,0:T(8,128)(2,1)} %refs_8_.1, bf16[3584,128]{1,0:T(8,128)(2,1)} %refs_11_.3), kind=kOutput, calls=%fused_computation.8 | convolution fusion | flops 374341632 | bytes 12124160 | tf_op jit(solution)/shard_map/dot_general | solution.py:197
  261.1 9.5 %fusion.39 = f32[1024,256]{1,0:T(8,128)S(1)} fusion(f32[1024,2048]{1,0:T(8,128)} %param.20, f32[2048,256]{0,1:T(8,128)} %all-gather.7.cloned.1.call-done), kind=kOutput, calls=%fused_computation.64 | convolution fusion | flops 6442450944 | bytes 11534336 | tf_op jit(solution)/shard_map/dot_general | solution.py:209
  276.8 10.3 %collective-permute-done.8 = f32[512,256]{1,0:T(8,128)} collective-permute-done((f32[512,256]{1,0:T(8,128)}, f32[512,256]{1,0:T(8,128)}, u32[]{:S(2)}, u32[]{:S(2)}) %collective-permute-start.8) | collective-permute-done | bytes 524320 | tf_op jit(solution)/shard_map/ppermute | solution.py:149
  290.0 2.0 collective-permute-done.6
  292.0 1.8 fusion.38
  293.8 8.8 %collective-permute-done.9 = f32[256,256]{1,0:T(8,128)S(1)} collective-permute-done((f32[256,256]{1,0:T(8,128)S(1)}, f32[256,256]{1,0:T(8,128)S(1)}, u32[]{:S(2)}, u32[]{:S(2)}) %collective-permute-start.9) | collective-permute-done | bytes 262176 | tf_op jit(solution)/shard_map/ppermute | solution.py:149
  302.6 2.5 collective-permute-start.10
  305.2 4.0 slice.48
  309.2 8.1 %collective-permute-done.10 = f32[256,256]{1,0:T(8,128)} collective-permute-done((f32[256,256]{1,0:T(8,128)S(1)}, f32[256,256]{1,0:T(8,128)}, u32[]{:S(2)}, u32[]{:S(2)}) %collective-permute-start.10) | collective-permute-done | bytes 262176 | tf_op jit(solution)/shard_map/ppermute | solution.py:149
  317.3 1.9 collective-permute-start.15
  319.2 1.9 maximum_select_fusion.2
  322.3 2.1 slice.46
  324.4 2.7 slice.47
  329.9 17.3 %collective-permute-done.11 = f32[512,256]{1,0:T(8,128)} collective-permute-done((f32[512,256]{1,0:T(8,128)}, f32[512,256]{1,0:T(8,128)}, u32[]{:S(2)}, u32[]{:S(2)}) %collective-permute-start.11) | collective-permute-done | bytes 524320 | tf_op jit(solution)/shard_map/ppermute | solution.py:149
  347.2 5.0 collective-permute-start.13
  352.3 18.3 %convolution_bitcast_fusion.other = f32[2048,256]{1,0:T(8,128)} fusion(f32[1024,2048]{1,0:T(8,128)} %param.20, f32[512,256]{1,0:T(8,128)} %collective-permute-done.11, f32[512,256]{1,0:T(8,128)} %maximum_select_fusion.2, pred[]{:T(512)S(6)} %eq.29), kind=kOutput, calls=%fused_computation.9 | convolution fusion | flops 6443237376 | bytes 11534337 | tf_op jit(solution)/shard_map/dot_general | solution.py:229
  370.6 3.1 collective-permute-start.14
  373.6 3.0 collective-permute-start.16
  376.6 34.7 %shard_map.130 = f32[768,128]{1,0:T(8,128)} custom-call(s32[4]{0:T(128)} %get-tuple-element.16.idx, bf16[768,8192]{1,0:T(8,128)(2,1)} %all-gather.5.cloned.1.call-done.refs_0_.refs_1_.refs_2_.refs_3_, bf16[768,8192]{1,0:T(8,128)(2,1)} %all-gather.5.cloned.1.call-done.refs_0_.refs_1_.refs_2_.refs_3_, ...), custom_call_target="tpu_custom_call" | custom-call | flops 23957864448 | bytes 46661632 | tf_op jit(solution)/shard_map/pallas_call | solution.py:63
  412.5 1.6 copy-done.3
  414.1 22.4 %shard_map.131.refs_10_ = f32[768,128]{1,0:T(8,128)} custom-call(s32[4]{0:T(128)} %get-tuple-element.10.idx, bf16[768,4096]{1,0:T(8,128)(2,1)} %all-gather.9.cloned.1.call-done.refs_0_.refs_1_.refs_2_.refs_3_, bf16[768,4096]{1,0:T(8,128)(2,1)} %all-gather.9.cloned.1.call-done.refs_0_.refs_1_.refs_2_.refs_3_, ...), custom_call_target="tpu_custom_call" | custom-call | flops 13690208256 | bytes 29360128 | tf_op jit(solution)/shard_map/pallas_call | solution.py:63
  436.5 5.4 collective-permute-done.14.refs_9_
  441.9 14.0 %shard_map.132.refs_10_ = f32[768,128]{1,0:T(8,128)} custom-call(s32[4]{0:T(128)} %get-tuple-element.10.idx, bf16[768,4096]{1,0:T(8,128)(2,1)} %all-gather.9.cloned.1.call-done.refs_0_.refs_1_.refs_2_.refs_3_, bf16[768,4096]{1,0:T(8,128)(2,1)} %all-gather.9.cloned.1.call-done.refs_0_.refs_1_.refs_2_.refs_3_, ...), custom_call_target="tpu_custom_call" | custom-call | flops 6845104128 | bytes 17825792 | tf_op jit(solution)/shard_map/pallas_call | solution.py:63
  456.0 10.0 %shard_map.133 = f32[768,128]{1,0:T(8,128)} custom-call(s32[4]{0:T(128)} %get-tuple-element.10.idx, bf16[768,4096]{1,0:T(8,128)(2,1)} %all-gather.9.cloned.1.call-done.refs_0_.refs_1_.refs_2_.refs_3_, bf16[768,4096]{1,0:T(8,128)(2,1)} %all-gather.9.cloned.1.call-done.refs_0_.refs_1_.refs_2_.refs_3_, ...), custom_call_target="tpu_custom_call" | custom-call | flops 3422552064 | bytes 12058624 | tf_op jit(solution)/shard_map/pallas_call | solution.py:63
  467.1 1.7 fusion.23
  469.3 1.7 fusion.26
  471.1 4.1 collective-permute-done.17
  475.2 1.7 collective-permute-start.18
  477.6 1.9 collective-permute-done.18
  481.1 2.8 collective-permute-done.19
  483.9 70.8 %all-gather = f32[8,6,4096]{2,1,0:T(8,128)S(1)} all-gather(f32[1,6,4096]{2,1,0:T(8,128)S(1)} %maximum_bitcast_fusion), channel_id=1, replica_groups=mesh['fsdp'=8,'solve'=4] {'fsdp'}, dimensions={0}, use_global_device_ids=true | all-gather | bytes 884736 | tf_op jit(solution)/shard_map/all_gather | solution.py:271
  555.8 3.7 shard_map.134
  563.1 2.9 collective-permute-done.21
  567.4 3.3 collective-permute-done.22
  572.1 2.4 collective-permute-done.23
  576.0 5.3 shard_map.135.refs_0_
  581.3 5.4 shard_map.136
  (84 shorter events, 31.8 us)
Async XLA Ops:
  7.2 266.9 %copy-start = (bf16[768,2048]{1,0:T(8,128)(2,1)S(1)}, bf16[768,2048]{1,0:T(8,128)(2,1)}, u32[]{:S(2)}) copy-start(bf16[768,2048]{1,0:T(8,128)(2,1)} %param.11) | copy-start | bytes 9437188
  7.2 127.8 %all-gather.5.cloned.1.call-start = ((), (), s32[]{:S(2)}) async-start(), calls=%async_computation | async-start | bytes 15728640 | tf_op jit(solution)/shard_map/all_gather | solution.py:168
  7.9 253.2 %all-gather.7.cloned.1.call-start = ((), (), s32[]{:S(2)}) async-start(), calls=%async_computation.1 | async-start | bytes 2359296 | tf_op jit(solution)/shard_map/all_gather | solution.py:208
  8.0 228.5 %collective-permute-start.1 = (bf16[3584,1024]{1,0:T(8,128)(2,1)}, bf16[3584,1024]{1,0:T(8,128)(2,1)}, u32[]{:S(2)}, u32[]{:S(2)}) collective-permute-start(bf16[3584,1024]{1,0:T(8,128)(2,1)} %refs_4_.7), channel_id=1, source_target_pairs={{8,0},{12,4},{16,24},{20,28},{9,1},{13,5},{17,25},{21,29},{10,2},{... | collective-permute-start | bytes 22020104 | tf_op jit(solution)/shard_map/ppermute | solution.py:164
  14.8 221.7 %collective-permute-start.2 = (bf16[2560,1024]{1,0:T(8,128)(2,1)}, bf16[2560,1024]{1,0:T(8,128)(2,1)}, u32[]{:S(2)}, u32[]{:S(2)}) collective-permute-start(bf16[2560,1024]{1,0:T(8,128)(2,1)} %slice.39), channel_id=1, source_target_pairs={{0,8},{4,12},{24,16},{28,20},{1,9},{5,13},{25,17},{29,21},{2,10},{... | collective-permute-start | bytes 15728648 | tf_op jit(solution)/shard_map/ppermute | solution.py:166
  25.4 387.2 %all-gather.9.cloned.1.call-start = ((), (), s32[]{:S(2)}) async-start(), calls=%async_computation.2 | async-start | bytes 7864320 | tf_op jit(solution)/shard_map/all_gather | solution.py:173
  28.9 169.4 %collective-permute-start.3 = (bf16[1024,1024]{1,0:T(8,128)(2,1)}, bf16[1024,1024]{1,0:T(8,128)(2,1)}, u32[]{:S(2)}, u32[]{:S(2)}) collective-permute-start(bf16[1024,1024]{1,0:T(8,128)(2,1)} %slice.40), channel_id=1, source_target_pairs={{0,8},{4,12},{24,16},{28,20},{1,9},{5,13},{25,17},{29,21},{2,10},{... | collective-permute-start | bytes 6291464 | tf_op jit(solution)/shard_map/ppermute | solution.py:175
  136.5 100.0 %collective-permute-start.4 = (bf16[192,4096]{1,0:T(8,128)(2,1)S(1)}, bf16[192,4096]{1,0:T(8,128)(2,1)}, u32[]{:S(2)}, u32[]{:S(2)}) collective-permute-start(bf16[192,4096]{1,0:T(8,128)(2,1)S(1)} %dynamic_slice.15), channel_id=1, source_target_pairs={{0,24},{4,28},{8,16},{12,20},{16,8},{20,12},{24,0},{28,4},{1,25},{... | collective-permute-start | bytes 4718600 | tf_op jit(solution)/shard_map/ppermute | solution.py:155
  139.9 230.7 %collective-permute-start = (bf16[3584,1024]{1,0:T(8,128)(2,1)}, bf16[3584,1024]{1,0:T(8,128)(2,1)}, u32[]{:S(2)}, u32[]{:S(2)}) collective-permute-start(bf16[3584,1024]{1,0:T(8,128)(2,1)} %refs_4_.7), channel_id=1, source_target_pairs={{0,4},{4,0},{8,12},{12,8},{16,20},{20,16},{24,28},{28,24},{1,5},{5... | collective-permute-start | bytes 22020104 | tf_op jit(solution)/shard_map/ppermute | solution.py:149
  245.2 128.4 %collective-permute-start.5 = (bf16[3584,1024]{1,0:T(8,128)(2,1)}, bf16[3584,1024]{1,0:T(8,128)(2,1)}, u32[]{:S(2)}, u32[]{:S(2)}) collective-permute-start(bf16[3584,1024]{1,0:T(8,128)(2,1)} %maximum_add_fusion.refs_6_), channel_id=1, source_target_pairs={{0,4},{4,0},{8,12},{12,8},{16,20},{20,16},{24,28},{28,24},{1,5},{5... | collective-permute-start | bytes 22020104 | tf_op jit(solution)/shard_map/ppermute | solution.py:149
  245.2 167.3 %collective-permute-start.12 = (bf16[768,3584]{1,0:T(8,128)(2,1)}, bf16[768,3584]{1,0:T(8,128)(2,1)}, u32[]{:S(2)}, u32[]{:S(2)}) collective-permute-start(bf16[768,3584]{1,0:T(8,128)(2,1)} %refs_8_.1), channel_id=1, source_target_pairs={{8,16},{12,20},{16,8},{20,12},{9,17},{13,21},{17,9},{21,13},{10,18... | collective-permute-start | bytes 16515080 | tf_op jit(solution)/shard_map/ppermute | solution.py:155
  261.1 12.9 %copy-start.4 = (bf16[2048,128]{1,0:T(8,128)(2,1)S(1)}, bf16[2048,128]{1,0:T(8,128)(2,1)}, u32[]{:S(2)}) copy-start(bf16[2048,128]{1,0:T(8,128)(2,1)} %param.16) | copy-start | bytes 1572868
  261.1 14.1 %copy-start.6 = (f32[768,64]{0,1:T(8,128)S(1)}, f32[768,64]{0,1:T(8,128)}, u32[]{:S(2)}) copy-start(f32[768,64]{0,1:T(8,128)} %fusion.5) | copy-start | bytes 589828
  270.6 1.0 copy-start.2
  272.5 14.7 %collective-permute-start.8 = (f32[512,256]{1,0:T(8,128)}, f32[512,256]{1,0:T(8,128)}, u32[]{:S(2)}, u32[]{:S(2)}) collective-permute-start(f32[512,256]{1,0:T(8,128)} %constant_dynamic-slice_fusion.1), channel_id=1, source_target_pairs={{0,2},{1,3},{2,0},{3,1},{4,6},{5,7},{6,4},{7,5},{8,10},{9,11},{10,... | collective-permute-start | bytes 1572872 | tf_op jit(solution)/shard_map/ppermute | solution.py:149
  275.2 33.9 %copy-start.9 = (s32[3]{0:T(128)S(1)}, s32[3]{0:T(128)}, u32[]{:S(2)}) copy-start(s32[3]{0:T(128)} %param.18) | copy-start | bytes 40
  275.3 16.7 %collective-permute-start.6 = (f32[768,192]{0,1:T(8,128)S(1)}, f32[768,192]{0,1:T(8,128)S(1)}, u32[]{:S(2)}, u32[]{:S(2)}) collective-permute-start(f32[768,192]{0,1:T(8,128)S(1)} %pad_maximum_fusion), channel_id=1, source_target_pairs={{0,1},{1,0},{2,3},{3,2},{4,5},{5,4},{6,7},{7,6},{8,9},{9,8},{10,11... | collective-permute-start | bytes 1769480 | tf_op jit(solution)/shard_map/ppermute | solution.py:149
  288.4 14.1 %collective-permute-start.9 = (f32[256,256]{1,0:T(8,128)S(1)}, f32[256,256]{1,0:T(8,128)S(1)}, u32[]{:S(2)}, u32[]{:S(2)}) collective-permute-start(f32[256,256]{1,0:T(8,128)S(1)} %constant_dynamic-slice_fusion), channel_id=1, source_target_pairs={{0,1},{1,0},{2,3},{3,2},{4,5},{5,4},{6,7},{7,6},{8,9},{9,8},{10,11... | collective-permute-start | bytes 786440 | tf_op jit(solution)/shard_map/ppermute | solution.py:149
  293.8 28.3 %collective-permute-start.7 = (f32[768,192]{0,1:T(8,128)}, f32[768,192]{0,1:T(8,128)}, u32[]{:S(2)}, u32[]{:S(2)}) collective-permute-start(f32[768,192]{0,1:T(8,128)} %fusion.38), channel_id=1, source_target_pairs={{0,2},{1,3},{2,0},{3,1},{4,6},{5,7},{6,4},{7,5},{8,10},{9,11},{10,... | collective-permute-start | bytes 1769480 | tf_op jit(solution)/shard_map/ppermute | solution.py:149
  302.6 26.4 %copy-start.5 = (f32[256,256]{1,0:T(8,128)}, f32[256,256]{1,0:T(8,128)S(1)}, u32[]{:S(2)}) copy-start(f32[256,256]{1,0:T(8,128)S(1)} %dynamic-slice_add_fusion.1) | copy-start | bytes 786436
  302.6 14.7 %collective-permute-start.10 = (f32[256,256]{1,0:T(8,128)S(1)}, f32[256,256]{1,0:T(8,128)}, u32[]{:S(2)}, u32[]{:S(2)}) collective-permute-start(f32[256,256]{1,0:T(8,128)S(1)} %dynamic-slice_add_fusion.1), channel_id=1, source_target_pairs={{0,1},{1,0},{2,3},{3,2},{4,5},{5,4},{6,7},{7,6},{8,9},{9,8},{10,11... | collective-permute-start | bytes 786440 | tf_op jit(solution)/shard_map/ppermute | solution.py:149
  317.3 95.2 %collective-permute-start.15 = (bf16[768,2048]{1,0:T(8,128)(2,1)}, bf16[768,2048]{1,0:T(8,128)(2,1)S(1)}, u32[]{:S(2)}, u32[]{:S(2)}) collective-permute-start(bf16[768,2048]{1,0:T(8,128)(2,1)} %slice.48), channel_id=1, source_target_pairs={{0,24},{4,28},{24,0},{28,4},{1,25},{5,29},{25,1},{29,5},{2,26},{6,... | collective-permute-start | bytes 9437192 | tf_op jit(solution)/shard_map/ppermute | solution.py:155
  322.0 25.2 %collective-permute-start.11 = (f32[512,256]{1,0:T(8,128)}, f32[512,256]{1,0:T(8,128)}, u32[]{:S(2)}, u32[]{:S(2)}) collective-permute-start(f32[512,256]{1,0:T(8,128)} %maximum_select_fusion.2), channel_id=1, source_target_pairs={{0,2},{1,3},{2,0},{3,1},{4,6},{5,7},{6,4},{7,5},{8,10},{9,11},{10,... | collective-permute-start | bytes 1572872 | tf_op jit(solution)/shard_map/ppermute | solution.py:149
  347.2 108.7 %collective-permute-start.13 = (bf16[768,512]{1,0:T(8,128)(2,1)}, bf16[768,512]{1,0:T(8,128)(2,1)}, u32[]{:S(2)}, u32[]{:S(2)}) collective-permute-start(bf16[768,512]{1,0:T(8,128)(2,1)} %slice.46), channel_id=1, source_target_pairs={{0,24},{4,28},{24,0},{28,4},{1,25},{5,29},{25,1},{29,5},{2,26},{6,... | collective-permute-start | bytes 2359304 | tf_op jit(solution)/shard_map/ppermute | solution.py:155
  370.6 71.4 %collective-permute-start.14 = (bf16[768,1024]{1,0:T(8,128)(2,1)}, bf16[768,1024]{1,0:T(8,128)(2,1)}, u32[]{:S(2)}, u32[]{:S(2)}) collective-permute-start(bf16[768,1024]{1,0:T(8,128)(2,1)} %slice.47), channel_id=1, source_target_pairs={{0,24},{4,28},{24,0},{28,4},{1,25},{5,29},{25,1},{29,5},{2,26},{6,... | collective-permute-start | bytes 4718600 | tf_op jit(solution)/shard_map/ppermute | solution.py:155
  373.6 93.5 %collective-permute-start.16 = (f32[768,64]{0,1:T(8,128)}, f32[768,64]{0,1:T(8,128)}, u32[]{:S(2)}, u32[]{:S(2)}) collective-permute-start(f32[768,64]{0,1:T(8,128)} %get-tuple-element.17), channel_id=1, source_target_pairs={{0,24},{4,28},{8,16},{12,20},{16,8},{20,12},{24,0},{28,4},{1,25},{... | collective-permute-start | bytes 589832 | tf_op jit(solution)/shard_map/ppermute | solution.py:155
  412.5 1.6 copy-start.3
  456.0 24.7 %copy-start.7 = (f32[768,64]{0,1:T(8,128)S(1)}, f32[768,64]{0,1:T(8,128)}, u32[]{:S(2)}) copy-start(f32[768,64]{0,1:T(8,128)} %get-tuple-element.18) | copy-start | bytes 589828
  456.0 24.7 %copy-start.8 = (f32[768,64]{0,1:T(8,128)S(1)}, f32[768,64]{0,1:T(8,128)}, u32[]{:S(2)}) copy-start(f32[768,64]{0,1:T(8,128)} %get-tuple-element.19) | copy-start | bytes 589828
  468.9 6.2 %collective-permute-start.17 = (f32[3,4096]{1,0:T(4,128)S(1)}, f32[3,4096]{1,0:T(4,128)S(1)}, u32[]{:S(2)}, u32[]{:S(2)}) collective-permute-start(f32[3,4096]{1,0:T(4,128)S(1)} %reshape.102), channel_id=1, source_target_pairs={{0,24},{4,28},{8,16},{12,20},{16,8},{20,12},{24,0},{28,4},{1,25},{... | collective-permute-start | bytes 147464 | tf_op jit(solution)/shard_map/ppermute | solution.py:155
  475.2 4.3 collective-permute-start.18
  479.5 4.3 collective-permute-start.19
  560.2 1.2 collective-permute-start.20
  562.1 3.8 collective-permute-start.21
  566.0 4.7 collective-permute-start.22
  570.7 3.8 collective-permute-start.23
  574.5 12.2 %collective-permute-start.24 = (f32[24,256]{1,0:T(8,128)S(1)}, f32[24,256]{1,0:T(8,128)S(1)}, u32[]{:S(2)}, u32[]{:S(2)}) collective-permute-start(f32[24,256]{1,0:T(8,128)S(1)} %add.110), channel_id=1, source_target_pairs={{0,2},{1,3},{2,0},{3,1},{4,6},{5,7},{6,4},{7,5},{8,10},{9,11},{10,... | collective-permute-start | bytes 73736 | tf_op jit(solution)/shard_map/ppermute | solution.py:149
  581.3 6.1 %copy-start.1 = (bf16[768,2048]{1,0:T(8,128)(2,1)S(1)}, bf16[768,2048]{1,0:T(8,128)(2,1)}, u32[]{:S(2)}) copy-start(bf16[768,2048]{1,0:T(8,128)(2,1)} %param.11) | copy-start | bytes 9437188
Sparse Core Ops, SparseCore 0:
  9.8 125.0 all-gather.4
  136.6 41.8 all-gather.6
  245.4 103.5 all-gather.8

commit v3 on v2

--- a/solution.py
+++ b/solution.py
@@ -108,7 +108,13 @@
     right = part(idx[1], right_out.shape[1])
     high, low = split(right)
     right_out[...] = jnp.concatenate([high, high, low], axis=0)
-    scores[...] = jnp.dot(right, other[...], precision=lax.Precision.HIGHEST, preferred_element_type=f32)
+    scores[...] = lax.dot_general(
+        right,
+        other[...],
+        (((1,), (1,)), ((), ())),
+        precision=lax.Precision.HIGHEST,
+        preferred_element_type=f32,
+    )
 
 
 def gram_kernel(scale, gram, left, right, *refs):
@@ -158,12 +164,11 @@
         return chips // 4 <= chip < chips - chips // 4
 
     tiles = gate_pre.shape[1] // TILE
-    first = tiles * 5 // 7 * TILE
     blocks = {0: down_weight}
-    if h > 2:
-        from_inner = lax.ppermute(down_weight, "fsdp", [(i, i ^ 2) for i in range(n) if inner(i // 2)])
-        outer_pairs = [(i, i ^ 2) for i in range(n) if not inner(i // 2)]
-        part_a = lax.ppermute(down_weight[:first], "fsdp", outer_pairs)
+    step = 2
+    while step < h:
+        blocks.update({k ^ step: swap(v, "fsdp", n, step) for k, v in list(blocks.items())})
+        step *= 2
     gate_inner = mirror(gate_pre, inner)
     cot_full = lax.all_gather(cotangent, "solve", axis=1, tiled=True)
     part = rows // m
@@ -171,23 +176,17 @@
     quarter = lax.dynamic_slice(cot_full, (s * part, (1 - side) * near), (part, near))
     quarter = mirror(quarter)
     cot_far = lax.all_gather(quarter, "solve", axis=0, tiled=True)
-    if h > 2:
-        part_b = lax.ppermute(down_weight[first:], "fsdp", outer_pairs)
-        part_b, _ = lax.optimization_barrier((part_b, quarter))
-        blocks[2] = from_inner + jnp.concatenate([part_a, part_b], axis=0)
-    step = 4
-    while step < h:
-        blocks.update({k ^ step: swap(v, "fsdp", n, step) for k, v in list(blocks.items())})
-        step *= 2
-    if h > 1:
-        blocks.update({k ^ 1: swap(v, "fsdp", n, 1) for k, v in list(blocks.items())})
+    sibling = swap(down_weight, "fsdp", n, 1)
+    blocks.update({k ^ 1: swap(v, "fsdp", n, 1) for k, v in list(blocks.items()) if k})
+    blocks[1] = sibling
     order = sorted(blocks)
     weights = [blocks[k] for k in order]
     share = max(1, tiles // 7)
     cuts = [0, tiles - 3 * share, tiles - share, tiles]
     chunks = []
     for j, (a, b) in enumerate(zip(cuts[:-1], cuts[1:])):
-        gate_outer = mirror(gate_pre[:, a * TILE : b * TILE], lambda chip: not inner(chip))
+        gate_outer, _ = lax.optimization_barrier((gate_pre[:, a * TILE : b * TILE], quarter))
+        gate_outer = mirror(gate_outer, lambda chip: not inner(chip))
         chunks.append((j, a, b, gate_outer))
 
     gate = gate_pre.astype(f32)
@@ -205,8 +204,8 @@
         early = early + swap(early, "solve", m, bit)
         bit *= 2
 
-    query_block = lax.all_gather(queries, "fsdp", axis=1, tiled=True)
-    partial = jnp.dot(inverse_factor, query_block, precision=top)
+    query_block = lax.all_gather(queries.astype(jnp.bfloat16), "fsdp", axis=1, tiled=True)
+    partial = jnp.dot(inverse_factor, query_block.astype(f32), precision=lax.Precision.HIGH)
     whitened = partial
     bit = m // 2
     while bit:
@@ -226,9 +225,7 @@
             jnp.concatenate([moved, whitened_rows], axis=0),
         )
         bit *= 2
-    query_side = lax.dot_general(
-        inverse_factor, whitened_rows, (((0,), (0,)), ((), ())), precision=top
-    )
+    query_side = lax.dot_general(whitened_rows, inverse_factor, (((0,), (0,)), ((), ())), precision=lax.Precision.HIGH)
 
     own_idx = jnp.stack([f ^ k for k in order]).astype(jnp.int32)
     far_idx = own_idx - side * h
@@ -246,7 +243,7 @@
     in_down = early[:, :half]
     out_down = early[:, half : 2 * half] * weight_of
     in_up = early[:, 2 * half :] * weight_of
-    in_up_far = mirror(in_up)
+    in_up_far = mirror(in_up.astype(jnp.bfloat16)).astype(f32)
 
     def pair(outs, ins):
         shape = (local_seqs, SEQ_LEN, half)

time: 595 us -> 580 us (0.975)
  blocking collectives: 70.8 us -> 98.8 us
  matrix products: 45.5 us -> 32.1 us
  starting transfers between devices: 50.5 us -> 41.4 us
  local copies, waits for them, and re-layouts: 26.3 us -> 17.4 us
  other arithmetic: 19.5 us -> 10.6 us
    ppermute x3 -> x0, waiting for transfers between devices: 58.4 us -> none  [the longest x1 58.4 us: local(): part_b = lax.ppermute(down_weight[first:], 'fsdp', outer_pairs)]
    ppermute x15 -> x16, waiting for transfers between devices: 61.5 us -> 99.5 us  [swap(): return lax.ppermute(x, axis, [(i, i ^ bit) for i in range(size)])]
    all_gather x1, blocking collectives: 70.8 us -> 98.8 us  [local(): lax.all_gather(jnp.concatenate([up, down], axis=0), 'fsdp', axis=0, tiled...]
    all_gather x1, waiting for transfers between devices: 104 us -> 122 us  [local(): cot_full = lax.all_gather(cotangent, 'solve', axis=1, tiled=True)]
    ppermute x3 -> x0, starting transfers between devices: 14.5 us -> none  [the longest x1 10.5 us: local(): part_a = lax.ppermute(down_weight[:first], 'fsdp', outer_pairs)]
    dot_general x2, matrix products: 27.7 us -> 15.2 us  [the longest x1 9.12 us: local(): lax.dot_general(whitened_rows, inverse_factor, (((0,), (0,)), ((), ())),...]
    slice x2 -> x0, local copies, waits for them, and re-layouts: 8.89 us -> none  [the longest x1 5.42 us: local(): part_a = lax.ppermute(down_weight[:first], 'fsdp', outer_pairs)]
    add x1 -> x0, other arithmetic: 8.73 us -> none  [local(): blocks[2] = from_inner + jnp.concatenate([part_a, part_b], axis=0)]
  transfers between devices with their start and end apart: 28 -> 26, of which waited for: 17 -> 17; matrix products, arithmetic and copies ran while one was open for 14% -> 9% of each run, Pallas kernels for 15% -> 16%
where the time goes in v3:
time: 580 us; the launch traced here: 579 us
  waiting for transfers between devices  269 us (46%)
  blocking collectives  98.8 us (17%)
  Pallas kernels  96.2 us (17%)
  starting transfers between devices  41.4 us (7%)
  matrix products  32.1 us (6%)
  local copies, waits for them, and re-layouts  17.4 us (3%)
  between operations  14.1 us (2%)
  other arithmetic  10.6 us (2%)
    all_gather x1, waiting for transfers between devices, local(): cot_full = lax.all_gather(cotangent, 'solve', axis=1, tiled=True)  122 us
    ppermute x16, waiting for transfers between devices, swap(): return lax.ppermute(x, axis, [(i, i ^ bit) for i in range(size)])  99.5 us
    all_gather x1, blocking collectives, local(): lax.all_gather(jnp.concatenate([up, down], axis=0), 'fsdp', axis=0, tiled...  98.8 us
    pallas_call x4, Pallas kernels, tokens(): pl.pallas_call(functools.partial(tokens_kernel, count, len(gate_parts), s...  81.1 us
    ppermute x7, waiting for transfers between devices, mirror(): return lax.ppermute(x, 'fsdp', pairs)  46.2 us
    ppermute x7, starting transfers between devices, mirror(): return lax.ppermute(x, 'fsdp', pairs)  24.6 us
    ppermute x16, starting transfers between devices, swap(): return lax.ppermute(x, axis, [(i, i ^ bit) for i in range(size)])  16.7 us
  transfers between devices with their start and end apart: 26, of which 17 were waited for; matrix products, arithmetic and copies ran while one was open for 9% of the time, Pallas kernels for 16%

profile of v3, /device:TPU:0, one launch (start us, length us, event | category | flops | bytes accessed | tf_op | source)
XLA Modules:
  0.0 579.2 jit_solution(7704198176177594834)
XLA Ops:
  8.0 3.1 collective-permute-start.1
  11.1 1.6 convert_element_type.29
  12.8 122.2 %all-gather.5.cloned.1.call-done.refs_0_.refs_1_.refs_2_.refs_3_ = bf16[768,8192]{1,0:T(8,128)(2,1)} async-done(((bf16[768,2048]{1,0:T(8,128)(2,1)}), bf16[768,8192]{1,0:T(8,128)(2,1)}) %all-gather.5.cloned.1.call-update) | async-done | bytes 12582928 | tf_op jit(solution)/shard_map/all_gather | solution.py:173
  135.0 1.5 dynamic_slice.19
  136.5 3.4 collective-permute-start.9
  139.9 38.3 %collective-permute-done.1.refs_6_ = bf16[3584,1024]{1,0:T(8,128)(2,1)} collective-permute-done((bf16[3584,1024]{1,0:T(8,128)(2,1)}, bf16[3584,1024]{1,0:T(8,128)(2,1)}, u32[]{:S(2)}, u32[]{:S(2)}) %collective-permute-start.1) | collective-permute-done | bytes 7340064 | tf_op jit(solution)/shard_map/ppermute | solution.py:155
  178.2 35.6 %collective-permute-done.9 = bf16[192,4096]{1,0:T(8,128)(2,1)} collective-permute-done((bf16[192,4096]{1,0:T(8,128)(2,1)S(1)}, bf16[192,4096]{1,0:T(8,128)(2,1)}, u32[]{:S(2)}, u32[]{:S(2)}) %collective-permute-start.9) | collective-permute-done | bytes 1572896 | tf_op jit(solution)/shard_map/ppermute | solution.py:161
  213.8 3.1 collective-permute-start.10
  216.9 3.1 fusion.16
  220.0 10.3 %fusion.5 = f32[768,64]{0,1:T(8,128)} fusion(bf16[768,3584]{1,0:T(8,128)(2,1)} %param.14, bf16[768,3584]{1,0:T(8,128)(2,1)} %refs_8_.1, bf16[3584,128]{1,0:T(8,128)(2,1)} %refs_11_.3), kind=kOutput, calls=%fused_computation.7 | convolution fusion | flops 374341632 | bytes 12124160 | tf_op jit(solution)/shard_map/dot_general | solution.py:196
  230.3 6.0 %fusion.41 = f32[1024,256]{1,0:T(8,128)S(1)} fusion(f32[1024,2048]{1,0:T(8,128)} %param.20, bf16[2048,256]{0,1:T(8,128)(2,1)} %all-gather.7.cloned.1.call-done), kind=kOutput, calls=%fused_computation.64 | convolution fusion | flops 3221225472 | bytes 10485760 | tf_op jit(solution)/shard_map/dot_general | solution.py:208
  238.1 1.6 collective-permute-start.5
  241.0 1.5 collective-permute-start.3
  242.5 11.8 %collective-permute-done.5 = f32[512,256]{1,0:T(8,128)} collective-permute-done((f32[512,256]{1,0:T(8,128)}, f32[512,256]{1,0:T(8,128)}, u32[]{:S(2)}, u32[]{:S(2)}) %collective-permute-start.5) | collective-permute-done | bytes 524320 | tf_op jit(solution)/shard_map/ppermute | solution.py:155
  255.6 1.5 collective-permute-start.6
  257.1 1.5 collective-permute-done.3
  259.7 10.1 %collective-permute-done.6 = f32[256,256]{1,0:T(8,128)S(1)} collective-permute-done((f32[256,256]{1,0:T(8,128)S(1)}, f32[256,256]{1,0:T(8,128)S(1)}, u32[]{:S(2)}, u32[]{:S(2)}) %collective-permute-start.6) | collective-permute-done | bytes 262176 | tf_op jit(solution)/shard_map/ppermute | solution.py:155
  269.9 2.0 collective-permute-start.7
  271.9 4.0 slice.40
  275.9 8.0 %collective-permute-done.7 = f32[256,256]{1,0:T(8,128)S(1)} collective-permute-done((f32[256,256]{1,0:T(8,128)S(1)}, f32[256,256]{1,0:T(8,128)S(1)}, u32[]{:S(2)}, u32[]{:S(2)}) %collective-permute-start.7) | collective-permute-done | bytes 262176 | tf_op jit(solution)/shard_map/ppermute | solution.py:155
  285.3 2.7 collective-permute-done.4
  288.0 3.9 collective-permute-start.13
  292.0 2.1 slice.38
  294.1 2.7 slice.39
  299.6 10.7 %collective-permute-done.8 = f32[512,256]{1,0:T(8,128)} collective-permute-done((f32[512,256]{1,0:T(8,128)}, f32[512,256]{1,0:T(8,128)}, u32[]{:S(2)}, u32[]{:S(2)}) %collective-permute-start.8) | collective-permute-done | bytes 524320 | tf_op jit(solution)/shard_map/ppermute | solution.py:155
  310.3 3.8 collective-permute-start.14
  314.1 9.1 %fusion.7.other = f32[256,2048]{1,0:T(8,128)} fusion(f32[1024,2048]{1,0:T(8,128)} %param.20, f32[512,256]{1,0:T(8,128)} %collective-permute-done.8, f32[512,256]{1,0:T(8,128)} %maximum_select_fusion.2, pred[]{:T(512)S(6)} %eq.29), kind=kOutput, calls=%fused_computation.9 | convolution fusion | flops 3222011904 | bytes 11534337 | tf_op jit(solution)/shard_map/dot_general | solution.py:228
  323.2 1.9 collective-permute-start.12
  325.2 34.7 %shard_map.130 = f32[768,128]{1,0:T(8,128)} custom-call(s32[4]{0:T(128)} %get-tuple-element.22.idx, bf16[768,8192]{1,0:T(8,128)(2,1)} %all-gather.5.cloned.1.call-done.refs_0_.refs_1_.refs_2_.refs_3_, bf16[768,8192]{1,0:T(8,128)(2,1)} %all-gather.5.cloned.1.call-done.refs_0_.refs_1_.refs_2_.refs_3_, ...), custom_call_target="tpu_custom_call" | custom-call | flops 23957864448 | bytes 46661632 | tf_op jit(solution)/shard_map/pallas_call | solution.py:63
  361.1 5.9 %collective-permute-start.11 = (bf16[768,512]{1,0:T(8,128)(2,1)}, bf16[768,512]{1,0:T(8,128)(2,1)}, u32[]{:S(2)}, u32[]{:S(2)}) collective-permute-start(bf16[768,512]{1,0:T(8,128)(2,1)} %slice.38), channel_id=1, source_target_pairs={{0,24},{4,28},{24,0},{28,4},{1,25},{5,29},{25,1},{29,5},{2,26},{6,... | collective-permute-start | bytes 2359304 | tf_op jit(solution)/shard_map/ppermute | solution.py:161
  367.0 1.6 copy-done.3
  368.7 22.4 %shard_map.131.refs_10_ = f32[768,128]{1,0:T(8,128)} custom-call(s32[4]{0:T(128)} %get-tuple-element.11.idx, bf16[768,4096]{1,0:T(8,128)(2,1)} %all-gather.9.cloned.1.call-done.refs_0_.refs_1_.refs_2_.refs_3_, bf16[768,4096]{1,0:T(8,128)(2,1)} %all-gather.9.cloned.1.call-done.refs_0_.refs_1_.refs_2_.refs_3_, ...), custom_call_target="tpu_custom_call" | custom-call | flops 13690208256 | bytes 29360128 | tf_op jit(solution)/shard_map/pallas_call | solution.py:63
  391.1 7.8 %collective-permute-done.12.refs_9_ = bf16[768,1024]{1,0:T(8,128)(2,1)} collective-permute-done((bf16[768,1024]{1,0:T(8,128)(2,1)}, bf16[768,1024]{1,0:T(8,128)(2,1)}, u32[]{:S(2)}, u32[]{:S(2)}) %collective-permute-start.12) | collective-permute-done | bytes 1572896 | tf_op jit(solution)/shard_map/ppermute | solution.py:161
  398.9 14.0 %shard_map.132.refs_10_ = f32[768,128]{1,0:T(8,128)} custom-call(s32[4]{0:T(128)} %get-tuple-element.11.idx, bf16[768,4096]{1,0:T(8,128)(2,1)} %all-gather.9.cloned.1.call-done.refs_0_.refs_1_.refs_2_.refs_3_, bf16[768,4096]{1,0:T(8,128)(2,1)} %all-gather.9.cloned.1.call-done.refs_0_.refs_1_.refs_2_.refs_3_, ...), custom_call_target="tpu_custom_call" | custom-call | flops 6845104128 | bytes 17825792 | tf_op jit(solution)/shard_map/pallas_call | solution.py:63
  412.9 9.9 %shard_map.133 = f32[768,128]{1,0:T(8,128)} custom-call(s32[4]{0:T(128)} %get-tuple-element.11.idx, bf16[768,4096]{1,0:T(8,128)(2,1)} %all-gather.9.cloned.1.call-done.refs_0_.refs_1_.refs_2_.refs_3_, bf16[768,4096]{1,0:T(8,128)(2,1)} %all-gather.9.cloned.1.call-done.refs_0_.refs_1_.refs_2_.refs_3_, ...), custom_call_target="tpu_custom_call" | custom-call | flops 3422552064 | bytes 12058624 | tf_op jit(solution)/shard_map/pallas_call | solution.py:63
  425.5 2.5 collective-permute-start.15
  428.9 2.8 collective-permute-done.15
  431.8 1.9 collective-permute-start.16
  434.3 1.7 collective-permute-done.16
  436.8 3.6 collective-permute-done.17
  440.5 98.8 %all-gather = f32[8,6,4096]{2,1,0:T(8,128)S(1)} all-gather(f32[1,6,4096]{2,1,0:T(8,128)S(1)} %maximum_bitcast_fusion), channel_id=1, replica_groups=mesh['fsdp'=8,'solve'=4] {'fsdp'}, dimensions={0}, use_global_device_ids=true | all-gather | bytes 884736 | tf_op jit(solution)/shard_map/all_gather | solution.py:268
  540.3 4.4 shard_map.134
  547.4 3.8 collective-permute-done.19
  552.0 4.0 collective-permute-done.20
  557.4 2.3 collective-permute-done.21
  559.8 1.5 collective-permute-start.22
  561.3 5.3 shard_map.135.refs_0_
  566.6 5.4 shard_map.136
  (82 shorter events, 23.2 us)
Async XLA Ops:
  7.2 232.6 %copy-start = (bf16[768,2048]{1,0:T(8,128)(2,1)S(1)}, bf16[768,2048]{1,0:T(8,128)(2,1)}, u32[]{:S(2)}) copy-start(bf16[768,2048]{1,0:T(8,128)(2,1)} %param.11) | copy-start | bytes 9437188
  7.2 127.8 %all-gather.5.cloned.1.call-start = ((), (), s32[]{:S(2)}) async-start(), calls=%async_computation | async-start | bytes 15728640 | tf_op jit(solution)/shard_map/all_gather | solution.py:173
  7.9 222.3 %all-gather.7.cloned.1.call-start = ((), (), s32[]{:S(2)}) async-start(), calls=%async_computation.1 | async-start | bytes 1179648 | tf_op jit(solution)/shard_map/all_gather | solution.py:207
  8.0 170.2 %collective-permute-start.1 = (bf16[3584,1024]{1,0:T(8,128)(2,1)}, bf16[3584,1024]{1,0:T(8,128)(2,1)}, u32[]{:S(2)}, u32[]{:S(2)}) collective-permute-start(bf16[3584,1024]{1,0:T(8,128)(2,1)} %refs_4_.7), channel_id=1, source_target_pairs={{0,8},{4,12},{8,0},{12,4},{16,24},{20,28},{24,16},{28,20},{1,9},{5... | collective-permute-start | bytes 22020104 | tf_op jit(solution)/shard_map/ppermute | solution.py:155
  12.7 354.3 %all-gather.9.cloned.1.call-start = ((), (), s32[]{:S(2)}) async-start(), calls=%async_computation.2 | async-start | bytes 7864320 | tf_op jit(solution)/shard_map/all_gather | solution.py:178
  136.5 77.3 %collective-permute-start.9 = (bf16[192,4096]{1,0:T(8,128)(2,1)S(1)}, bf16[192,4096]{1,0:T(8,128)(2,1)}, u32[]{:S(2)}, u32[]{:S(2)}) collective-permute-start(bf16[192,4096]{1,0:T(8,128)(2,1)S(1)} %dynamic_slice.19), channel_id=1, source_target_pairs={{0,24},{4,28},{8,16},{12,20},{16,8},{20,12},{24,0},{28,4},{1,25},{... | collective-permute-start | bytes 4718600 | tf_op jit(solution)/shard_map/ppermute | solution.py:161
  139.9 183.4 %collective-permute-start = (bf16[3584,1024]{1,0:T(8,128)(2,1)}, bf16[3584,1024]{1,0:T(8,128)(2,1)}, u32[]{:S(2)}, u32[]{:S(2)}) collective-permute-start(bf16[3584,1024]{1,0:T(8,128)(2,1)} %refs_4_.7), channel_id=1, source_target_pairs={{0,4},{4,0},{8,12},{12,8},{16,20},{20,16},{24,28},{28,24},{1,5},{5... | collective-permute-start | bytes 22020104 | tf_op jit(solution)/shard_map/ppermute | solution.py:155
  178.2 147.0 %collective-permute-start.2 = (bf16[3584,1024]{1,0:T(8,128)(2,1)}, bf16[3584,1024]{1,0:T(8,128)(2,1)}, u32[]{:S(2)}, u32[]{:S(2)}) collective-permute-start(bf16[3584,1024]{1,0:T(8,128)(2,1)} %collective-permute-done.1.refs_6_), channel_id=1, source_target_pairs={{0,4},{4,0},{8,12},{12,8},{16,20},{20,16},{24,28},{28,24},{1,5},{5... | collective-permute-start | bytes 22020104 | tf_op jit(solution)/shard_map/ppermute | solution.py:155
  213.8 153.2 %collective-permute-start.10 = (bf16[768,3584]{1,0:T(8,128)(2,1)}, bf16[768,3584]{1,0:T(8,128)(2,1)}, u32[]{:S(2)}, u32[]{:S(2)}) collective-permute-start(bf16[768,3584]{1,0:T(8,128)(2,1)} %refs_8_.1), channel_id=1, source_target_pairs={{8,16},{12,20},{16,8},{20,12},{9,17},{13,21},{17,9},{21,13},{10,18... | collective-permute-start | bytes 16515080 | tf_op jit(solution)/shard_map/ppermute | solution.py:161
  230.3 9.5 %copy-start.5 = (bf16[2048,128]{1,0:T(8,128)(2,1)S(1)}, bf16[2048,128]{1,0:T(8,128)(2,1)}, u32[]{:S(2)}) copy-start(bf16[2048,128]{1,0:T(8,128)(2,1)} %param.16) | copy-start | bytes 1572868
  230.3 10.7 %copy-start.7 = (f32[768,64]{0,1:T(8,128)S(1)}, f32[768,64]{0,1:T(8,128)}, u32[]{:S(2)}) copy-start(f32[768,64]{0,1:T(8,128)} %fusion.5) | copy-start | bytes 589828
  236.3 1.0 copy-start.2
  238.1 16.2 %collective-permute-start.5 = (f32[512,256]{1,0:T(8,128)}, f32[512,256]{1,0:T(8,128)}, u32[]{:S(2)}, u32[]{:S(2)}) collective-permute-start(f32[512,256]{1,0:T(8,128)} %constant_dynamic-slice_fusion.1), channel_id=1, source_target_pairs={{0,2},{1,3},{2,0},{3,1},{4,6},{5,7},{6,4},{7,5},{8,10},{9,11},{10,... | collective-permute-start | bytes 1572872 | tf_op jit(solution)/shard_map/ppermute | solution.py:155
  240.9 34.9 %copy-start.11 = (s32[3]{0:T(128)S(1)}, s32[3]{0:T(128)}, u32[]{:S(2)}) copy-start(s32[3]{0:T(128)} %param.18) | copy-start | bytes 40
  241.0 17.7 %collective-permute-start.3 = (f32[768,192]{0,1:T(8,128)S(1)}, f32[768,192]{0,1:T(8,128)S(1)}, u32[]{:S(2)}, u32[]{:S(2)}) collective-permute-start(f32[768,192]{0,1:T(8,128)S(1)} %pad_maximum_fusion), channel_id=1, source_target_pairs={{0,1},{1,0},{2,3},{3,2},{4,5},{5,4},{6,7},{7,6},{8,9},{9,8},{10,11... | collective-permute-start | bytes 1769480 | tf_op jit(solution)/shard_map/ppermute | solution.py:155
  255.6 14.2 %collective-permute-start.6 = (f32[256,256]{1,0:T(8,128)S(1)}, f32[256,256]{1,0:T(8,128)S(1)}, u32[]{:S(2)}, u32[]{:S(2)}) collective-permute-start(f32[256,256]{1,0:T(8,128)S(1)} %constant_dynamic-slice_fusion), channel_id=1, source_target_pairs={{0,1},{1,0},{2,3},{3,2},{4,5},{5,4},{6,7},{7,6},{8,9},{9,8},{10,11... | collective-permute-start | bytes 786440 | tf_op jit(solution)/shard_map/ppermute | solution.py:155
  259.6 25.6 %copy-start.4 = (f32[768,192]{0,1:T(8,128)}, f32[768,192]{0,1:T(8,128)S(1)}, u32[]{:S(2)}) copy-start(f32[768,192]{0,1:T(8,128)S(1)} %fusion.39) | copy-start | bytes 1769476
  259.7 28.4 %collective-permute-start.4 = (f32[768,192]{0,1:T(8,128)S(1)}, f32[768,192]{0,1:T(8,128)}, u32[]{:S(2)}, u32[]{:S(2)}) collective-permute-start(f32[768,192]{0,1:T(8,128)S(1)} %fusion.39), channel_id=1, source_target_pairs={{0,2},{1,3},{2,0},{3,1},{4,6},{5,7},{6,4},{7,5},{8,10},{9,11},{10,... | collective-permute-start | bytes 1769480 | tf_op jit(solution)/shard_map/ppermute | solution.py:155
  269.8 15.4 %copy-start.6 = (f32[256,256]{1,0:T(8,128)}, f32[256,256]{1,0:T(8,128)S(1)}, u32[]{:S(2)}) copy-start(f32[256,256]{1,0:T(8,128)S(1)} %dynamic-slice_add_fusion.1) | copy-start | bytes 786436
  269.9 14.1 %collective-permute-start.7 = (f32[256,256]{1,0:T(8,128)S(1)}, f32[256,256]{1,0:T(8,128)S(1)}, u32[]{:S(2)}, u32[]{:S(2)}) collective-permute-start(f32[256,256]{1,0:T(8,128)S(1)} %dynamic-slice_add_fusion.1), channel_id=1, source_target_pairs={{0,1},{1,0},{2,3},{3,2},{4,5},{5,4},{6,7},{7,6},{8,9},{9,8},{10,11... | collective-permute-start | bytes 786440 | tf_op jit(solution)/shard_map/ppermute | solution.py:155
  284.8 25.5 %collective-permute-start.8 = (f32[512,256]{1,0:T(8,128)}, f32[512,256]{1,0:T(8,128)}, u32[]{:S(2)}, u32[]{:S(2)}) collective-permute-start(f32[512,256]{1,0:T(8,128)} %maximum_select_fusion.2), channel_id=1, source_target_pairs={{0,2},{1,3},{2,0},{3,1},{4,6},{5,7},{6,4},{7,5},{8,10},{9,11},{10,... | collective-permute-start | bytes 1572872 | tf_op jit(solution)/shard_map/ppermute | solution.py:155
  288.0 79.0 %collective-permute-start.13 = (bf16[768,2048]{1,0:T(8,128)(2,1)}, bf16[768,2048]{1,0:T(8,128)(2,1)S(1)}, u32[]{:S(2)}, u32[]{:S(2)}) collective-permute-start(bf16[768,2048]{1,0:T(8,128)(2,1)} %slice.40), channel_id=1, source_target_pairs={{0,24},{4,28},{24,0},{28,4},{1,25},{5,29},{25,1},{29,5},{2,26},{6,... | collective-permute-start | bytes 9437192 | tf_op jit(solution)/shard_map/ppermute | solution.py:161
  310.3 113.7 %collective-permute-start.14 = (bf16[768,64]{0,1:T(8,128)(2,1)}, bf16[768,64]{0,1:T(8,128)(2,1)}, u32[]{:S(2)}, u32[]{:S(2)}) collective-permute-start(bf16[768,64]{0,1:T(8,128)(2,1)} %get-tuple-element.19), channel_id=1, source_target_pairs={{0,24},{4,28},{8,16},{12,20},{16,8},{20,12},{24,0},{28,4},{1,25},{... | collective-permute-start | bytes 294920 | tf_op jit(solution)/shard_map/ppermute | solution.py:161
  323.2 75.6 %collective-permute-start.12 = (bf16[768,1024]{1,0:T(8,128)(2,1)}, bf16[768,1024]{1,0:T(8,128)(2,1)}, u32[]{:S(2)}, u32[]{:S(2)}) collective-permute-start(bf16[768,1024]{1,0:T(8,128)(2,1)} %slice.39), channel_id=1, source_target_pairs={{0,24},{4,28},{24,0},{28,4},{1,25},{5,29},{25,1},{29,5},{2,26},{6,... | collective-permute-start | bytes 4718600 | tf_op jit(solution)/shard_map/ppermute | solution.py:161
  361.1 51.9 %collective-permute-start.11 = (bf16[768,512]{1,0:T(8,128)(2,1)}, bf16[768,512]{1,0:T(8,128)(2,1)}, u32[]{:S(2)}, u32[]{:S(2)}) collective-permute-start(bf16[768,512]{1,0:T(8,128)(2,1)} %slice.38), channel_id=1, source_target_pairs={{0,24},{4,28},{24,0},{28,4},{1,25},{5,29},{25,1},{29,5},{2,26},{6,... | collective-permute-start | bytes 2359304 | tf_op jit(solution)/shard_map/ppermute | solution.py:161
  367.0 1.7 copy-start.3
  412.9 15.1 %copy-start.10 = (f32[768,64]{0,1:T(8,128)S(1)}, f32[768,64]{0,1:T(8,128)}, u32[]{:S(2)}) copy-start(f32[768,64]{0,1:T(8,128)} %get-tuple-element.20) | copy-start | bytes 589828
  412.9 23.5 %copy-start.8 = (f32[768,64]{0,1:T(8,128)S(1)}, f32[768,64]{0,1:T(8,128)}, u32[]{:S(2)}) copy-start(f32[768,64]{0,1:T(8,128)} %get-tuple-element.23) | copy-start | bytes 589828
  412.9 23.5 %copy-start.9 = (f32[768,64]{0,1:T(8,128)S(1)}, f32[768,64]{0,1:T(8,128)}, u32[]{:S(2)}) copy-start(f32[768,64]{0,1:T(8,128)} %get-tuple-element.24) | copy-start | bytes 589828
  425.5 6.2 %collective-permute-start.15 = (f32[3,4096]{1,0:T(4,128)S(1)}, f32[3,4096]{1,0:T(4,128)S(1)}, u32[]{:S(2)}, u32[]{:S(2)}) collective-permute-start(f32[3,4096]{1,0:T(4,128)S(1)} %reshape.102), channel_id=1, source_target_pairs={{0,24},{4,28},{8,16},{12,20},{16,8},{20,12},{24,0},{28,4},{1,25},{... | collective-permute-start | bytes 147464 | tf_op jit(solution)/shard_map/ppermute | solution.py:161
  431.8 4.3 collective-permute-start.16
  436.1 4.3 collective-permute-start.17
  545.5 1.2 collective-permute-start.18
  547.4 3.8 collective-permute-start.19
  551.2 4.7 collective-permute-start.20
  556.0 3.8 collective-permute-start.21
  559.8 12.2 %collective-permute-start.22 = (f32[24,256]{1,0:T(8,128)S(1)}, f32[24,256]{1,0:T(8,128)S(1)}, u32[]{:S(2)}, u32[]{:S(2)}) collective-permute-start(f32[24,256]{1,0:T(8,128)S(1)} %add.106), channel_id=1, source_target_pairs={{0,2},{1,3},{2,0},{3,1},{4,6},{5,7},{6,4},{7,5},{8,10},{9,11},{10,... | collective-permute-start | bytes 73736 | tf_op jit(solution)/shard_map/ppermute | solution.py:155
  566.6 6.1 %copy-start.1 = (bf16[768,2048]{1,0:T(8,128)(2,1)S(1)}, bf16[768,2048]{1,0:T(8,128)(2,1)}, u32[]{:S(2)}) copy-start(bf16[768,2048]{1,0:T(8,128)(2,1)} %param.11) | copy-start | bytes 9437188
Sparse Core Ops, SparseCore 0:
  9.8 125.0 all-gather.4
  137.1 27.8 all-gather.6
  213.9 97.5 all-gather.8

commit v4 on v3

--- a/solution.py
+++ b/solution.py
@@ -78,7 +78,7 @@
     )(idx, *operands)
 
 
-def features_kernel(examples, seqs, idx, both, other, left_out, right_out, scores):
+def features_kernel(examples, seqs, count, idx, both, other, left_out, right_out, scores):
     f32 = jnp.float32
     shape = (examples, both.shape[0])
     pick = lax.broadcasted_iota(jnp.int32, shape, 1)
@@ -108,13 +108,14 @@
     right = part(idx[1], right_out.shape[1])
     high, low = split(right)
     right_out[...] = jnp.concatenate([high, high, low], axis=0)
-    scores[...] = lax.dot_general(
+    product = lax.dot_general(
         right,
         other[...],
         (((1,), (1,)), ((), ())),
         precision=lax.Precision.HIGHEST,
         preferred_element_type=f32,
     )
+    scores[...] = product / jnp.sqrt(f32(count))
 
 
 def gram_kernel(scale, gram, left, right, *refs):
@@ -154,6 +155,17 @@
     def swap(x, axis, size, bit):
         return lax.ppermute(x, axis, [(i, i ^ bit) for i in range(size)])
 
+    def total(x, axis, size):
+        bit = 1
+        while bit < size:
+            if 2 * bit < size:
+                one, two, both = (swap(x, axis, size, b) for b in (bit, 2 * bit, 3 * bit))
+                x = (x + one) + (two + both)
+            else:
+                x = x + swap(x, axis, size, bit)
+            bit *= 4
+        return x
+
     mirror_of = [(chips - 1 - i // 2) * 2 + i % 2 for i in range(n)]
 
     def mirror(x, keep=lambda chip: True):
@@ -199,10 +211,7 @@
         ],
         axis=1,
     )
-    bit = 1
-    while bit < m:
-        early = early + swap(early, "solve", m, bit)
-        bit *= 2
+    early = total(early, "solve", m)
 
     query_block = lax.all_gather(queries.astype(jnp.bfloat16), "fsdp", axis=1, tiled=True)
     partial = jnp.dot(inverse_factor, query_block.astype(f32), precision=lax.Precision.HIGH)
@@ -261,10 +270,7 @@
         far = tokens(far_idx, cot_far, [(v, a) for v in weights], gates, far, proj_hidden, a, b - a)
     up_far = pair(far[:, half:], in_up_far)
     up = up_own + mirror(up_far)
-    bit = 1
-    while bit < m:
-        up = up + swap(up, "solve", m, bit)
-        bit *= 2
+    up = total(up, "solve", m)
     both = lax.all_gather(jnp.concatenate([up, down], axis=0), "fsdp", axis=0, tiled=True)
 
     examples = n * local_seqs
@@ -273,7 +279,7 @@
     count = queries.shape[1] * n
     at = jnp.stack([f * row_width, s * col_width]).astype(jnp.int32)
     left, right, scores = pl.pallas_call(
-        functools.partial(features_kernel, examples, local_seqs),
+        functools.partial(features_kernel, examples, local_seqs, 2 * half * half),
         out_shape=(
             jax.ShapeDtypeStruct((3 * examples, row_width), jnp.bfloat16),
             jax.ShapeDtypeStruct((3 * examples, col_width), jnp.bfloat16),
@@ -281,13 +287,8 @@
         ),
         in_specs=[pl.BlockSpec(memory_space=pltpu.SMEM)] + [pl.BlockSpec(memory_space=pltpu.VMEM)] * 2,
     )(at, both, query_side)
-    total = 2 * half * half
-    scores = scores / jnp.sqrt(f32(total))
-    for axis, size in (("fsdp", n), ("solve", m)):
-        bit = 1
-        while bit < size:
-            scores = scores + swap(scores, axis, size, bit)
-            bit *= 2
+    scores = total(scores, "fsdp", n)
+    scores = total(scores, "solve", m)
     block = 128
     steps = row_width // block
     ends = [0, steps // 2, steps]

time: 580 us -> 574 us (0.990)
  blocking collectives: 98.8 us -> 60 us
  waiting for transfers between devices: 269 us -> 298 us
  starting transfers between devices: 41.4 us -> 50.7 us
  matrix products: 32.1 us -> 24.7 us
    all_gather x1, blocking collectives: 98.8 us -> 60 us  [local(): lax.all_gather(jnp.concatenate([up, down], axis=0), 'fsdp', axis=0, tiled...]
    ppermute x7, waiting for transfers between devices: 46.2 us -> 66.5 us  [mirror(): return lax.ppermute(x, 'fsdp', pairs)]
    ppermute x16 -> x20, starting transfers between devices: 16.7 us -> 26.7 us  [swap(): return lax.ppermute(x, axis, [(i, i ^ bit) for i in range(size)])]
    ppermute x16 -> x20, waiting for transfers between devices: 99.5 us -> 108 us  [swap(): return lax.ppermute(x, axis, [(i, i ^ bit) for i in range(size)])]
  transfers between devices with their start and end apart: 26 -> 30, of which waited for: 17 -> 16; matrix products, arithmetic and copies ran while one was open for 9% -> 8% of each run, Pallas kernels for 16% -> 16%
where the time goes in v4:
time: 574 us; the launch traced here: 573 us
  waiting for transfers between devices  298 us (52%)
  Pallas kernels  96.2 us (17%)
  blocking collectives  60 us (10%)
  starting transfers between devices  50.7 us (9%)
  matrix products  24.7 us (4%)
  local copies, waits for them, and re-layouts  19.3 us (3%)
  between operations  14 us (2%)
  other arithmetic  10.4 us (2%)
    all_gather x1, waiting for transfers between devices, local(): cot_full = lax.all_gather(cotangent, 'solve', axis=1, tiled=True)  122 us
    ppermute x20, waiting for transfers between devices, swap(): return lax.ppermute(x, axis, [(i, i ^ bit) for i in range(size)])  108 us
    pallas_call x4, Pallas kernels, tokens(): pl.pallas_call(functools.partial(tokens_kernel, count, len(gate_parts), s...  81.1 us
    ppermute x7, waiting for transfers between devices, mirror(): return lax.ppermute(x, 'fsdp', pairs)  66.5 us
    all_gather x1, blocking collectives, local(): lax.all_gather(jnp.concatenate([up, down], axis=0), 'fsdp', axis=0, tiled...  60 us
    ppermute x20, starting transfers between devices, swap(): return lax.ppermute(x, axis, [(i, i ^ bit) for i in range(size)])  26.7 us
    ppermute x7, starting transfers between devices, mirror(): return lax.ppermute(x, 'fsdp', pairs)  23.8 us
  transfers between devices with their start and end apart: 30, of which 16 were waited for; matrix products, arithmetic and copies ran while one was open for 8% of the time, Pallas kernels for 16%

profile of v4, /device:TPU:0, one launch (start us, length us, event | category | flops | bytes accessed | tf_op | source)
XLA Modules:
  0.0 573.1 jit_solution(12656257000722221239)
XLA Ops:
  8.0 3.1 collective-permute-start.1
  11.1 1.6 convert_element_type.29
  12.8 122.2 %all-gather.5.cloned.1.call-done.refs_0_.refs_1_.refs_2_.refs_3_ = bf16[768,8192]{1,0:T(8,128)(2,1)} async-done(((bf16[768,2048]{1,0:T(8,128)(2,1)}), bf16[768,8192]{1,0:T(8,128)(2,1)}) %all-gather.5.cloned.1.call-update) | async-done | bytes 12582928 | tf_op jit(solution)/shard_map/all_gather | solution.py:185
  135.0 1.5 dynamic_slice.19
  136.5 3.4 collective-permute-start.10
  139.9 38.3 %collective-permute-done.1.refs_6_ = bf16[3584,1024]{1,0:T(8,128)(2,1)} collective-permute-done((bf16[3584,1024]{1,0:T(8,128)(2,1)}, bf16[3584,1024]{1,0:T(8,128)(2,1)}, u32[]{:S(2)}, u32[]{:S(2)}) %collective-permute-start.1) | collective-permute-done | bytes 7340064 | tf_op jit(solution)/shard_map/ppermute | solution.py:156
  178.2 35.6 %collective-permute-done.10 = bf16[192,4096]{1,0:T(8,128)(2,1)} collective-permute-done((bf16[192,4096]{1,0:T(8,128)(2,1)S(1)}, bf16[192,4096]{1,0:T(8,128)(2,1)}, u32[]{:S(2)}, u32[]{:S(2)}) %collective-permute-start.10) | collective-permute-done | bytes 1572896 | tf_op jit(solution)/shard_map/ppermute | solution.py:173
  213.8 3.1 collective-permute-start.11
  216.9 6.2 %fusion.39 = f32[1024,256]{1,0:T(8,128)S(1)} fusion(f32[1024,2048]{1,0:T(8,128)} %param.20, bf16[2048,256]{0,1:T(8,128)(2,1)} %all-gather.7.cloned.1.call-done), kind=kOutput, calls=%fused_computation.65 | convolution fusion | flops 3221225472 | bytes 10485760 | tf_op jit(solution)/shard_map/dot_general | solution.py:217
  226.4 7.1 %fusion.5 = f32[768,64]{0,1:T(8,128)} fusion(bf16[768,3584]{1,0:T(8,128)(2,1)} %param.14, bf16[768,3584]{1,0:T(8,128)(2,1)} %refs_8_.1, bf16[3584,128]{1,0:T(8,128)(2,1)S(1)} %copy-done.3), kind=kOutput, calls=%fused_computation.7 | convolution fusion | flops 374341632 | bytes 12124160 | tf_op jit(solution)/shard_map/dot_general | solution.py:208
  234.6 15.9 %collective-permute-done.6 = f32[512,256]{1,0:T(8,128)} collective-permute-done((f32[512,256]{1,0:T(8,128)}, f32[512,256]{1,0:T(8,128)}, u32[]{:S(2)}, u32[]{:S(2)}) %collective-permute-start.6) | collective-permute-done | bytes 524320 | tf_op jit(solution)/shard_map/ppermute | solution.py:156
  254.7 2.2 fusion.14
  257.9 1.7 collective-permute-start.4
  261.2 1.5 collective-permute-start.8
  263.4 21.3 %collective-permute-done.4 = f32[768,192]{0,1:T(8,128)S(1)} collective-permute-done((f32[768,192]{0,1:T(8,128)S(1)}, f32[768,192]{0,1:T(8,128)S(1)}, u32[]{:S(2)}, u32[]{:S(2)}) %collective-permute-start.4) | collective-permute-done | bytes 589856 | tf_op jit(solution)/shard_map/ppermute | solution.py:156
  284.7 2.5 collective-permute-start.5
  287.2 1.8 collective-permute-start.3
  289.6 2.2 slice.38
  291.8 2.7 slice.39
  294.6 4.1 slice.40
  298.8 15.6 %collective-permute-done.5 = f32[768,192]{0,1:T(8,128)S(1)} collective-permute-done((f32[768,192]{0,1:T(8,128)S(1)}, f32[768,192]{0,1:T(8,128)S(1)}, u32[]{:S(2)}, u32[]{:S(2)}) %collective-permute-start.5) | collective-permute-done | bytes 589856 | tf_op jit(solution)/shard_map/ppermute | solution.py:156
  314.4 2.6 collective-permute-start.9
  317.0 8.6 %collective-permute-done.3 = f32[768,192]{0,1:T(8,128)} collective-permute-done((f32[768,192]{0,1:T(8,128)S(1)}, f32[768,192]{0,1:T(8,128)}, u32[]{:S(2)}, u32[]{:S(2)}) %collective-permute-start.3) | collective-permute-done | bytes 589856 | tf_op jit(solution)/shard_map/ppermute | solution.py:156
  325.7 5.7 collective-permute-start.14
  331.4 1.6 add_add_fusion
  334.1 5.6 fusion.7.other
  339.7 5.6 collective-permute-start.13
  345.3 34.7 %shard_map.130 = f32[768,128]{1,0:T(8,128)} custom-call(s32[4]{0:T(128)} %get-tuple-element.22.idx, bf16[768,8192]{1,0:T(8,128)(2,1)} %all-gather.5.cloned.1.call-done.refs_0_.refs_1_.refs_2_.refs_3_, bf16[768,8192]{1,0:T(8,128)(2,1)} %all-gather.5.cloned.1.call-done.refs_0_.refs_1_.refs_2_.refs_3_, ...), custom_call_target="tpu_custom_call" | custom-call | flops 23957864448 | bytes 46661632 | tf_op jit(solution)/shard_map/pallas_call | solution.py:63
  381.1 2.3 collective-permute-start.12
  383.4 17.2 %collective-permute-done.14.refs_9_ = bf16[768,2048]{1,0:T(8,128)(2,1)S(1)} collective-permute-done((bf16[768,2048]{1,0:T(8,128)(2,1)}, bf16[768,2048]{1,0:T(8,128)(2,1)S(1)}, u32[]{:S(2)}, u32[]{:S(2)}) %collective-permute-start.14) | collective-permute-done | bytes 3145760 | tf_op jit(solution)/shard_map/ppermute | solution.py:173
  400.6 1.7 copy-done.5
  402.3 22.4 %shard_map.131.refs_10_ = f32[768,128]{1,0:T(8,128)} custom-call(s32[4]{0:T(128)} %get-tuple-element.11.idx, bf16[768,4096]{1,0:T(8,128)(2,1)} %all-gather.9.cloned.1.call-done.refs_0_.refs_1_.refs_2_.refs_3_, bf16[768,4096]{1,0:T(8,128)(2,1)} %all-gather.9.cloned.1.call-done.refs_0_.refs_1_.refs_2_.refs_3_, ...), custom_call_target="tpu_custom_call" | custom-call | flops 13690208256 | bytes 29360128 | tf_op jit(solution)/shard_map/pallas_call | solution.py:63
  424.7 11.8 %collective-permute-done.13.refs_9_ = bf16[768,1024]{1,0:T(8,128)(2,1)} collective-permute-done((bf16[768,1024]{1,0:T(8,128)(2,1)}, bf16[768,1024]{1,0:T(8,128)(2,1)}, u32[]{:S(2)}, u32[]{:S(2)}) %collective-permute-start.13) | collective-permute-done | bytes 1572896 | tf_op jit(solution)/shard_map/ppermute | solution.py:173
  436.5 14.0 %shard_map.132.refs_10_ = f32[768,128]{1,0:T(8,128)} custom-call(s32[4]{0:T(128)} %get-tuple-element.11.idx, bf16[768,4096]{1,0:T(8,128)(2,1)} %all-gather.9.cloned.1.call-done.refs_0_.refs_1_.refs_2_.refs_3_, bf16[768,4096]{1,0:T(8,128)(2,1)} %all-gather.9.cloned.1.call-done.refs_0_.refs_1_.refs_2_.refs_3_, ...), custom_call_target="tpu_custom_call" | custom-call | flops 6845104128 | bytes 17825792 | tf_op jit(solution)/shard_map/pallas_call | solution.py:63
  450.8 9.9 %shard_map.133 = f32[768,128]{1,0:T(8,128)} custom-call(s32[4]{0:T(128)} %get-tuple-element.11.idx, bf16[768,4096]{1,0:T(8,128)(2,1)} %all-gather.9.cloned.1.call-done.refs_0_.refs_1_.refs_2_.refs_3_, bf16[768,4096]{1,0:T(8,128)(2,1)} %all-gather.9.cloned.1.call-done.refs_0_.refs_1_.refs_2_.refs_3_, ...), custom_call_target="tpu_custom_call" | custom-call | flops 3422552064 | bytes 12058624 | tf_op jit(solution)/shard_map/pallas_call | solution.py:63
  463.4 3.6 collective-permute-start.16
  467.9 1.6 collective-permute-done.16
  469.5 1.7 collective-permute-start.18
  471.6 1.5 collective-permute-start.17
  473.9 2.5 collective-permute-done.19
  476.5 60.0 %all-gather = f32[8,6,4096]{2,1,0:T(8,128)S(1)} all-gather(f32[1,6,4096]{2,1,0:T(8,128)S(1)} %maximum_bitcast_fusion), channel_id=1, replica_groups=mesh['fsdp'=8,'solve'=4] {'fsdp'}, dimensions={0}, use_global_device_ids=true | all-gather | bytes 884736 | tf_op jit(solution)/shard_map/all_gather | solution.py:274
  537.5 4.4 shard_map.134
  541.9 1.7 collective-permute-start.22
  544.1 1.9 collective-permute-done.21
  546.7 1.5 collective-permute-start.23
  548.2 3.5 collective-permute-done.23
  555.2 5.3 shard_map.135.refs_0_
  560.5 5.4 shard_map.136
  (96 shorter events, 26.9 us)
Async XLA Ops:
  7.2 247.6 %copy-start = (bf16[768,2048]{1,0:T(8,128)(2,1)S(1)}, bf16[768,2048]{1,0:T(8,128)(2,1)}, u32[]{:S(2)}) copy-start(bf16[768,2048]{1,0:T(8,128)(2,1)} %param.11) | copy-start | bytes 9437188
  7.2 127.8 %all-gather.5.cloned.1.call-start = ((), (), s32[]{:S(2)}) async-start(), calls=%async_computation | async-start | bytes 15728640 | tf_op jit(solution)/shard_map/all_gather | solution.py:185
  7.9 209.0 %all-gather.7.cloned.1.call-start = ((), (), s32[]{:S(2)}) async-start(), calls=%async_computation.1 | async-start | bytes 1179648 | tf_op jit(solution)/shard_map/all_gather | solution.py:216
  8.0 170.2 %collective-permute-start.1 = (bf16[3584,1024]{1,0:T(8,128)(2,1)}, bf16[3584,1024]{1,0:T(8,128)(2,1)}, u32[]{:S(2)}, u32[]{:S(2)}) collective-permute-start(bf16[3584,1024]{1,0:T(8,128)(2,1)} %refs_4_.7), channel_id=1, source_target_pairs={{0,8},{4,12},{8,0},{12,4},{16,24},{20,28},{24,16},{28,20},{1,9},{5... | collective-permute-start | bytes 22020104 | tf_op jit(solution)/shard_map/ppermute | solution.py:156
  12.7 387.9 %all-gather.9.cloned.1.call-start = ((), (), s32[]{:S(2)}) async-start(), calls=%async_computation.2 | async-start | bytes 7864320 | tf_op jit(solution)/shard_map/all_gather | solution.py:190
  136.5 77.3 %collective-permute-start.10 = (bf16[192,4096]{1,0:T(8,128)(2,1)S(1)}, bf16[192,4096]{1,0:T(8,128)(2,1)}, u32[]{:S(2)}, u32[]{:S(2)}) collective-permute-start(bf16[192,4096]{1,0:T(8,128)(2,1)S(1)} %dynamic_slice.19), channel_id=1, source_target_pairs={{0,24},{4,28},{8,16},{12,20},{16,8},{20,12},{24,0},{28,4},{1,25},{... | collective-permute-start | bytes 4718600 | tf_op jit(solution)/shard_map/ppermute | solution.py:173
  139.9 199.8 %collective-permute-start = (bf16[3584,1024]{1,0:T(8,128)(2,1)}, bf16[3584,1024]{1,0:T(8,128)(2,1)}, u32[]{:S(2)}, u32[]{:S(2)}) collective-permute-start(bf16[3584,1024]{1,0:T(8,128)(2,1)} %refs_4_.7), channel_id=1, source_target_pairs={{0,4},{4,0},{8,12},{12,8},{16,20},{20,16},{24,28},{28,24},{1,5},{5... | collective-permute-start | bytes 22020104 | tf_op jit(solution)/shard_map/ppermute | solution.py:156
  178.2 167.0 %collective-permute-start.2 = (bf16[3584,1024]{1,0:T(8,128)(2,1)}, bf16[3584,1024]{1,0:T(8,128)(2,1)}, u32[]{:S(2)}, u32[]{:S(2)}) collective-permute-start(bf16[3584,1024]{1,0:T(8,128)(2,1)} %collective-permute-done.1.refs_6_), channel_id=1, source_target_pairs={{0,4},{4,0},{8,12},{12,8},{16,20},{20,16},{24,28},{28,24},{1,5},{5... | collective-permute-start | bytes 22020104 | tf_op jit(solution)/shard_map/ppermute | solution.py:156
  213.8 169.6 %collective-permute-start.11 = (bf16[768,3584]{1,0:T(8,128)(2,1)}, bf16[768,3584]{1,0:T(8,128)(2,1)}, u32[]{:S(2)}, u32[]{:S(2)}) collective-permute-start(bf16[768,3584]{1,0:T(8,128)(2,1)} %refs_8_.1), channel_id=1, source_target_pairs={{8,16},{12,20},{16,8},{20,12},{9,17},{13,21},{17,9},{21,13},{10,18... | collective-permute-start | bytes 16515080 | tf_op jit(solution)/shard_map/ppermute | solution.py:173
  216.9 9.4 %copy-start.3 = (bf16[3584,128]{1,0:T(8,128)(2,1)S(1)}, bf16[3584,128]{1,0:T(8,128)(2,1)}, u32[]{:S(2)}) copy-start(bf16[3584,128]{1,0:T(8,128)(2,1)} %refs_11_.3) | copy-start | bytes 2752516
  223.1 1.0 copy-start.4
  225.0 8.5 %copy-start.2 = (bf16[768,2048]{1,0:T(8,128)(2,1)S(1)}, bf16[768,2048]{1,0:T(8,128)(2,1)}, u32[]{:S(2)}) copy-start(bf16[768,2048]{1,0:T(8,128)(2,1)} %param.12) | copy-start | bytes 9437188
  225.0 8.5 %copy-start.7 = (bf16[2048,128]{1,0:T(8,128)(2,1)S(1)}, bf16[2048,128]{1,0:T(8,128)(2,1)}, u32[]{:S(2)}) copy-start(bf16[2048,128]{1,0:T(8,128)(2,1)} %param.16) | copy-start | bytes 1572868
  225.0 25.6 %collective-permute-start.6 = (f32[512,256]{1,0:T(8,128)}, f32[512,256]{1,0:T(8,128)}, u32[]{:S(2)}, u32[]{:S(2)}) collective-permute-start(f32[512,256]{1,0:T(8,128)} %constant_dynamic-slice_fusion.1), channel_id=1, source_target_pairs={{0,2},{1,3},{2,0},{3,1},{4,6},{5,7},{6,4},{7,5},{8,10},{9,11},{10,... | collective-permute-start | bytes 1572872 | tf_op jit(solution)/shard_map/ppermute | solution.py:156
  251.8 0.8 copy-start.6
  253.3 6.7 %collective-permute-start.7 = (f32[256,256]{1,0:T(8,128)}, f32[256,256]{1,0:T(8,128)}, u32[]{:S(2)}, u32[]{:S(2)}) collective-permute-start(f32[256,256]{1,0:T(8,128)} %constant_dynamic-slice_fusion), channel_id=1, source_target_pairs={{0,1},{1,0},{2,3},{3,2},{4,5},{5,4},{6,7},{7,6},{8,9},{9,8},{10,11... | collective-permute-start | bytes 786440 | tf_op jit(solution)/shard_map/ppermute | solution.py:156
  256.9 41.8 %copy-start.14 = (s32[3]{0:T(128)S(1)}, s32[3]{0:T(128)}, u32[]{:S(2)}) copy-start(s32[3]{0:T(128)} %param.18) | copy-start | bytes 40
  257.9 26.8 %collective-permute-start.4 = (f32[768,192]{0,1:T(8,128)S(1)}, f32[768,192]{0,1:T(8,128)S(1)}, u32[]{:S(2)}, u32[]{:S(2)}) collective-permute-start(f32[768,192]{0,1:T(8,128)S(1)} %pad_maximum_fusion), channel_id=1, source_target_pairs={{0,2},{1,3},{2,0},{3,1},{4,6},{5,7},{6,4},{7,5},{8,10},{9,11},{10,... | collective-permute-start | bytes 1769480 | tf_op jit(solution)/shard_map/ppermute | solution.py:156
  261.2 55.8 %copy-start.8 = (f32[256,256]{1,0:T(8,128)}, f32[256,256]{1,0:T(8,128)S(1)}, u32[]{:S(2)}) copy-start(f32[256,256]{1,0:T(8,128)S(1)} %dynamic-slice_add_fusion.1) | copy-start | bytes 786436
  261.2 26.0 %collective-permute-start.8 = (f32[256,256]{1,0:T(8,128)S(1)}, f32[256,256]{1,0:T(8,128)S(1)}, u32[]{:S(2)}, u32[]{:S(2)}) collective-permute-start(f32[256,256]{1,0:T(8,128)S(1)} %dynamic-slice_add_fusion.1), channel_id=1, source_target_pairs={{0,1},{1,0},{2,3},{3,2},{4,5},{5,4},{6,7},{7,6},{8,9},{9,8},{10,11... | collective-permute-start | bytes 786440 | tf_op jit(solution)/shard_map/ppermute | solution.py:156
  284.7 32.3 %copy-start.12 = (f32[768,192]{0,1:T(8,128)}, f32[768,192]{0,1:T(8,128)S(1)}, u32[]{:S(2)}) copy-start(f32[768,192]{0,1:T(8,128)S(1)} %collective-permute-done.4) | copy-start | bytes 1769476
  284.7 29.7 %collective-permute-start.5 = (f32[768,192]{0,1:T(8,128)S(1)}, f32[768,192]{0,1:T(8,128)S(1)}, u32[]{:S(2)}, u32[]{:S(2)}) collective-permute-start(f32[768,192]{0,1:T(8,128)S(1)} %pad_maximum_fusion), channel_id=1, source_target_pairs={{0,3},{1,2},{2,1},{3,0},{4,7},{5,6},{6,5},{7,4},{8,11},{9,10},{10,... | collective-permute-start | bytes 1769480 | tf_op jit(solution)/shard_map/ppermute | solution.py:156
  287.2 38.5 %collective-permute-start.3 = (f32[768,192]{0,1:T(8,128)S(1)}, f32[768,192]{0,1:T(8,128)}, u32[]{:S(2)}, u32[]{:S(2)}) collective-permute-start(f32[768,192]{0,1:T(8,128)S(1)} %pad_maximum_fusion), channel_id=1, source_target_pairs={{0,1},{1,0},{2,3},{3,2},{4,5},{5,4},{6,7},{7,6},{8,9},{9,8},{10,11... | collective-permute-start | bytes 1769480 | tf_op jit(solution)/shard_map/ppermute | solution.py:156
  289.6 44.5 %slice-start = ((s8[8388608]{0:T(1024)(128)(4,1)}), s8[4194304]{0:T(1024)(128)(4,1)S(1)}, s32[]{:S(2)}) async-start(s8[8388608]{0:T(1024)(128)(4,1)} %bitcast.33), calls=%async_computation.3 | async-start | bytes 8388608
  294.6 39.5 %slice-start.1 = ((s8[8388608]{0:T(1024)(128)(4,1)}), s8[4194304]{0:T(1024)(128)(4,1)S(1)}, s32[]{:S(2)}) async-start(s8[8388608]{0:T(1024)(128)(4,1)} %bitcast.33), calls=%async_computation.4 | async-start | bytes 8388608
  314.4 2.6 copy-start.13
  314.4 19.5 %collective-permute-start.9 = (f32[512,256]{1,0:T(8,128)S(1)}, f32[512,256]{1,0:T(8,128)S(1)}, u32[]{:S(2)}, u32[]{:S(2)}) collective-permute-start(f32[512,256]{1,0:T(8,128)S(1)} %maximum_select_fusion.2), channel_id=1, source_target_pairs={{0,2},{1,3},{2,0},{3,1},{4,6},{5,7},{6,4},{7,5},{8,10},{9,11},{10,... | collective-permute-start | bytes 1572872 | tf_op jit(solution)/shard_map/ppermute | solution.py:156
  325.7 74.9 %collective-permute-start.14 = (bf16[768,2048]{1,0:T(8,128)(2,1)}, bf16[768,2048]{1,0:T(8,128)(2,1)S(1)}, u32[]{:S(2)}, u32[]{:S(2)}) collective-permute-start(bf16[768,2048]{1,0:T(8,128)(2,1)} %slice.40), channel_id=1, source_target_pairs={{0,24},{4,28},{24,0},{28,4},{1,25},{5,29},{25,1},{29,5},{2,26},{6,... | collective-permute-start | bytes 9437192 | tf_op jit(solution)/shard_map/ppermute | solution.py:173
  333.9 128.0 %collective-permute-start.15 = (bf16[768,64]{0,1:T(8,128)(2,1)}, bf16[768,64]{0,1:T(8,128)(2,1)}, u32[]{:S(2)}, u32[]{:S(2)}) collective-permute-start(bf16[768,64]{0,1:T(8,128)(2,1)} %get-tuple-element.19), channel_id=1, source_target_pairs={{0,24},{4,28},{8,16},{12,20},{16,8},{20,12},{24,0},{28,4},{1,25},{... | collective-permute-start | bytes 294920 | tf_op jit(solution)/shard_map/ppermute | solution.py:173
  339.7 96.8 %collective-permute-start.13 = (bf16[768,1024]{1,0:T(8,128)(2,1)}, bf16[768,1024]{1,0:T(8,128)(2,1)}, u32[]{:S(2)}, u32[]{:S(2)}) collective-permute-start(bf16[768,1024]{1,0:T(8,128)(2,1)} %slice.39), channel_id=1, source_target_pairs={{0,24},{4,28},{24,0},{28,4},{1,25},{5,29},{25,1},{29,5},{2,26},{6,... | collective-permute-start | bytes 4718600 | tf_op jit(solution)/shard_map/ppermute | solution.py:173
  381.1 69.7 %collective-permute-start.12 = (bf16[768,512]{1,0:T(8,128)(2,1)}, bf16[768,512]{1,0:T(8,128)(2,1)}, u32[]{:S(2)}, u32[]{:S(2)}) collective-permute-start(bf16[768,512]{1,0:T(8,128)(2,1)} %slice.38), channel_id=1, source_target_pairs={{0,24},{4,28},{24,0},{28,4},{1,25},{5,29},{25,1},{29,5},{2,26},{6,... | collective-permute-start | bytes 2359304 | tf_op jit(solution)/shard_map/ppermute | solution.py:173
  400.6 1.7 copy-start.5
  450.6 16.4 %copy-start.11 = (f32[768,64]{0,1:T(8,128)S(1)}, f32[768,64]{0,1:T(8,128)}, u32[]{:S(2)}) copy-start(f32[768,64]{0,1:T(8,128)} %get-tuple-element.20) | copy-start | bytes 589828
  450.6 22.5 %copy-start.9 = (f32[768,64]{0,1:T(8,128)S(1)}, f32[768,64]{0,1:T(8,128)}, u32[]{:S(2)}) copy-start(f32[768,64]{0,1:T(8,128)} %get-tuple-element.23) | copy-start | bytes 589828
  450.6 22.5 %copy-start.10 = (f32[768,64]{0,1:T(8,128)S(1)}, f32[768,64]{0,1:T(8,128)}, u32[]{:S(2)}) copy-start(f32[768,64]{0,1:T(8,128)} %get-tuple-element.24) | copy-start | bytes 589828
  463.4 6.1 %collective-permute-start.16 = (f32[3,4096]{1,0:T(4,128)S(1)}, f32[3,4096]{1,0:T(4,128)S(1)}, u32[]{:S(2)}, u32[]{:S(2)}) collective-permute-start(f32[3,4096]{1,0:T(4,128)S(1)} %reshape.102), channel_id=1, source_target_pairs={{0,24},{4,28},{8,16},{12,20},{16,8},{20,12},{24,0},{28,4},{1,25},{... | collective-permute-start | bytes 147464 | tf_op jit(solution)/shard_map/ppermute | solution.py:173
  469.5 4.3 collective-permute-start.18
  471.2 5.2 collective-permute-start.19
  471.6 4.8 collective-permute-start.17
  541.9 4.0 collective-permute-start.21
  541.9 4.0 collective-permute-start.22
  543.6 2.3 collective-permute-start.20
  546.7 5.0 collective-permute-start.23
  551.7 14.2 %collective-permute-start.25 = (f32[24,256]{1,0:T(8,128)S(1)}, f32[24,256]{1,0:T(8,128)S(1)}, u32[]{:S(2)}, u32[]{:S(2)}) collective-permute-start(f32[24,256]{1,0:T(8,128)S(1)} %add.120), channel_id=1, source_target_pairs={{0,2},{1,3},{2,0},{3,1},{4,6},{5,7},{6,4},{7,5},{8,10},{9,11},{10,... | collective-permute-start | bytes 73736 | tf_op jit(solution)/shard_map/ppermute | solution.py:156
  552.4 13.5 %collective-permute-start.26 = (f32[24,256]{1,0:T(8,128)S(1)}, f32[24,256]{1,0:T(8,128)S(1)}, u32[]{:S(2)}, u32[]{:S(2)}) collective-permute-start(f32[24,256]{1,0:T(8,128)S(1)} %add.120), channel_id=1, source_target_pairs={{0,3},{1,2},{2,1},{3,0},{4,7},{5,6},{6,5},{7,4},{8,11},{9,10},{10,... | collective-permute-start | bytes 73736 | tf_op jit(solution)/shard_map/ppermute | solution.py:156
  553.9 12.1 %collective-permute-start.24 = (f32[24,256]{1,0:T(8,128)S(1)}, f32[24,256]{1,0:T(8,128)S(1)}, u32[]{:S(2)}, u32[]{:S(2)}) collective-permute-start(f32[24,256]{1,0:T(8,128)S(1)} %add.120), channel_id=1, source_target_pairs={{0,1},{1,0},{2,3},{3,2},{4,5},{5,4},{6,7},{7,6},{8,9},{9,8},{10,11... | collective-permute-start | bytes 73736 | tf_op jit(solution)/shard_map/ppermute | solution.py:156
  560.5 6.1 %copy-start.1 = (bf16[768,2048]{1,0:T(8,128)(2,1)S(1)}, bf16[768,2048]{1,0:T(8,128)(2,1)}, u32[]{:S(2)}) copy-start(bf16[768,2048]{1,0:T(8,128)(2,1)} %param.11) | copy-start | bytes 9437188
Sparse Core Ops, SparseCore 0:
  9.8 125.0 all-gather.4
  137.1 27.8 all-gather.6
  213.9 108.5 all-gather.8

commit v5 on v4

--- a/solution.py
+++ b/solution.py
@@ -76,6 +76,47 @@
             transcendentals=rows * TILE * tiles,
         ),
     )(idx, *operands)
+
+
+def grad_kernel(count, idx, *refs):
+    del idx
+    out = refs[-1]
+    grad = None
+    for cot, weight in zip(refs[:count], refs[count : 2 * count]):
+        term = lax.dot_general(
+            cot[...], weight[...], (((1,), (1,)), ((), ())), preferred_element_type=jnp.float32
+        )
+        grad = term if grad is None else grad + term
+    out[...] = grad
+
+
+def gradient(idx, cot, weights):
+    count = len(weights)
+    rows = cot.shape[0]
+    units, width = weights[0].shape
+    in_specs = [
+        pl.BlockSpec(
+            (rows, width), functools.partial(lambda k, i, ix: (0, ix[k]), k), pipeline_mode=pl.Buffered(1)
+        )
+        for k in range(count)
+    ]
+    in_specs += [pl.BlockSpec((TILE, width), lambda i, ix: (i, 0))] * count
+    return pl.pallas_call(
+        functools.partial(grad_kernel, count),
+        out_shape=jax.ShapeDtypeStruct((rows, units), jnp.float32),
+        grid_spec=pltpu.PrefetchScalarGridSpec(
+            num_scalar_prefetch=1,
+            grid=(units // TILE,),
+            in_specs=in_specs,
+            out_specs=pl.BlockSpec((rows, TILE), lambda i, ix: (0, i)),
+        ),
+        compiler_params=pltpu.CompilerParams(dimension_semantics=("arbitrary",)),
+        cost_estimate=pl.CostEstimate(
+            flops=2 * rows * units * count * width,
+            bytes_accessed=units * count * width * 2 + rows * count * width * 2 + rows * units * 4,
+            transcendentals=0,
+        ),
+    )(idx, *([cot] * count), *weights)
 
 
 def features_kernel(examples, seqs, count, idx, both, other, left_out, right_out, scores):
@@ -238,6 +279,7 @@
 
     own_idx = jnp.stack([f ^ k for k in order]).astype(jnp.int32)
     far_idx = own_idx - side * h
+    own_idx, query_side = lax.optimization_barrier((own_idx, query_side))
     own = tokens(
         own_idx, cot_full, [(v, 0) for v in weights], [(gate_pre, 0)], None, proj_hidden, 0, tiles
     )
@@ -262,13 +304,17 @@
     down = pair(out_down, in_down)
     up_own = pair(own[:, half:], in_up)
 
+    grad = gradient(far_idx, cot_far, weights)
     far = None
     for j, a, b, gate_outer in chunks:
-        if j == len(chunks) - 1:
-            far_idx, query_side = lax.optimization_barrier((far_idx, query_side))
-        gates = [(gate_inner, a), (gate_outer, 0)]
-        far = tokens(far_idx, cot_far, [(v, a) for v in weights], gates, far, proj_hidden, a, b - a)
-    up_far = pair(far[:, half:], in_up_far)
+        if far is not None:
+            gate_outer, far = lax.optimization_barrier((gate_outer, far))
+        units = slice(a * TILE, b * TILE)
+        gate = gate_inner[:, units].astype(f32) + gate_outer.astype(f32)
+        grad_up = (grad[:, units] * (gate * jax.nn.sigmoid(gate))).astype(jnp.bfloat16)
+        term = jnp.dot(grad_up, proj_hidden[units, half:], preferred_element_type=f32)
+        far = term if far is None else far + term
+    up_far = pair(far, in_up_far)
     up = up_own + mirror(up_far)
     up = total(up, "solve", m)
     both = lax.all_gather(jnp.concatenate([up, down], axis=0), "fsdp", axis=0, tiled=True)

time: 574 us -> 639 us (1.11)
  blocking collectives: 60 us -> 121 us
  Pallas kernels: 96.2 us -> 81.2 us
  matrix products: 24.7 us -> 38.4 us
  waiting for transfers between devices: 298 us -> 310 us
  local copies, waits for them, and re-layouts: 19.3 us -> 12.3 us
    all_gather x1, blocking collectives: 60 us -> 121 us  [local(): lax.all_gather(jnp.concatenate([up, down], axis=0), 'fsdp', axis=0, tiled...]
    pallas_call x4 -> x1, Pallas kernels: 81.1 us -> 34.7 us  [tokens(): pl.pallas_call(functools.partial(tokens_kernel, count, len(gate_parts), s...]
    pallas_call x0 -> x1, Pallas kernels: none -> 31.4 us  [gradient(): pl.pallas_call(functools.partial(grad_kernel, count), out_shape=jax.Shape...]
    dot_general x0 -> x3, matrix products: none -> 12.9 us  [local(): jnp.dot(grad_up, proj_hidden[units, half:], preferred_element_type=f32)]
    ppermute x20, waiting for transfers between devices: 108 us -> 116 us  [swap(): return lax.ppermute(x, axis, [(i, i ^ bit) for i in range(size)])]
  transfers between devices with their start and end apart: 30 -> 30, of which waited for: 16 -> 15; matrix products, arithmetic and copies ran while one was open for 8% -> 9% of each run, Pallas kernels for 16% -> 12%
where the time goes in v5:
time: 639 us; the launch traced here: 638 us
  waiting for transfers between devices  310 us (49%)
  blocking collectives  121 us (19%)
  Pallas kernels  81.2 us (13%)
  starting transfers between devices  51 us (8%)
  matrix products  38.4 us (6%)
  between operations  14.1 us (2%)
  local copies, waits for them, and re-layouts  12.3 us (2%)
  other arithmetic  10.9 us (2%)
    all_gather x1, waiting for transfers between devices, local(): cot_full = lax.all_gather(cotangent, 'solve', axis=1, tiled=True)  122 us
    all_gather x1, blocking collectives, local(): lax.all_gather(jnp.concatenate([up, down], axis=0), 'fsdp', axis=0, tiled...  121 us
    ppermute x20, waiting for transfers between devices, swap(): return lax.ppermute(x, axis, [(i, i ^ bit) for i in range(size)])  116 us
    ppermute x7, waiting for transfers between devices, mirror(): return lax.ppermute(x, 'fsdp', pairs)  70.4 us
    pallas_call x1, Pallas kernels, tokens(): pl.pallas_call(functools.partial(tokens_kernel, count, len(gate_parts), s...  34.7 us
    pallas_call x1, Pallas kernels, gradient(): pl.pallas_call(functools.partial(grad_kernel, count), out_shape=jax.Shape...  31.4 us
    ppermute x7, starting transfers between devices, mirror(): return lax.ppermute(x, 'fsdp', pairs)  27.1 us
    ppermute x20, starting transfers between devices, swap(): return lax.ppermute(x, axis, [(i, i ^ bit) for i in range(size)])  23.8 us
  transfers between devices with their start and end apart: 30, of which 15 were waited for; matrix products, arithmetic and copies ran while one was open for 9% of the time, Pallas kernels for 12%

profile of v5, /device:TPU:0, one launch (start us, length us, event | category | flops | bytes accessed | tf_op | source)
XLA Modules:
  0.0 638.3 jit_solution(10934659068483860668)
XLA Ops:
  8.0 3.1 collective-permute-start.5
  11.1 1.6 convert_element_type.52
  12.8 122.2 %all-gather.7.cloned.1.call-done.refs_0_.refs_1_.refs_2_.refs_3_ = bf16[768,8192]{1,0:T(8,128)(2,1)} async-done(((bf16[768,2048]{1,0:T(8,128)(2,1)}), bf16[768,8192]{1,0:T(8,128)(2,1)}) %all-gather.7.cloned.1.call-update) | async-done | bytes 12582928 | tf_op jit(solution)/shard_map/all_gather | solution.py:226
  135.0 1.5 dynamic_slice.19
  136.5 3.4 collective-permute-start.10
  139.9 38.3 %collective-permute-done.5.refs_6_ = bf16[3584,1024]{1,0:T(8,128)(2,1)} collective-permute-done((bf16[3584,1024]{1,0:T(8,128)(2,1)}, bf16[3584,1024]{1,0:T(8,128)(2,1)}, u32[]{:S(2)}, u32[]{:S(2)}) %collective-permute-start.5) | collective-permute-done | bytes 7340064 | tf_op jit(solution)/shard_map/ppermute | solution.py:197
  178.2 35.6 %collective-permute-done.10 = bf16[192,4096]{1,0:T(8,128)(2,1)} collective-permute-done((bf16[192,4096]{1,0:T(8,128)(2,1)S(1)}, bf16[192,4096]{1,0:T(8,128)(2,1)}, u32[]{:S(2)}, u32[]{:S(2)}) %collective-permute-start.10) | collective-permute-done | bytes 1572896 | tf_op jit(solution)/shard_map/ppermute | solution.py:214
  213.9 8.8 %fusion.6 = f32[768,64]{0,1:T(8,128)} fusion(bf16[768,3584]{1,0:T(8,128)(2,1)} %param.14, bf16[768,3584]{1,0:T(8,128)(2,1)} %refs_8_.1, bf16[3584,128]{1,0:T(8,128)(2,1)} %refs_9_.1), kind=kOutput, calls=%fused_computation.9 | convolution fusion | flops 374341632 | bytes 12124160 | tf_op jit(solution)/shard_map/dot_general | solution.py:249
  222.7 6.6 %fusion.55 = f32[1024,256]{1,0:T(8,128)S(1)} fusion(f32[1024,2048]{1,0:T(8,128)} %param.20, bf16[2048,256]{0,1:T(8,128)(2,1)} %all-gather.5.cloned.1.call-done), kind=kOutput, calls=%fused_computation.82 | convolution fusion | flops 3221225472 | bytes 10485760 | tf_op jit(solution)/shard_map/dot_general | solution.py:258
  230.2 1.6 collective-permute-start
  235.4 2.5 collective-permute-start.9
  237.9 29.1 %collective-permute-done = f32[512,256]{1,0:T(8,128)} collective-permute-done((f32[512,256]{1,0:T(8,128)}, f32[512,256]{1,0:T(8,128)}, u32[]{:S(2)}, u32[]{:S(2)}) %collective-permute-start) | collective-permute-done | bytes 524320 | tf_op jit(solution)/shard_map/ppermute | solution.py:197
  268.3 1.5 collective-permute-start.1
  270.5 10.5 %collective-permute-done.1 = f32[256,256]{1,0:T(8,128)S(1)} collective-permute-done((f32[256,256]{1,0:T(8,128)S(1)}, f32[256,256]{1,0:T(8,128)S(1)}, u32[]{:S(2)}, u32[]{:S(2)}) %collective-permute-start.1) | collective-permute-done | bytes 262176 | tf_op jit(solution)/shard_map/ppermute | solution.py:197
  281.0 2.5 collective-permute-start.7
  285.5 1.5 collective-permute-start.2
  287.5 2.2 slice.62
  289.8 2.7 slice.63
  292.5 2.4 slice.66
  294.9 24.9 %collective-permute-done.2 = f32[256,256]{1,0:T(8,128)} collective-permute-done((f32[256,256]{1,0:T(8,128)}, f32[256,256]{1,0:T(8,128)}, u32[]{:S(2)}, u32[]{:S(2)}) %collective-permute-start.2) | collective-permute-done | bytes 262176 | tf_op jit(solution)/shard_map/ppermute | solution.py:197
  319.8 3.1 collective-permute-start.13
  324.4 1.4 add_add_fusion
  326.7 3.2 collective-permute-start.15
  329.9 3.6 collective-permute-done.3
  333.5 5.6 fusion.14.other
  339.1 5.9 collective-permute-start.14
  345.1 34.7 %shard_map.130 = f32[768,128]{1,0:T(8,128)} custom-call(s32[4]{0:T(128)} %get-tuple-element.15.idx, bf16[768,8192]{1,0:T(8,128)(2,1)} %all-gather.7.cloned.1.call-done.refs_0_.refs_1_.refs_2_.refs_3_, bf16[768,8192]{1,0:T(8,128)(2,1)} %all-gather.7.cloned.1.call-done.refs_0_.refs_1_.refs_2_.refs_3_, ...), custom_call_target="tpu_custom_call" | custom-call | flops 23957864448 | bytes 46661632 | tf_op jit(solution)/shard_map/pallas_call | solution.py:63
  380.9 1.9 collective-permute-start.11
  382.9 5.9 collective-permute-start.12
  388.8 31.4 %shard_map.131 = f32[768,3584]{1,0:T(8,128)} custom-call(s32[4]{0:T(128)} %get-tuple-element.29.idx, bf16[768,4096]{1,0:T(8,128)(2,1)} %all-gather.9.cloned.1.call-done.refs_0_.refs_1_.refs_2_.refs_3_, bf16[768,4096]{1,0:T(8,128)(2,1)} %all-gather.9.cloned.1.call-done.refs_0_.refs_1_.refs_2_.refs_3_, ...), custom_call_target="tpu_custom_call" | custom-call | flops 22548578304 | bytes 46661632 | tf_op jit(solution)/shard_map/pallas_call | solution.py:104
  420.2 6.1 fusion.9
  426.3 33.0 %collective-permute-done.12 = bf16[768,1024]{1,0:T(8,128)(2,1)} collective-permute-done((bf16[768,1024]{1,0:T(8,128)(2,1)}, bf16[768,1024]{1,0:T(8,128)(2,1)}, u32[]{:S(2)}, u32[]{:S(2)}) %collective-permute-start.12) | collective-permute-done | bytes 1572896 | tf_op jit(solution)/shard_map/ppermute | solution.py:214
  459.4 4.1 fusion.12
  463.5 2.6 convolution_add_fusion
  467.4 3.6 collective-permute-start.16
  471.9 1.7 collective-permute-done.16
  474.3 2.3 collective-permute-start.19
  478.0 1.5 collective-permute-done.19
  479.5 1.4 collective-permute-done.17
  480.9 120.8 %all-gather = f32[8,6,4096]{2,1,0:T(8,128)S(1)} all-gather(f32[1,6,4096]{2,1,0:T(8,128)S(1)} %maximum_bitcast_fusion), channel_id=1, replica_groups=mesh['fsdp'=8,'solve'=4] {'fsdp'}, dimensions={0}, use_global_device_ids=true | all-gather | bytes 884736 | tf_op jit(solution)/shard_map/all_gather | solution.py:320
  602.7 4.4 shard_map.132
  607.2 1.7 collective-permute-start.22
  609.3 1.9 collective-permute-done.21
  611.9 1.4 collective-permute-start.23
  613.4 3.5 collective-permute-done.23
  617.0 2.1 collective-permute-start.26
  620.4 5.3 shard_map.133.refs_0_
  625.7 5.4 shard_map.134
  (93 shorter events, 21.8 us)
Async XLA Ops:
  7.2 225.7 %copy-start = (bf16[768,2048]{1,0:T(8,128)(2,1)S(1)}, bf16[768,2048]{1,0:T(8,128)(2,1)}, u32[]{:S(2)}) copy-start(bf16[768,2048]{1,0:T(8,128)(2,1)} %param.11) | copy-start | bytes 9437188
  7.2 127.8 %all-gather.7.cloned.1.call-start = ((), (), s32[]{:S(2)}) async-start(), calls=%async_computation.1 | async-start | bytes 15728640 | tf_op jit(solution)/shard_map/all_gather | solution.py:226
  7.9 214.8 %all-gather.5.cloned.1.call-start = ((), (), s32[]{:S(2)}) async-start(), calls=%async_computation | async-start | bytes 1179648 | tf_op jit(solution)/shard_map/all_gather | solution.py:257
  8.0 170.2 %collective-permute-start.5 = (bf16[3584,1024]{1,0:T(8,128)(2,1)}, bf16[3584,1024]{1,0:T(8,128)(2,1)}, u32[]{:S(2)}, u32[]{:S(2)}) collective-permute-start(bf16[3584,1024]{1,0:T(8,128)(2,1)} %refs_4_.3), channel_id=1, source_target_pairs={{0,8},{4,12},{8,0},{12,4},{16,24},{20,28},{24,16},{28,20},{1,9},{5... | collective-permute-start | bytes 22020104 | tf_op jit(solution)/shard_map/ppermute | solution.py:197
  12.7 376.1 %all-gather.9.cloned.1.call-start = ((), (), s32[]{:S(2)}) async-start(), calls=%async_computation.2 | async-start | bytes 7864320 | tf_op jit(solution)/shard_map/all_gather | solution.py:231
  136.5 77.3 %collective-permute-start.10 = (bf16[192,4096]{1,0:T(8,128)(2,1)S(1)}, bf16[192,4096]{1,0:T(8,128)(2,1)}, u32[]{:S(2)}, u32[]{:S(2)}) collective-permute-start(bf16[192,4096]{1,0:T(8,128)(2,1)S(1)} %dynamic_slice.19), channel_id=1, source_target_pairs={{0,24},{4,28},{8,16},{12,20},{16,8},{20,12},{24,0},{28,4},{1,25},{... | collective-permute-start | bytes 4718600 | tf_op jit(solution)/shard_map/ppermute | solution.py:214
  139.9 205.2 %collective-permute-start.4 = (bf16[3584,1024]{1,0:T(8,128)(2,1)}, bf16[3584,1024]{1,0:T(8,128)(2,1)}, u32[]{:S(2)}, u32[]{:S(2)}) collective-permute-start(bf16[3584,1024]{1,0:T(8,128)(2,1)} %refs_4_.3), channel_id=1, source_target_pairs={{0,4},{4,0},{8,12},{12,8},{16,20},{20,16},{24,28},{28,24},{1,5},{5... | collective-permute-start | bytes 22020104 | tf_op jit(solution)/shard_map/ppermute | solution.py:197
  178.2 166.9 %collective-permute-start.6 = (bf16[3584,1024]{1,0:T(8,128)(2,1)}, bf16[3584,1024]{1,0:T(8,128)(2,1)}, u32[]{:S(2)}, u32[]{:S(2)}) collective-permute-start(bf16[3584,1024]{1,0:T(8,128)(2,1)} %collective-permute-done.5.refs_6_), channel_id=1, source_target_pairs={{0,4},{4,0},{8,12},{12,8},{16,20},{20,16},{24,28},{28,24},{1,5},{5... | collective-permute-start | bytes 22020104 | tf_op jit(solution)/shard_map/ppermute | solution.py:197
  222.7 9.1 %copy-start.2 = (bf16[768,2048]{1,0:T(8,128)(2,1)S(1)}, bf16[768,2048]{1,0:T(8,128)(2,1)}, u32[]{:S(2)}) copy-start(bf16[768,2048]{1,0:T(8,128)(2,1)} %param.12) | copy-start | bytes 9437188
  222.7 9.1 %copy-start.4 = (bf16[2048,128]{1,0:T(8,128)(2,1)S(1)}, bf16[2048,128]{1,0:T(8,128)(2,1)}, u32[]{:S(2)}) copy-start(bf16[2048,128]{1,0:T(8,128)(2,1)} %param.16) | copy-start | bytes 1572868
  229.3 3.5 copy-start.3
  229.4 4.7 copy-start.5
  230.2 40.2 %copy-start.12 = (s32[3]{0:T(128)S(1)}, s32[3]{0:T(128)}, u32[]{:S(2)}) copy-start(s32[3]{0:T(128)} %param.18) | copy-start | bytes 40
  230.2 36.7 %collective-permute-start = (f32[512,256]{1,0:T(8,128)}, f32[512,256]{1,0:T(8,128)}, u32[]{:S(2)}, u32[]{:S(2)}) collective-permute-start(f32[512,256]{1,0:T(8,128)} %constant_dynamic-slice_fusion.1), channel_id=1, source_target_pairs={{0,2},{1,3},{2,0},{3,1},{4,6},{5,7},{6,4},{7,5},{8,10},{9,11},{10,... | collective-permute-start | bytes 1572872 | tf_op jit(solution)/shard_map/ppermute | solution.py:197
  234.9 50.5 %collective-permute-start.8 = (f32[768,192]{0,1:T(8,128)}, f32[768,192]{0,1:T(8,128)S(1)}, u32[]{:S(2)}, u32[]{:S(2)}) collective-permute-start(f32[768,192]{0,1:T(8,128)} %pad_maximum_fusion), channel_id=1, source_target_pairs={{0,2},{1,3},{2,0},{3,1},{4,6},{5,7},{6,4},{7,5},{8,10},{9,11},{10,... | collective-permute-start | bytes 1769480 | tf_op jit(solution)/shard_map/ppermute | solution.py:197
  235.4 88.9 %collective-permute-start.9 = (f32[768,192]{0,1:T(8,128)}, f32[768,192]{0,1:T(8,128)}, u32[]{:S(2)}, u32[]{:S(2)}) collective-permute-start(f32[768,192]{0,1:T(8,128)} %pad_maximum_fusion), channel_id=1, source_target_pairs={{0,3},{1,2},{2,1},{3,0},{4,7},{5,6},{6,5},{7,4},{8,11},{9,10},{10,... | collective-permute-start | bytes 1769480 | tf_op jit(solution)/shard_map/ppermute | solution.py:197
  268.3 12.8 %collective-permute-start.1 = (f32[256,256]{1,0:T(8,128)S(1)}, f32[256,256]{1,0:T(8,128)S(1)}, u32[]{:S(2)}, u32[]{:S(2)}) collective-permute-start(f32[256,256]{1,0:T(8,128)S(1)} %constant_dynamic-slice_fusion), channel_id=1, source_target_pairs={{0,1},{1,0},{2,3},{3,2},{4,5},{5,4},{6,7},{7,6},{8,9},{9,8},{10,11... | collective-permute-start | bytes 786440 | tf_op jit(solution)/shard_map/ppermute | solution.py:197
  281.0 43.4 %collective-permute-start.7 = (f32[768,192]{0,1:T(8,128)}, f32[768,192]{0,1:T(8,128)}, u32[]{:S(2)}, u32[]{:S(2)}) collective-permute-start(f32[768,192]{0,1:T(8,128)} %pad_maximum_fusion), channel_id=1, source_target_pairs={{0,1},{1,0},{2,3},{3,2},{4,5},{5,4},{6,7},{7,6},{8,9},{9,8},{10,11... | collective-permute-start | bytes 1769480 | tf_op jit(solution)/shard_map/ppermute | solution.py:197
  285.5 4.3 copy-start.10
  285.5 34.4 %collective-permute-start.2 = (f32[256,256]{1,0:T(8,128)}, f32[256,256]{1,0:T(8,128)}, u32[]{:S(2)}, u32[]{:S(2)}) collective-permute-start(f32[256,256]{1,0:T(8,128)} %dynamic-slice_add_fusion.1), channel_id=1, source_target_pairs={{0,1},{1,0},{2,3},{3,2},{4,5},{5,4},{6,7},{7,6},{8,9},{9,8},{10,11... | collective-permute-start | bytes 786440 | tf_op jit(solution)/shard_map/ppermute | solution.py:197
  287.5 46.0 %slice-start = ((s8[8388608]{0:T(1024)(128)(4,1)}), s8[4194304]{0:T(1024)(128)(4,1)S(1)}, s32[]{:S(2)}) async-start(s8[8388608]{0:T(1024)(128)(4,1)} %bitcast.35), calls=%async_computation.3 | async-start | bytes 8388608
  289.8 34.6 %copy-start.6 = (f32[768,64]{0,1:T(8,128)S(1)}, f32[768,64]{0,1:T(8,128)}, u32[]{:S(2)}) copy-start(f32[768,64]{0,1:T(8,128)} %fusion.6) | copy-start | bytes 589828
  292.5 31.9 %copy-start.11 = (f32[768,192]{0,1:T(8,128)S(1)}, f32[768,192]{0,1:T(8,128)}, u32[]{:S(2)}) copy-start(f32[768,192]{0,1:T(8,128)} %copy-done.10) | copy-start | bytes 1769476
  292.5 41.1 %slice-start.1 = ((s8[8388608]{0:T(1024)(128)(4,1)}), s8[4194304]{0:T(1024)(128)(4,1)S(1)}, s32[]{:S(2)}) async-start(s8[8388608]{0:T(1024)(128)(4,1)} %bitcast.35), calls=%async_computation.4 | async-start | bytes 8388608
  319.8 100.4 %collective-permute-start.13 = (bf16[768,3584]{1,0:T(8,128)(2,1)}, bf16[768,3584]{1,0:T(8,128)(2,1)}, u32[]{:S(2)}, u32[]{:S(2)}) collective-permute-start(bf16[768,3584]{1,0:T(8,128)(2,1)} %refs_8_.1), channel_id=1, source_target_pairs={{8,16},{12,20},{16,8},{20,12},{9,17},{13,21},{17,9},{21,13},{10,18... | collective-permute-start | bytes 16515080 | tf_op jit(solution)/shard_map/ppermute | solution.py:214
  324.3 9.2 %collective-permute-start.3 = (f32[512,256]{1,0:T(8,128)S(1)}, f32[512,256]{1,0:T(8,128)S(1)}, u32[]{:S(2)}, u32[]{:S(2)}) collective-permute-start(f32[512,256]{1,0:T(8,128)S(1)} %maximum_select_fusion.2), channel_id=1, source_target_pairs={{0,2},{1,3},{2,0},{3,1},{4,6},{5,7},{6,4},{7,5},{8,10},{9,11},{10,... | collective-permute-start | bytes 1572872 | tf_op jit(solution)/shard_map/ppermute | solution.py:197
  326.7 139.5 %collective-permute-start.15 = (bf16[768,64]{0,1:T(8,128)(2,1)}, bf16[768,64]{0,1:T(8,128)(2,1)}, u32[]{:S(2)}, u32[]{:S(2)}) collective-permute-start(bf16[768,64]{0,1:T(8,128)(2,1)} %get-tuple-element.27), channel_id=1, source_target_pairs={{0,24},{4,28},{8,16},{12,20},{16,8},{20,12},{24,0},{28,4},{1,25},{... | collective-permute-start | bytes 294920 | tf_op jit(solution)/shard_map/ppermute | solution.py:214
  339.1 81.1 %collective-permute-start.14 = (bf16[768,2048]{1,0:T(8,128)(2,1)S(1)}, bf16[768,2048]{1,0:T(8,128)(2,1)}, u32[]{:S(2)}, u32[]{:S(2)}) collective-permute-start(bf16[768,2048]{1,0:T(8,128)(2,1)S(1)} %slice.66), channel_id=1, source_target_pairs={{0,24},{4,28},{24,0},{28,4},{1,25},{5,29},{25,1},{29,5},{2,26},{6,... | collective-permute-start | bytes 9437192 | tf_op jit(solution)/shard_map/ppermute | solution.py:214
  380.9 82.6 %collective-permute-start.11 = (bf16[768,512]{1,0:T(8,128)(2,1)}, bf16[768,512]{1,0:T(8,128)(2,1)}, u32[]{:S(2)}, u32[]{:S(2)}) collective-permute-start(bf16[768,512]{1,0:T(8,128)(2,1)} %slice.62), channel_id=1, source_target_pairs={{0,24},{4,28},{24,0},{28,4},{1,25},{5,29},{25,1},{29,5},{2,26},{6,... | collective-permute-start | bytes 2359304 | tf_op jit(solution)/shard_map/ppermute | solution.py:214
  382.9 76.5 %collective-permute-start.12 = (bf16[768,1024]{1,0:T(8,128)(2,1)}, bf16[768,1024]{1,0:T(8,128)(2,1)}, u32[]{:S(2)}, u32[]{:S(2)}) collective-permute-start(bf16[768,1024]{1,0:T(8,128)(2,1)} %slice.63), channel_id=1, source_target_pairs={{0,24},{4,28},{24,0},{28,4},{1,25},{5,29},{25,1},{29,5},{2,26},{6,... | collective-permute-start | bytes 4718600 | tf_op jit(solution)/shard_map/ppermute | solution.py:214
  463.5 7.6 %copy-start.9 = (f32[768,64]{0,1:T(8,128)S(1)}, f32[768,64]{0,1:T(8,128)}, u32[]{:S(2)}) copy-start(f32[768,64]{0,1:T(8,128)} %get-tuple-element.28) | copy-start | bytes 589828
  463.5 13.7 %copy-start.7 = (f32[768,64]{0,1:T(8,128)S(1)}, f32[768,64]{0,1:T(8,128)}, u32[]{:S(2)}) copy-start(f32[768,64]{0,1:T(8,128)} %get-tuple-element.31) | copy-start | bytes 589828
  463.5 13.7 %copy-start.8 = (f32[768,64]{0,1:T(8,128)S(1)}, f32[768,64]{0,1:T(8,128)}, u32[]{:S(2)}) copy-start(f32[768,64]{0,1:T(8,128)} %get-tuple-element.32) | copy-start | bytes 589828
  467.4 6.2 collective-permute-start.16
  473.7 4.3 collective-permute-start.18
  474.3 5.2 collective-permute-start.19
  476.6 4.3 collective-permute-start.17
  607.2 4.0 collective-permute-start.21
  607.2 4.0 collective-permute-start.22
  608.9 2.3 collective-permute-start.20
  611.9 5.0 collective-permute-start.23
  616.9 14.2 %collective-permute-start.25 = (f32[24,256]{1,0:T(8,128)S(1)}, f32[24,256]{1,0:T(8,128)S(1)}, u32[]{:S(2)}, u32[]{:S(2)}) collective-permute-start(f32[24,256]{1,0:T(8,128)S(1)} %add.152), channel_id=1, source_target_pairs={{0,2},{1,3},{2,0},{3,1},{4,6},{5,7},{6,4},{7,5},{8,10},{9,11},{10,... | collective-permute-start | bytes 73736 | tf_op jit(solution)/shard_map/ppermute | solution.py:197
  617.0 14.2 %collective-permute-start.26 = (f32[24,256]{1,0:T(8,128)S(1)}, f32[24,256]{1,0:T(8,128)S(1)}, u32[]{:S(2)}, u32[]{:S(2)}) collective-permute-start(f32[24,256]{1,0:T(8,128)S(1)} %add.152), channel_id=1, source_target_pairs={{0,3},{1,2},{2,1},{3,0},{4,7},{5,6},{6,5},{7,4},{8,11},{9,10},{10,... | collective-permute-start | bytes 73736 | tf_op jit(solution)/shard_map/ppermute | solution.py:197
  619.1 12.1 %collective-permute-start.24 = (f32[24,256]{1,0:T(8,128)S(1)}, f32[24,256]{1,0:T(8,128)S(1)}, u32[]{:S(2)}, u32[]{:S(2)}) collective-permute-start(f32[24,256]{1,0:T(8,128)S(1)} %add.152), channel_id=1, source_target_pairs={{0,1},{1,0},{2,3},{3,2},{4,5},{5,4},{6,7},{7,6},{8,9},{9,8},{10,11... | collective-permute-start | bytes 73736 | tf_op jit(solution)/shard_map/ppermute | solution.py:197
  625.7 6.1 copy-start.1
Sparse Core Ops, SparseCore 0:
  9.8 125.0 all-gather.6
  137.1 27.8 all-gather.4
  213.9 113.8 all-gather.8

commit v6 on v5

--- a/solution.py
+++ b/solution.py
@@ -1,4 +1,5 @@
 import functools
+import math
 
 import jax
 import jax.numpy as jnp
@@ -119,44 +120,28 @@
     )(idx, *([cot] * count), *weights)
 
 
-def features_kernel(examples, seqs, count, idx, both, other, left_out, right_out, scores):
+def split(x):
+    high = x.astype(jnp.bfloat16)
+    return high, (x - high.astype(jnp.float32)).astype(jnp.bfloat16)
+
+
+def features_kernel(scale, idx, both, pick_left, pick_right, high_side, low_side, left_out, right_out, scores):
     f32 = jnp.float32
-    shape = (examples, both.shape[0])
-    pick = lax.broadcasted_iota(jnp.int32, shape, 1)
-    row = lax.broadcasted_iota(jnp.int32, shape, 0)
-    up = jnp.zeros(shape, f32)
-    down = jnp.zeros(shape, f32)
-    for i in range(examples // seqs):
-        for e in range(seqs):
-            here = row == seqs * i + e
-            up = jnp.where((pick == 2 * seqs * i + e) & here, 1.0, up)
-            down = jnp.where((pick == 2 * seqs * i + seqs + e) & here, 1.0, down)
-
-    def split(x):
-        high = x.astype(jnp.bfloat16)
-        return high, (x - high.astype(f32)).astype(jnp.bfloat16)
-
-    def part(offset, width):
-        size = both.shape[1]
-        is_up = offset >= size
-        at = pl.multiple_of(offset - jnp.where(is_up, size, 0), 128)
+
+    def part(offset, width, pick):
+        at = pl.multiple_of(offset, 128)
         high, low = split(both[:, pl.ds(at, width)])
-        sel = jnp.where(is_up, up, down).astype(jnp.bfloat16)
-        return jnp.dot(sel, high, preferred_element_type=f32) + jnp.dot(sel, low, preferred_element_type=f32)
-
-    high, low = split(part(idx[0], left_out.shape[1]))
+        return jnp.dot(pick, high, preferred_element_type=f32) + jnp.dot(pick, low, preferred_element_type=f32)
+
+    def against(x, side):
+        return lax.dot_general(x, side, (((1,), (1,)), ((), ())), preferred_element_type=f32)
+
+    high, low = split(part(idx[0], left_out.shape[1], pick_left[...]))
     left_out[...] = jnp.concatenate([high, low, high], axis=0)
-    right = part(idx[1], right_out.shape[1])
-    high, low = split(right)
+    high, low = split(part(idx[1], right_out.shape[1], pick_right[...]))
     right_out[...] = jnp.concatenate([high, high, low], axis=0)
-    product = lax.dot_general(
-        right,
-        other[...],
-        (((1,), (1,)), ((), ())),
-        precision=lax.Precision.HIGHEST,
-        preferred_element_type=f32,
-    )
-    scores[...] = product / jnp.sqrt(f32(count))
+    product = against(high, high_side[...]) + (against(low, high_side[...]) + against(high, low_side[...]))
+    scores[...] = product * scale
 
 
 def gram_kernel(scale, gram, left, right, *refs):
@@ -196,8 +181,7 @@
     def swap(x, axis, size, bit):
         return lax.ppermute(x, axis, [(i, i ^ bit) for i in range(size)])
 
-    def total(x, axis, size):
-        bit = 1
+    def total(x, axis, size, bit=1):
         while bit < size:
             if 2 * bit < size:
                 one, two, both = (swap(x, axis, size, b) for b in (bit, 2 * bit, 3 * bit))
@@ -279,7 +263,8 @@
 
     own_idx = jnp.stack([f ^ k for k in order]).astype(jnp.int32)
     far_idx = own_idx - side * h
-    own_idx, query_side = lax.optimization_barrier((own_idx, query_side))
+    other_side = swap(query_side, "fsdp", n, 1)
+    own_idx, query_side, _ = lax.optimization_barrier((own_idx, query_side, quarter))
     own = tokens(
         own_idx, cot_full, [(v, 0) for v in weights], [(gate_pre, 0)], None, proj_hidden, 0, tiles
     )
@@ -315,6 +300,7 @@
         term = jnp.dot(grad_up, proj_hidden[units, half:], preferred_element_type=f32)
         far = term if far is None else far + term
     up_far = pair(far, in_up_far)
+    query_side = split(query_side + other_side)
     up = up_own + mirror(up_far)
     up = total(up, "solve", m)
     both = lax.all_gather(jnp.concatenate([up, down], axis=0), "fsdp", axis=0, tiled=True)
@@ -323,17 +309,29 @@
     row_width = gram.shape[0]
     col_width = gram.shape[1]
     count = queries.shape[1] * n
-    at = jnp.stack([f * row_width, s * col_width]).astype(jnp.int32)
+    size = half * half
+
+    def place(offset):
+        up_part = offset >= size
+        shape = (examples, 2 * examples)
+        row = lax.broadcasted_iota(jnp.int32, shape, 0)
+        column = lax.broadcasted_iota(jnp.int32, shape, 1)
+        wanted = row // local_seqs * 2 * local_seqs + row % local_seqs + jnp.where(up_part, 0, local_seqs)
+        return (column == wanted).astype(jnp.bfloat16), jnp.where(up_part, offset - size, offset)
+
+    pick_left, at_left = place(f * row_width)
+    pick_right, at_right = place(s * col_width)
+    at = jnp.stack([at_left, at_right]).astype(jnp.int32)
     left, right, scores = pl.pallas_call(
-        functools.partial(features_kernel, examples, local_seqs, 2 * half * half),
+        functools.partial(features_kernel, 1.0 / math.sqrt(2 * size)),
         out_shape=(
             jax.ShapeDtypeStruct((3 * examples, row_width), jnp.bfloat16),
             jax.ShapeDtypeStruct((3 * examples, col_width), jnp.bfloat16),
             jax.ShapeDtypeStruct((examples, count), f32),
         ),
-        in_specs=[pl.BlockSpec(memory_space=pltpu.SMEM)] + [pl.BlockSpec(memory_space=pltpu.VMEM)] * 2,
-    )(at, both, query_side)
-    scores = total(scores, "fsdp", n)
+        in_specs=[pl.BlockSpec(memory_space=pltpu.SMEM)] + [pl.BlockSpec(memory_space=pltpu.VMEM)] * 5,
+    )(at, both, pick_left, pick_right, *query_side)
+    scores = total(scores, "fsdp", n, 2)
     scores = total(scores, "solve", m)
     block = 128
     steps = row_width // block

time: 639 us -> 621 us (0.972)
  blocking collectives: 121 us -> 110 us
    ppermute x20, waiting for transfers between devices: 116 us -> 106 us  [swap(): return lax.ppermute(x, axis, [(i, i ^ bit) for i in range(size)])]
    all_gather x1, blocking collectives: 121 us -> 110 us  [local(): lax.all_gather(jnp.concatenate([up, down], axis=0), 'fsdp', axis=0, tiled...]
    ppermute x7, waiting for transfers between devices: 70.4 us -> 77.6 us  [mirror(): return lax.ppermute(x, 'fsdp', pairs)]
    ppermute x7, starting transfers between devices: 27.1 us -> 20.6 us  [mirror(): return lax.ppermute(x, 'fsdp', pairs)]
  transfers between devices with their start and end apart: 30 -> 30, of which waited for: 15 -> 13; matrix products, arithmetic and copies ran while one was open for 9% -> 10% of each run, Pallas kernels for 12% -> 12%
where the time goes in v6:
time: 621 us; the launch traced here: 620 us
  waiting for transfers between devices  306 us (49%)
  blocking collectives  110 us (18%)
  Pallas kernels  80.3 us (13%)
  starting transfers between devices  45.2 us (7%)
  matrix products  39.1 us (6%)
  between operations  14.1 us (2%)
  local copies, waits for them, and re-layouts  13.7 us (2%)
  other arithmetic  11.3 us (2%)
    all_gather x1, waiting for transfers between devices, local(): cot_full = lax.all_gather(cotangent, 'solve', axis=1, tiled=True)  122 us
    all_gather x1, blocking collectives, local(): lax.all_gather(jnp.concatenate([up, down], axis=0), 'fsdp', axis=0, tiled...  110 us
    ppermute x20, waiting for transfers between devices, swap(): return lax.ppermute(x, axis, [(i, i ^ bit) for i in range(size)])  106 us
    ppermute x7, waiting for transfers between devices, mirror(): return lax.ppermute(x, 'fsdp', pairs)  77.6 us
    pallas_call x1, Pallas kernels, tokens(): pl.pallas_call(functools.partial(tokens_kernel, count, len(gate_parts), s...  34.7 us
    pallas_call x1, Pallas kernels, gradient(): pl.pallas_call(functools.partial(grad_kernel, count), out_shape=jax.Shape...  31.4 us
    ppermute x20, starting transfers between devices, swap(): return lax.ppermute(x, axis, [(i, i ^ bit) for i in range(size)])  24.5 us
    ppermute x7, starting transfers between devices, mirror(): return lax.ppermute(x, 'fsdp', pairs)  20.6 us
  transfers between devices with their start and end apart: 30, of which 13 were waited for; matrix products, arithmetic and copies ran while one was open for 10% of the time, Pallas kernels for 12%

profile of v6, /device:TPU:0, one launch (start us, length us, event | category | flops | bytes accessed | tf_op | source)
XLA Modules:
  0.0 620.4 jit_solution(12151470159022059672)
XLA Ops:
  8.0 3.1 collective-permute-start.6
  11.1 1.6 convert_element_type.67
  12.8 122.2 %all-gather.7.cloned.1.call-done.refs_0_.refs_1_.refs_2_.refs_3_ = bf16[768,8192]{1,0:T(8,128)(2,1)} async-done(((bf16[768,2048]{1,0:T(8,128)(2,1)}), bf16[768,8192]{1,0:T(8,128)(2,1)}) %all-gather.7.cloned.1.call-update) | async-done | bytes 12582928 | tf_op jit(solution)/shard_map/all_gather | solution.py:210
  135.0 1.5 dynamic_slice.19
  136.5 3.4 collective-permute-start.4
  139.9 38.3 %collective-permute-done.6.refs_6_ = bf16[3584,1024]{1,0:T(8,128)(2,1)} collective-permute-done((bf16[3584,1024]{1,0:T(8,128)(2,1)}, bf16[3584,1024]{1,0:T(8,128)(2,1)}, u32[]{:S(2)}, u32[]{:S(2)}) %collective-permute-start.6) | collective-permute-done | bytes 7340064 | tf_op jit(solution)/shard_map/ppermute | solution.py:182
  178.2 35.6 %collective-permute-done.4 = bf16[192,4096]{1,0:T(8,128)(2,1)} collective-permute-done((bf16[192,4096]{1,0:T(8,128)(2,1)S(1)}, bf16[192,4096]{1,0:T(8,128)(2,1)}, u32[]{:S(2)}, u32[]{:S(2)}) %collective-permute-start.4) | collective-permute-done | bytes 1572896 | tf_op jit(solution)/shard_map/ppermute | solution.py:198
  213.9 8.8 %fusion.6 = f32[768,64]{0,1:T(8,128)} fusion(bf16[768,3584]{1,0:T(8,128)(2,1)} %param.14, bf16[768,3584]{1,0:T(8,128)(2,1)} %refs_8_.1, bf16[3584,128]{1,0:T(8,128)(2,1)} %refs_9_.1), kind=kOutput, calls=%fused_computation.9 | convolution fusion | flops 374341632 | bytes 12124160 | tf_op jit(solution)/shard_map/dot_general | solution.py:233
  222.7 6.6 %fusion.57 = f32[1024,256]{1,0:T(8,128)S(1)} fusion(f32[1024,2048]{1,0:T(8,128)} %param.20, bf16[2048,256]{0,1:T(8,128)(2,1)} %all-gather.5.cloned.1.call-done), kind=kOutput, calls=%fused_computation.96 | convolution fusion | flops 3221225472 | bytes 10485760 | tf_op jit(solution)/shard_map/dot_general | solution.py:242
  230.2 1.6 collective-permute-start
  234.6 2.5 collective-permute-start.10
  237.2 29.8 %collective-permute-done = f32[512,256]{1,0:T(8,128)} collective-permute-done((f32[512,256]{1,0:T(8,128)}, f32[512,256]{1,0:T(8,128)}, u32[]{:S(2)}, u32[]{:S(2)}) %collective-permute-start) | collective-permute-done | bytes 524320 | tf_op jit(solution)/shard_map/ppermute | solution.py:182
  266.9 1.3 dynamic-slice_add_fusion
  268.2 1.5 collective-permute-start.1
  269.8 11.2 %collective-permute-done.1 = f32[256,256]{1,0:T(8,128)S(1)} collective-permute-done((f32[256,256]{1,0:T(8,128)S(1)}, f32[256,256]{1,0:T(8,128)S(1)}, u32[]{:S(2)}, u32[]{:S(2)}) %collective-permute-start.1) | collective-permute-done | bytes 262176 | tf_op jit(solution)/shard_map/ppermute | solution.py:182
  281.1 2.5 collective-permute-start.2
  284.3 11.1 %collective-permute-done.2 = f32[256,256]{1,0:T(8,128)S(1)} collective-permute-done((f32[256,256]{1,0:T(8,128)S(1)}, f32[256,256]{1,0:T(8,128)S(1)}, u32[]{:S(2)}, u32[]{:S(2)}) %collective-permute-start.2) | collective-permute-done | bytes 262176 | tf_op jit(solution)/shard_map/ppermute | solution.py:182
  295.4 2.1 collective-permute-start.8
  298.1 2.1 slice.62
  300.2 2.7 slice.63
  302.9 4.0 slice.66
  307.6 3.1 collective-permute-start.13
  310.7 11.5 %collective-permute-done.8 = f32[768,192]{0,1:T(8,128)} collective-permute-done((f32[768,192]{0,1:T(8,128)S(1)}, f32[768,192]{0,1:T(8,128)}, u32[]{:S(2)}, u32[]{:S(2)}) %collective-permute-start.8) | collective-permute-done | bytes 589856 | tf_op jit(solution)/shard_map/ppermute | solution.py:182
  322.2 1.4 add_add_fusion
  324.1 3.3 collective-permute-start.15
  327.3 7.5 %fusion.14 = f32[256,2048]{1,0:T(8,128)S(1)} fusion(f32[1024,2048]{1,0:T(8,128)} %param.20, f32[512,256]{1,0:T(8,128)} %collective-permute-done.3, f32[512,256]{1,0:T(8,128)S(1)} %maximum_select_fusion.2, pred[]{:T(512)S(6)} %eq.35), kind=kOutput, calls=%fused_computation.19 | convolution fusion | flops 3222011904 | bytes 11534337 | tf_op jit(solution)/shard_map/dot_general | solution.py:262
  334.9 2.5 collective-permute-start.14
  337.5 34.7 %shard_map.130 = f32[768,128]{1,0:T(8,128)} custom-call(s32[4]{0:T(128)} %get-tuple-element.15.idx, bf16[768,8192]{1,0:T(8,128)(2,1)} %all-gather.7.cloned.1.call-done.refs_0_.refs_1_.refs_2_.refs_3_, bf16[768,8192]{1,0:T(8,128)(2,1)} %all-gather.7.cloned.1.call-done.refs_0_.refs_1_.refs_2_.refs_3_, ...), custom_call_target="tpu_custom_call" | custom-call | flops 23957864448 | bytes 46661632 | tf_op jit(solution)/shard_map/pallas_call | solution.py:64
  373.3 5.1 collective-permute-start.12
  378.5 31.4 %shard_map.131 = f32[768,3584]{1,0:T(8,128)} custom-call(s32[4]{0:T(128)} %get-tuple-element.29.idx, bf16[768,4096]{1,0:T(8,128)(2,1)} %all-gather.9.cloned.1.call-done.refs_0_.refs_1_.refs_2_.refs_3_, bf16[768,4096]{1,0:T(8,128)(2,1)} %all-gather.9.cloned.1.call-done.refs_0_.refs_1_.refs_2_.refs_3_, ...), custom_call_target="tpu_custom_call" | custom-call | flops 22548578304 | bytes 46661632 | tf_op jit(solution)/shard_map/pallas_call | solution.py:105
  409.9 2.5 collective-permute-start.11
  412.4 6.1 fusion.9
  418.5 25.2 %collective-permute-done.12 = bf16[768,1024]{1,0:T(8,128)(2,1)} collective-permute-done((bf16[768,1024]{1,0:T(8,128)(2,1)}, bf16[768,1024]{1,0:T(8,128)(2,1)}, u32[]{:S(2)}, u32[]{:S(2)}) %collective-permute-start.12) | collective-permute-done | bytes 1572896 | tf_op jit(solution)/shard_map/ppermute | solution.py:198
  443.7 4.1 fusion.12
  447.8 12.1 %collective-permute-done.11 = bf16[768,512]{1,0:T(8,128)(2,1)S(1)} collective-permute-done((bf16[768,512]{1,0:T(8,128)(2,1)}, bf16[768,512]{1,0:T(8,128)(2,1)S(1)}, u32[]{:S(2)}, u32[]{:S(2)}) %collective-permute-start.11) | collective-permute-done | bytes 786464 | tf_op jit(solution)/shard_map/ppermute | solution.py:198
  460.0 2.4 convolution_add_fusion
  464.3 4.6 collective-permute-done.16
  469.0 3.4 collective-permute-start.19
  472.5 3.4 subtract_convert_fusion
  476.8 110.3 %all-gather = f32[8,6,4096]{2,1,0:T(8,128)S(1)} all-gather(f32[1,6,4096]{2,1,0:T(8,128)S(1)} %maximum_bitcast_fusion), channel_id=1, replica_groups=mesh['fsdp'=8,'solve'=4] {'fsdp'}, dimensions={0}, use_global_device_ids=true | all-gather | bytes 884736 | tf_op jit(solution)/shard_map/all_gather | solution.py:306
  588.1 3.5 shard_map.132
  592.4 1.5 collective-permute-start.23
  593.9 1.2 collective-permute-start.21
  595.1 1.6 collective-permute-done.22
  596.8 1.5 collective-permute-done.23
  599.3 2.0 collective-permute-start.26
  602.5 5.3 shard_map.133.refs_0_
  607.8 5.4 shard_map.134
  (84 shorter events, 15.9 us)
Async XLA Ops:
  7.2 225.7 %copy-start = (bf16[768,2048]{1,0:T(8,128)(2,1)S(1)}, bf16[768,2048]{1,0:T(8,128)(2,1)}, u32[]{:S(2)}) copy-start(bf16[768,2048]{1,0:T(8,128)(2,1)} %param.11) | copy-start | bytes 9437188
  7.2 127.8 %all-gather.7.cloned.1.call-start = ((), (), s32[]{:S(2)}) async-start(), calls=%async_computation.1 | async-start | bytes 15728640 | tf_op jit(solution)/shard_map/all_gather | solution.py:210
  7.9 214.8 %all-gather.5.cloned.1.call-start = ((), (), s32[]{:S(2)}) async-start(), calls=%async_computation | async-start | bytes 1179648 | tf_op jit(solution)/shard_map/all_gather | solution.py:241
  8.0 170.2 %collective-permute-start.6 = (bf16[3584,1024]{1,0:T(8,128)(2,1)}, bf16[3584,1024]{1,0:T(8,128)(2,1)}, u32[]{:S(2)}, u32[]{:S(2)}) collective-permute-start(bf16[3584,1024]{1,0:T(8,128)(2,1)} %refs_4_.3), channel_id=1, source_target_pairs={{0,8},{4,12},{8,0},{12,4},{16,24},{20,28},{24,16},{28,20},{1,9},{5... | collective-permute-start | bytes 22020104 | tf_op jit(solution)/shard_map/ppermute | solution.py:182
  12.7 365.8 %all-gather.9.cloned.1.call-start = ((), (), s32[]{:S(2)}) async-start(), calls=%async_computation.2 | async-start | bytes 7864320 | tf_op jit(solution)/shard_map/all_gather | solution.py:215
  136.5 77.3 %collective-permute-start.4 = (bf16[192,4096]{1,0:T(8,128)(2,1)S(1)}, bf16[192,4096]{1,0:T(8,128)(2,1)}, u32[]{:S(2)}, u32[]{:S(2)}) collective-permute-start(bf16[192,4096]{1,0:T(8,128)(2,1)S(1)} %dynamic_slice.19), channel_id=1, source_target_pairs={{0,24},{4,28},{8,16},{12,20},{16,8},{20,12},{24,0},{28,4},{1,25},{... | collective-permute-start | bytes 4718600 | tf_op jit(solution)/shard_map/ppermute | solution.py:198
  139.9 195.0 %collective-permute-start.5 = (bf16[3584,1024]{1,0:T(8,128)(2,1)}, bf16[3584,1024]{1,0:T(8,128)(2,1)}, u32[]{:S(2)}, u32[]{:S(2)}) collective-permute-start(bf16[3584,1024]{1,0:T(8,128)(2,1)} %refs_4_.3), channel_id=1, source_target_pairs={{0,4},{4,0},{8,12},{12,8},{16,20},{20,16},{24,28},{28,24},{1,5},{5... | collective-permute-start | bytes 22020104 | tf_op jit(solution)/shard_map/ppermute | solution.py:182
  178.2 159.3 %collective-permute-start.7 = (bf16[3584,1024]{1,0:T(8,128)(2,1)}, bf16[3584,1024]{1,0:T(8,128)(2,1)}, u32[]{:S(2)}, u32[]{:S(2)}) collective-permute-start(bf16[3584,1024]{1,0:T(8,128)(2,1)} %collective-permute-done.6.refs_6_), channel_id=1, source_target_pairs={{0,4},{4,0},{8,12},{12,8},{16,20},{20,16},{24,28},{28,24},{1,5},{5... | collective-permute-start | bytes 22020104 | tf_op jit(solution)/shard_map/ppermute | solution.py:182
  222.7 9.1 %copy-start.2 = (bf16[768,2048]{1,0:T(8,128)(2,1)S(1)}, bf16[768,2048]{1,0:T(8,128)(2,1)}, u32[]{:S(2)}) copy-start(bf16[768,2048]{1,0:T(8,128)(2,1)} %param.12) | copy-start | bytes 9437188
  222.7 9.1 %copy-start.4 = (bf16[2048,128]{1,0:T(8,128)(2,1)S(1)}, bf16[2048,128]{1,0:T(8,128)(2,1)}, u32[]{:S(2)}) copy-start(bf16[2048,128]{1,0:T(8,128)(2,1)} %param.16) | copy-start | bytes 1572868
  229.3 3.6 copy-start.3
  229.4 4.7 copy-start.6
  230.2 54.0 %copy-start.8 = (s32[3]{0:T(128)S(1)}, s32[3]{0:T(128)}, u32[]{:S(2)}) copy-start(s32[3]{0:T(128)} %param.18) | copy-start | bytes 40
  230.2 36.7 %collective-permute-start = (f32[512,256]{1,0:T(8,128)}, f32[512,256]{1,0:T(8,128)}, u32[]{:S(2)}, u32[]{:S(2)}) collective-permute-start(f32[512,256]{1,0:T(8,128)} %constant_dynamic-slice_fusion.1), channel_id=1, source_target_pairs={{0,2},{1,3},{2,0},{3,1},{4,6},{5,7},{6,4},{7,5},{8,10},{9,11},{10,... | collective-permute-start | bytes 1572872 | tf_op jit(solution)/shard_map/ppermute | solution.py:182
  234.1 73.5 %collective-permute-start.9 = (f32[768,192]{0,1:T(8,128)S(1)}, f32[768,192]{0,1:T(8,128)S(1)}, u32[]{:S(2)}, u32[]{:S(2)}) collective-permute-start(f32[768,192]{0,1:T(8,128)S(1)} %pad_maximum_fusion), channel_id=1, source_target_pairs={{0,2},{1,3},{2,0},{3,1},{4,6},{5,7},{6,4},{7,5},{8,10},{9,11},{10,... | collective-permute-start | bytes 1769480 | tf_op jit(solution)/shard_map/ppermute | solution.py:182
  234.6 76.1 %collective-permute-start.10 = (f32[768,192]{0,1:T(8,128)S(1)}, f32[768,192]{0,1:T(8,128)}, u32[]{:S(2)}, u32[]{:S(2)}) collective-permute-start(f32[768,192]{0,1:T(8,128)S(1)} %pad_maximum_fusion), channel_id=1, source_target_pairs={{0,3},{1,2},{2,1},{3,0},{4,7},{5,6},{6,5},{7,4},{8,11},{9,10},{10,... | collective-permute-start | bytes 1769480 | tf_op jit(solution)/shard_map/ppermute | solution.py:182
  268.2 12.8 %collective-permute-start.1 = (f32[256,256]{1,0:T(8,128)S(1)}, f32[256,256]{1,0:T(8,128)S(1)}, u32[]{:S(2)}, u32[]{:S(2)}) collective-permute-start(f32[256,256]{1,0:T(8,128)S(1)} %constant_dynamic-slice_fusion), channel_id=1, source_target_pairs={{0,1},{1,0},{2,3},{3,2},{4,5},{5,4},{6,7},{7,6},{8,9},{9,8},{10,11... | collective-permute-start | bytes 786440 | tf_op jit(solution)/shard_map/ppermute | solution.py:182
  281.1 26.5 %copy-start.5 = (f32[256,256]{1,0:T(8,128)}, f32[256,256]{1,0:T(8,128)S(1)}, u32[]{:S(2)}) copy-start(f32[256,256]{1,0:T(8,128)S(1)} %dynamic-slice_add_fusion.1) | copy-start | bytes 786436
  281.1 14.3 %collective-permute-start.2 = (f32[256,256]{1,0:T(8,128)S(1)}, f32[256,256]{1,0:T(8,128)S(1)}, u32[]{:S(2)}, u32[]{:S(2)}) collective-permute-start(f32[256,256]{1,0:T(8,128)S(1)} %dynamic-slice_add_fusion.1), channel_id=1, source_target_pairs={{0,1},{1,0},{2,3},{3,2},{4,5},{5,4},{6,7},{7,6},{8,9},{9,8},{10,11... | collective-permute-start | bytes 786440 | tf_op jit(solution)/shard_map/ppermute | solution.py:182
  295.4 26.8 %collective-permute-start.8 = (f32[768,192]{0,1:T(8,128)S(1)}, f32[768,192]{0,1:T(8,128)}, u32[]{:S(2)}, u32[]{:S(2)}) collective-permute-start(f32[768,192]{0,1:T(8,128)S(1)} %pad_maximum_fusion), channel_id=1, source_target_pairs={{0,1},{1,0},{2,3},{3,2},{4,5},{5,4},{6,7},{7,6},{8,9},{9,8},{10,11... | collective-permute-start | bytes 1769480 | tf_op jit(solution)/shard_map/ppermute | solution.py:182
  300.2 22.0 %copy-start.7 = (f32[768,64]{0,1:T(8,128)S(1)}, f32[768,64]{0,1:T(8,128)}, u32[]{:S(2)}) copy-start(f32[768,64]{0,1:T(8,128)} %fusion.6) | copy-start | bytes 589828
  307.6 102.3 %collective-permute-start.13 = (bf16[768,3584]{1,0:T(8,128)(2,1)}, bf16[768,3584]{1,0:T(8,128)(2,1)}, u32[]{:S(2)}, u32[]{:S(2)}) collective-permute-start(bf16[768,3584]{1,0:T(8,128)(2,1)} %refs_8_.1), channel_id=1, source_target_pairs={{8,16},{12,20},{16,8},{20,12},{9,17},{13,21},{17,9},{21,13},{10,18... | collective-permute-start | bytes 16515080 | tf_op jit(solution)/shard_map/ppermute | solution.py:198
  310.7 16.6 %collective-permute-start.3 = (f32[512,256]{1,0:T(8,128)S(1)}, f32[512,256]{1,0:T(8,128)}, u32[]{:S(2)}, u32[]{:S(2)}) collective-permute-start(f32[512,256]{1,0:T(8,128)S(1)} %maximum_select_fusion.2), channel_id=1, source_target_pairs={{0,2},{1,3},{2,0},{3,1},{4,6},{5,7},{6,4},{7,5},{8,10},{9,11},{10,... | collective-permute-start | bytes 1572872 | tf_op jit(solution)/shard_map/ppermute | solution.py:182
  324.1 138.3 %collective-permute-start.15 = (bf16[768,64]{0,1:T(8,128)(2,1)S(1)}, bf16[768,64]{0,1:T(8,128)(2,1)S(1)}, u32[]{:S(2)}, u32[]{:S(2)}) collective-permute-start(bf16[768,64]{0,1:T(8,128)(2,1)S(1)} %get-tuple-element.27), channel_id=1, source_target_pairs={{0,24},{4,28},{8,16},{12,20},{16,8},{20,12},{24,0},{28,4},{1,25},{... | collective-permute-start | bytes 294920 | tf_op jit(solution)/shard_map/ppermute | solution.py:198
  334.9 137.7 %collective-permute-start.20 = (f32[256,2048]{1,0:T(8,128)S(1)}, f32[256,2048]{1,0:T(8,128)}, u32[]{:S(2)}, u32[]{:S(2)}) collective-permute-start(f32[256,2048]{1,0:T(8,128)S(1)} %fusion.14), channel_id=1, source_target_pairs={{0,4},{4,0},{8,12},{12,8},{16,20},{20,16},{24,28},{28,24},{1,5},{5... | collective-permute-start | bytes 6291464 | tf_op jit(solution)/shard_map/ppermute | solution.py:182
  334.9 77.5 %collective-permute-start.14 = (bf16[768,2048]{1,0:T(8,128)(2,1)}, bf16[768,2048]{1,0:T(8,128)(2,1)}, u32[]{:S(2)}, u32[]{:S(2)}) collective-permute-start(bf16[768,2048]{1,0:T(8,128)(2,1)} %slice.66), channel_id=1, source_target_pairs={{0,24},{4,28},{24,0},{28,4},{1,25},{5,29},{25,1},{29,5},{2,26},{6,... | collective-permute-start | bytes 9437192 | tf_op jit(solution)/shard_map/ppermute | solution.py:198
  373.3 70.4 %collective-permute-start.12 = (bf16[768,1024]{1,0:T(8,128)(2,1)}, bf16[768,1024]{1,0:T(8,128)(2,1)}, u32[]{:S(2)}, u32[]{:S(2)}) collective-permute-start(bf16[768,1024]{1,0:T(8,128)(2,1)} %slice.63), channel_id=1, source_target_pairs={{0,24},{4,28},{24,0},{28,4},{1,25},{5,29},{25,1},{29,5},{2,26},{6,... | collective-permute-start | bytes 4718600 | tf_op jit(solution)/shard_map/ppermute | solution.py:198
  409.9 50.1 %collective-permute-start.11 = (bf16[768,512]{1,0:T(8,128)(2,1)}, bf16[768,512]{1,0:T(8,128)(2,1)S(1)}, u32[]{:S(2)}, u32[]{:S(2)}) collective-permute-start(bf16[768,512]{1,0:T(8,128)(2,1)} %slice.62), channel_id=1, source_target_pairs={{0,24},{4,28},{24,0},{28,4},{1,25},{5,29},{25,1},{29,5},{2,26},{6,... | collective-permute-start | bytes 2359304 | tf_op jit(solution)/shard_map/ppermute | solution.py:198
  462.7 6.2 %collective-permute-start.16 = (f32[3,4096]{1,0:T(4,128)S(1)}, f32[3,4096]{1,0:T(4,128)S(1)}, u32[]{:S(2)}, u32[]{:S(2)}) collective-permute-start(f32[3,4096]{1,0:T(4,128)S(1)} %reshape.102), channel_id=1, source_target_pairs={{0,24},{4,28},{8,16},{12,20},{16,8},{20,12},{24,0},{28,4},{1,25},{... | collective-permute-start | bytes 147464 | tf_op jit(solution)/shard_map/ppermute | solution.py:198
  469.0 7.0 %collective-permute-start.18 = (f32[3,4096]{1,0:T(4,128)S(1)}, f32[3,4096]{1,0:T(4,128)S(1)}, u32[]{:S(2)}, u32[]{:S(2)}) collective-permute-start(f32[3,4096]{1,0:T(4,128)S(1)} %add.178), channel_id=1, source_target_pairs={{0,2},{1,3},{2,0},{3,1},{4,6},{5,7},{6,4},{7,5},{8,10},{9,11},{10,... | collective-permute-start | bytes 147464 | tf_op jit(solution)/shard_map/ppermute | solution.py:182
  469.0 6.9 %collective-permute-start.19 = (f32[3,4096]{1,0:T(4,128)S(1)}, f32[3,4096]{1,0:T(4,128)S(1)}, u32[]{:S(2)}, u32[]{:S(2)}) collective-permute-start(f32[3,4096]{1,0:T(4,128)S(1)} %add.178), channel_id=1, source_target_pairs={{0,3},{1,2},{2,1},{3,0},{4,7},{5,6},{6,5},{7,4},{8,11},{9,10},{10,... | collective-permute-start | bytes 147464 | tf_op jit(solution)/shard_map/ppermute | solution.py:182
  472.4 4.3 collective-permute-start.17
  591.7 5.1 collective-permute-start.22
  592.4 5.8 collective-permute-start.23
  593.9 4.3 collective-permute-start.21
  599.0 14.2 %collective-permute-start.25 = (f32[24,256]{1,0:T(8,128)S(1)}, f32[24,256]{1,0:T(8,128)S(1)}, u32[]{:S(2)}, u32[]{:S(2)}) collective-permute-start(f32[24,256]{1,0:T(8,128)S(1)} %add_add_fusion.3), channel_id=1, source_target_pairs={{0,2},{1,3},{2,0},{3,1},{4,6},{5,7},{6,4},{7,5},{8,10},{9,11},{10,... | collective-permute-start | bytes 73736 | tf_op jit(solution)/shard_map/ppermute | solution.py:182
  599.3 13.9 %collective-permute-start.26 = (f32[24,256]{1,0:T(8,128)S(1)}, f32[24,256]{1,0:T(8,128)S(1)}, u32[]{:S(2)}, u32[]{:S(2)}) collective-permute-start(f32[24,256]{1,0:T(8,128)S(1)} %add_add_fusion.3), channel_id=1, source_target_pairs={{0,3},{1,2},{2,1},{3,0},{4,7},{5,6},{6,5},{7,4},{8,11},{9,10},{10,... | collective-permute-start | bytes 73736 | tf_op jit(solution)/shard_map/ppermute | solution.py:182
  601.3 11.9 %collective-permute-start.24 = (f32[24,256]{1,0:T(8,128)S(1)}, f32[24,256]{1,0:T(8,128)S(1)}, u32[]{:S(2)}, u32[]{:S(2)}) collective-permute-start(f32[24,256]{1,0:T(8,128)S(1)} %add_add_fusion.3), channel_id=1, source_target_pairs={{0,1},{1,0},{2,3},{3,2},{4,5},{5,4},{6,7},{7,6},{8,9},{9,8},{10,11... | collective-permute-start | bytes 73736 | tf_op jit(solution)/shard_map/ppermute | solution.py:182
  607.8 6.1 copy-start.1
Sparse Core Ops, SparseCore 0:
  9.8 125.0 all-gather.6
  137.1 27.8 all-gather.4
  213.9 113.9 all-gather.8

commit v7 on v6

--- a/solution.py
+++ b/solution.py
@@ -130,7 +130,7 @@
 
     def part(offset, width, pick):
         at = pl.multiple_of(offset, 128)
-        high, low = split(both[:, pl.ds(at, width)])
+        high, low = split(jnp.concatenate([both[i, :, pl.ds(at, width)] for i in range(both.shape[0])], axis=0))
         return jnp.dot(pick, high, preferred_element_type=f32) + jnp.dot(pick, low, preferred_element_type=f32)
 
     def against(x, side):
@@ -206,12 +206,15 @@
     while step < h:
         blocks.update({k ^ step: swap(v, "fsdp", n, step) for k, v in list(blocks.items())})
         step *= 2
-    gate_inner = mirror(gate_pre, inner)
+    head = tiles * 9 // 14
+    gate_inner_a = mirror(gate_pre[:, : head * TILE], inner)
+    part = rows // m
     cot_full = lax.all_gather(cotangent, "solve", axis=1, tiled=True)
-    part = rows // m
     near = cot_full.shape[1] // 2
-    quarter = lax.dynamic_slice(cot_full, (s * part, (1 - side) * near), (part, near))
+    quarter = lax.all_to_all(cotangent, "solve", split_axis=0, concat_axis=1, tiled=True)
+    quarter = lax.dynamic_slice(quarter, (0, (1 - side) * near), (part, near))
     quarter = mirror(quarter)
+    gate_inner_b = mirror(gate_pre[:, head * TILE :], inner)
     cot_far = lax.all_gather(quarter, "solve", axis=0, tiled=True)
     sibling = swap(down_weight, "fsdp", n, 1)
     blocks.update({k ^ 1: swap(v, "fsdp", n, 1) for k, v in list(blocks.items()) if k})
@@ -219,11 +222,10 @@
     order = sorted(blocks)
     weights = [blocks[k] for k in order]
     share = max(1, tiles // 7)
-    cuts = [0, tiles - 3 * share, tiles - share, tiles]
+    cuts = [0, head, tiles - share, tiles]
     chunks = []
     for j, (a, b) in enumerate(zip(cuts[:-1], cuts[1:])):
-        gate_outer, _ = lax.optimization_barrier((gate_pre[:, a * TILE : b * TILE], quarter))
-        gate_outer = mirror(gate_outer, lambda chip: not inner(chip))
+        gate_outer = mirror(gate_pre[:, a * TILE : b * TILE], lambda chip: not inner(chip))
         chunks.append((j, a, b, gate_outer))
 
     gate = gate_pre.astype(f32)
@@ -264,7 +266,8 @@
     own_idx = jnp.stack([f ^ k for k in order]).astype(jnp.int32)
     far_idx = own_idx - side * h
     other_side = swap(query_side, "fsdp", n, 1)
-    own_idx, query_side, _ = lax.optimization_barrier((own_idx, query_side, quarter))
+    own_idx, _ = lax.optimization_barrier((own_idx, quarter))
+    far_idx, query_side = lax.optimization_barrier((far_idx, query_side))
     own = tokens(
         own_idx, cot_full, [(v, 0) for v in weights], [(gate_pre, 0)], None, proj_hidden, 0, tiles
     )
@@ -295,15 +298,18 @@
         if far is not None:
             gate_outer, far = lax.optimization_barrier((gate_outer, far))
         units = slice(a * TILE, b * TILE)
-        gate = gate_inner[:, units].astype(f32) + gate_outer.astype(f32)
+        gate_inner = gate_inner_a if b <= head else gate_inner_b[:, (a - head) * TILE : (b - head) * TILE]
+        gate = gate_inner.astype(f32) + gate_outer.astype(f32)
         grad_up = (grad[:, units] * (gate * jax.nn.sigmoid(gate))).astype(jnp.bfloat16)
         term = jnp.dot(grad_up, proj_hidden[units, half:], preferred_element_type=f32)
         far = term if far is None else far + term
     up_far = pair(far, in_up_far)
-    query_side = split(query_side + other_side)
+    query_side = query_side + other_side
+    high = lax.reduce_precision(query_side, 8, 7)
+    query_side = (high.astype(jnp.bfloat16), (query_side - high).astype(jnp.bfloat16))
     up = up_own + mirror(up_far)
     up = total(up, "solve", m)
-    both = lax.all_gather(jnp.concatenate([up, down], axis=0), "fsdp", axis=0, tiled=True)
+    both = lax.all_gather(jnp.concatenate([up, down], axis=0), "fsdp", axis=0)
 
     examples = n * local_seqs
     row_width = gram.shape[0]

time: 621 us -> 706 us (1.14)
  starting transfers between devices: 45.2 us -> 86.6 us
  blocking collectives: 110 us -> 135 us
  waiting for transfers between devices: 306 us -> 324 us
    all_gather x1, waiting for transfers between devices: 122 us -> 0.01 us  [local(): cot_full = lax.all_gather(cotangent, 'solve', axis=1, tiled=True)]
    ppermute x20, waiting for transfers between devices: 106 us -> 217 us  [swap(): return lax.ppermute(x, axis, [(i, i ^ bit) for i in range(size)])]
    all_to_all x0 -> x1, waiting for transfers between devices: none -> 36.3 us  [local(): lax.all_to_all(cotangent, 'solve', split_axis=0, concat_axis=1, tiled=True)]
    ppermute x20, starting transfers between devices: 24.5 us -> 53.1 us  [swap(): return lax.ppermute(x, axis, [(i, i ^ bit) for i in range(size)])]
    all_gather x1, blocking collectives: 110 us -> 135 us  [local(): both = lax.all_gather(jnp.concatenate([up, down], axis=0), 'fsdp', axis=0)]
    ppermute x7 -> x8, waiting for transfers between devices: 77.6 us -> 69.9 us  [mirror(): return lax.ppermute(x, 'fsdp', pairs)]
    ppermute x7 -> x8, starting transfers between devices: 20.6 us -> 27.9 us  [mirror(): return lax.ppermute(x, 'fsdp', pairs)]
  transfers between devices with their start and end apart: 30 -> 32, of which waited for: 13 -> 13; matrix products, arithmetic and copies ran while one was open for 10% -> 9% of each run, Pallas kernels for 12% -> 11%
where the time goes in v7:
time: 706 us; the launch traced here: 705 us
  waiting for transfers between devices  324 us (46%)
  blocking collectives  135 us (19%)
  starting transfers between devices  86.6 us (12%)
  Pallas kernels  80.4 us (11%)
  matrix products  38.2 us (5%)
  local copies, waits for them, and re-layouts  17.2 us (2%)
  between operations  14.1 us (2%)
  other arithmetic  10.1 us (1%)
    ppermute x20, waiting for transfers between devices, swap(): return lax.ppermute(x, axis, [(i, i ^ bit) for i in range(size)])  217 us
    all_gather x1, blocking collectives, local(): both = lax.all_gather(jnp.concatenate([up, down], axis=0), 'fsdp', axis=0)  135 us
    ppermute x8, waiting for transfers between devices, mirror(): return lax.ppermute(x, 'fsdp', pairs)  69.9 us
    ppermute x20, starting transfers between devices, swap(): return lax.ppermute(x, axis, [(i, i ^ bit) for i in range(size)])  53.1 us
    all_to_all x1, waiting for transfers between devices, local(): lax.all_to_all(cotangent, 'solve', split_axis=0, concat_axis=1, tiled=True)  36.3 us
    pallas_call x1, Pallas kernels, tokens(): pl.pallas_call(functools.partial(tokens_kernel, count, len(gate_parts), s...  34.7 us
    pallas_call x1, Pallas kernels, gradient(): pl.pallas_call(functools.partial(grad_kernel, count), out_shape=jax.Shape...  31.4 us
    ppermute x8, starting transfers between devices, mirror(): return lax.ppermute(x, 'fsdp', pairs)  27.9 us
  transfers between devices with their start and end apart: 32, of which 13 were waited for; matrix products, arithmetic and copies ran while one was open for 9% of the time, Pallas kernels for 11%

profile of v7, /device:TPU:0, one launch (start us, length us, event | category | flops | bytes accessed | tf_op | source)
XLA Modules:
  0.0 705.1 jit_solution(4135907226368333342)
XLA Ops:
  7.2 5.5 all-to-all-start
  13.5 36.3 %all-to-all-done = bf16[4,192,2048]{2,1,0:T(8,128)(2,1)} async-done(((bf16[4,192,2048]{2,1,0:T(8,128)(2,1)}), bf16[4,192,2048]{2,1,0:T(8,128)(2,1)}, u32[]{:S(2)}, u32[]{:S(2)}) %all-to-all-start) | async-done | bytes 3145760 | tf_op jit(solution)/shard_map/all_to_all | solution.py:214
  49.8 2.3 copy.49
  52.2 3.9 collective-permute-start
  56.1 33.8 %collective-permute-done = bf16[192,4096]{1,0:T(8,128)(2,1)} collective-permute-done((bf16[192,4096]{1,0:T(8,128)(2,1)S(1)}, bf16[192,4096]{1,0:T(8,128)(2,1)}, u32[]{:S(2)}, u32[]{:S(2)}) %collective-permute-start) | collective-permute-done | bytes 1572896 | tf_op jit(solution)/shard_map/ppermute | solution.py:198
  90.1 33.4 %collective-permute-start.2 = (bf16[3584,1024]{1,0:T(8,128)(2,1)}, bf16[3584,1024]{1,0:T(8,128)(2,1)}, u32[]{:S(2)}, u32[]{:S(2)}) collective-permute-start(bf16[3584,1024]{1,0:T(8,128)(2,1)} %refs_4_.3), channel_id=1, source_target_pairs={{0,8},{4,12},{8,0},{12,4},{16,24},{20,28},{24,16},{28,20},{1,9},{5... | collective-permute-start | bytes 22020104 | tf_op jit(solution)/shard_map/ppermute | solution.py:182
  123.5 157.5 %collective-permute-done.2.refs_6_ = bf16[3584,1024]{1,0:T(8,128)(2,1)} collective-permute-done((bf16[3584,1024]{1,0:T(8,128)(2,1)}, bf16[3584,1024]{1,0:T(8,128)(2,1)}, u32[]{:S(2)}, u32[]{:S(2)}) %collective-permute-start.2) | collective-permute-done | bytes 7340064 | tf_op jit(solution)/shard_map/ppermute | solution.py:182
  281.1 3.2 fusion.26
  285.4 6.4 fusion.6
  291.9 6.0 fusion.58
  298.0 1.5 collective-permute-start.9
  302.4 34.2 %collective-permute-done.9 = f32[512,256]{1,0:T(8,128)S(1)} collective-permute-done((f32[512,256]{1,0:T(8,128)S(1)}, f32[512,256]{1,0:T(8,128)S(1)}, u32[]{:S(2)}, u32[]{:S(2)}) %collective-permute-start.9) | collective-permute-done | bytes 524320 | tf_op jit(solution)/shard_map/ppermute | solution.py:182
  336.8 1.4 collective-permute-start.10
  338.2 6.6 collective-permute-done.10
  346.2 5.4 collective-permute-done.5
  351.6 1.5 collective-permute-start.11
  353.7 4.0 slice.66
  358.4 5.2 collective-permute-start.14
  364.8 2.4 collective-permute-start.13
  367.9 2.1 slice.63
  370.0 2.5 slice.64
  372.5 3.0 slice.69
  376.3 1.4 collective-permute-start.12
  379.6 8.8 %collective-permute-done.12 = f32[512,256]{1,0:T(8,128)S(1)} collective-permute-done((f32[512,256]{1,0:T(8,128)S(1)}, f32[512,256]{1,0:T(8,128)S(1)}, u32[]{:S(2)}, u32[]{:S(2)}) %collective-permute-start.12) | collective-permute-done | bytes 524320 | tf_op jit(solution)/shard_map/ppermute | solution.py:182
  389.3 3.3 collective-permute-start.7
  392.6 7.5 %fusion.15 = f32[256,2048]{1,0:T(8,128)S(1)} fusion(f32[1024,2048]{1,0:T(8,128)} %param.20, f32[512,256]{1,0:T(8,128)} %copy-done.7, f32[512,256]{1,0:T(8,128)S(1)} %maximum_select_fusion.2, pred[]{:T(512)S(6)} %eq.38), kind=kOutput, calls=%fused_computation.21 | convolution fusion | flops 3222011904 | bytes 11534337 | tf_op jit(solution)/shard_map/dot_general | solution.py:264
  400.2 4.3 collective-permute-start.8
  404.5 2.0 collective-permute-start.15
  406.5 31.4 %shard_map.131 = f32[768,3584]{1,0:T(8,128)} custom-call(s32[4]{0:T(128)} %get-tuple-element.14.idx, bf16[768,4096]{1,0:T(8,128)(2,1)} %all-gather.10.cloned.1.call-done.refs_0_.refs_1_.refs_2_.refs_3_, bf16[768,4096]{1,0:T(8,128)(2,1)} %all-gather.10.cloned.1.call-done.refs_0_.refs_1_.refs_2_.refs_3_, ...), custom_call_target="tpu_custom_call" | custom-call | flops 22548578304 | bytes 46661632 | tf_op jit(solution)/shard_map/pallas_call | solution.py:105
  437.8 4.1 collective-permute-done.14
  441.9 3.3 collective-permute-start.16
  445.3 6.7 fusion.8
  452.0 31.9 %collective-permute-done.8 = bf16[768,768]{1,0:T(8,128)(2,1)} collective-permute-done((bf16[768,768]{1,0:T(8,128)(2,1)}, bf16[768,768]{1,0:T(8,128)(2,1)}, u32[]{:S(2)}, u32[]{:S(2)}) %collective-permute-start.8) | collective-permute-done | bytes 1179680 | tf_op jit(solution)/shard_map/ppermute | solution.py:198
  483.9 3.3 fusion.13
  487.2 2.6 convolution_add_fusion
  490.2 3.4 collective-permute-start.17
  493.6 34.7 %shard_map.130 = f32[768,128]{1,0:T(8,128)} custom-call(s32[4]{0:T(128)} %get-tuple-element.13.idx, bf16[768,8192]{1,0:T(8,128)(2,1)} %all-gather.6.cloned.1.call-done.refs_0_.refs_1_.refs_2_.refs_3_, bf16[768,8192]{1,0:T(8,128)(2,1)} %all-gather.6.cloned.1.call-done.refs_0_.refs_1_.refs_2_.refs_3_, ...), custom_call_target="tpu_custom_call" | custom-call | flops 23957864448 | bytes 46661632 | tf_op jit(solution)/shard_map/pallas_call | solution.py:64
  531.0 1.5 collective-permute-start.20
  532.4 1.5 collective-permute-start.18
  533.9 3.4 fusion.11
  537.4 134.9 %all-gather.1.both = f32[8,6,4096]{2,1,0:T(8,128)} all-gather(f32[1,6,4096]{2,1,0:T(8,128)S(1)} %maximum_bitcast_fusion), channel_id=2, replica_groups=mesh['fsdp'=8,'solve'=4] {'fsdp'}, dimensions={0}, use_global_device_ids=true | all-gather | bytes 884736 | tf_op jit(solution)/shard_map/all_gather | solution.py:312
  672.4 3.6 shard_map.132
  676.8 2.1 collective-permute-start.24
  679.5 1.6 collective-permute-done.23
  681.1 1.6 collective-permute-done.24
  684.3 1.8 collective-permute-start.27
  687.2 5.3 shard_map.133.refs_0_
  692.5 5.4 shard_map.134
  (93 shorter events, 21.3 us)
Async XLA Ops:
  7.2 277.1 %copy-start = (bf16[768,2048]{1,0:T(8,128)(2,1)S(1)}, bf16[768,2048]{1,0:T(8,128)(2,1)}, u32[]{:S(2)}) copy-start(bf16[768,2048]{1,0:T(8,128)(2,1)} %param.11) | copy-start | bytes 9437188
  7.2 5.5 copy-start.8
  7.2 42.6 %all-to-all-start = ((bf16[4,192,2048]{2,1,0:T(8,128)(2,1)}), bf16[4,192,2048]{2,1,0:T(8,128)(2,1)}, u32[]{:S(2)}, u32[]{:S(2)}) async-start(bf16[4,192,2048]{2,1,0:T(8,128)(2,1)} %bitcast.39), calls=%async_computation | async-start | bytes 6291456 | tf_op jit(solution)/shard_map/all_to_all | solution.py:214
  12.7 279.3 %all-gather.8.cloned.1.call-start = ((), (), s32[]{:S(2)}) async-start(), calls=%async_computation.2 | async-start | bytes 1179648 | tf_op jit(solution)/shard_map/all_gather | solution.py:243
  13.4 393.1 %all-gather.10.cloned.1.call-start = ((), (), s32[]{:S(2)}) async-start(), calls=%async_computation.3 | async-start | bytes 7864320 | tf_op jit(solution)/shard_map/all_gather | solution.py:218
  52.2 37.8 %collective-permute-start = (bf16[192,4096]{1,0:T(8,128)(2,1)S(1)}, bf16[192,4096]{1,0:T(8,128)(2,1)}, u32[]{:S(2)}, u32[]{:S(2)}) collective-permute-start(bf16[192,4096]{1,0:T(8,128)(2,1)S(1)} %constant_dynamic-slice_fusion.2), channel_id=1, source_target_pairs={{0,24},{4,28},{8,16},{12,20},{16,8},{20,12},{24,0},{28,4},{1,25},{... | collective-permute-start | bytes 4718600 | tf_op jit(solution)/shard_map/ppermute | solution.py:198
  90.0 403.6 %all-gather.6.cloned.1.call-start = ((), (), s32[]{:S(2)}) async-start(), calls=%async_computation.1 | async-start | bytes 15728640 | tf_op jit(solution)/shard_map/all_gather | solution.py:212
  90.1 191.0 %collective-permute-start.2 = (bf16[3584,1024]{1,0:T(8,128)(2,1)}, bf16[3584,1024]{1,0:T(8,128)(2,1)}, u32[]{:S(2)}, u32[]{:S(2)}) collective-permute-start(bf16[3584,1024]{1,0:T(8,128)(2,1)} %refs_4_.3), channel_id=1, source_target_pairs={{0,8},{4,12},{8,0},{12,4},{16,24},{20,28},{24,16},{28,20},{1,9},{5... | collective-permute-start | bytes 22020104 | tf_op jit(solution)/shard_map/ppermute | solution.py:182
  123.5 276.7 %collective-permute-start.1 = (bf16[3584,1024]{1,0:T(8,128)(2,1)}, bf16[3584,1024]{1,0:T(8,128)(2,1)}, u32[]{:S(2)}, u32[]{:S(2)}) collective-permute-start(bf16[3584,1024]{1,0:T(8,128)(2,1)} %refs_4_.3), channel_id=1, source_target_pairs={{0,4},{4,0},{8,12},{12,8},{16,20},{20,16},{24,28},{28,24},{1,5},{5... | collective-permute-start | bytes 22020104 | tf_op jit(solution)/shard_map/ppermute | solution.py:182
  281.1 123.4 %collective-permute-start.3 = (bf16[3584,1024]{1,0:T(8,128)(2,1)}, bf16[3584,1024]{1,0:T(8,128)(2,1)}, u32[]{:S(2)}, u32[]{:S(2)}) collective-permute-start(bf16[3584,1024]{1,0:T(8,128)(2,1)} %collective-permute-done.2.refs_6_), channel_id=1, source_target_pairs={{0,4},{4,0},{8,12},{12,8},{16,20},{20,16},{24,28},{28,24},{1,5},{5... | collective-permute-start | bytes 22020104 | tf_op jit(solution)/shard_map/ppermute | solution.py:182
  281.1 3.2 copy-start.2
  281.1 4.4 copy-start.10
  291.9 10.5 %copy-start.9 = (s32[3]{0:T(128)S(1)}, s32[3]{0:T(128)}, u32[]{:S(2)}) copy-start(s32[3]{0:T(128)} %param.18) | copy-start | bytes 40
  298.0 38.7 %collective-permute-start.9 = (f32[512,256]{1,0:T(8,128)S(1)}, f32[512,256]{1,0:T(8,128)S(1)}, u32[]{:S(2)}, u32[]{:S(2)}) collective-permute-start(f32[512,256]{1,0:T(8,128)S(1)} %constant_dynamic-slice_fusion.1), channel_id=1, source_target_pairs={{0,2},{1,3},{2,0},{3,1},{4,6},{5,7},{6,4},{7,5},{8,10},{9,11},{10,... | collective-permute-start | bytes 1572872 | tf_op jit(solution)/shard_map/ppermute | solution.py:182
  300.3 51.3 %collective-permute-start.5 = (f32[768,192]{0,1:T(8,128)}, f32[768,192]{0,1:T(8,128)S(1)}, u32[]{:S(2)}, u32[]{:S(2)}) collective-permute-start(f32[768,192]{0,1:T(8,128)} %pad_maximum_fusion), channel_id=1, source_target_pairs={{0,2},{1,3},{2,0},{3,1},{4,6},{5,7},{6,4},{7,5},{8,10},{9,11},{10,... | collective-permute-start | bytes 1769480 | tf_op jit(solution)/shard_map/ppermute | solution.py:182
  300.9 57.5 %collective-permute-start.6 = (f32[768,192]{0,1:T(8,128)}, f32[768,192]{0,1:T(8,128)}, u32[]{:S(2)}, u32[]{:S(2)}) collective-permute-start(f32[768,192]{0,1:T(8,128)} %pad_maximum_fusion), channel_id=1, source_target_pairs={{0,3},{1,2},{2,1},{3,0},{4,7},{5,6},{6,5},{7,4},{8,11},{9,10},{10,... | collective-permute-start | bytes 1769480 | tf_op jit(solution)/shard_map/ppermute | solution.py:182
  336.8 8.1 %collective-permute-start.10 = (f32[256,256]{1,0:T(8,128)S(1)}, f32[256,256]{1,0:T(8,128)S(1)}, u32[]{:S(2)}, u32[]{:S(2)}) collective-permute-start(f32[256,256]{1,0:T(8,128)S(1)} %constant_dynamic-slice_fusion), channel_id=1, source_target_pairs={{0,1},{1,0},{2,3},{3,2},{4,5},{5,4},{6,7},{7,6},{8,9},{9,8},{10,11... | collective-permute-start | bytes 786440 | tf_op jit(solution)/shard_map/ppermute | solution.py:182
  344.9 30.6 %collective-permute-start.4 = (f32[768,192]{0,1:T(8,128)}, f32[768,192]{0,1:T(8,128)S(1)}, u32[]{:S(2)}, u32[]{:S(2)}) collective-permute-start(f32[768,192]{0,1:T(8,128)} %pad_maximum_fusion), channel_id=1, source_target_pairs={{0,1},{1,0},{2,3},{3,2},{4,5},{5,4},{6,7},{7,6},{8,9},{9,8},{10,11... | collective-permute-start | bytes 1769480 | tf_op jit(solution)/shard_map/ppermute | solution.py:182
  346.2 29.2 %copy-start.3 = (f32[256,256]{1,0:T(8,128)}, f32[256,256]{1,0:T(8,128)S(1)}, u32[]{:S(2)}) copy-start(f32[256,256]{1,0:T(8,128)S(1)} %dynamic-slice_add_fusion.1) | copy-start | bytes 786436
  351.6 6.1 copy-start.4
  351.6 13.2 %collective-permute-start.11 = (f32[256,256]{1,0:T(8,128)S(1)}, f32[256,256]{1,0:T(8,128)S(1)}, u32[]{:S(2)}, u32[]{:S(2)}) collective-permute-start(f32[256,256]{1,0:T(8,128)S(1)} %dynamic-slice_add_fusion.1), channel_id=1, source_target_pairs={{0,1},{1,0},{2,3},{3,2},{4,5},{5,4},{6,7},{7,6},{8,9},{9,8},{10,11... | collective-permute-start | bytes 786440 | tf_op jit(solution)/shard_map/ppermute | solution.py:182
  358.4 83.5 %collective-permute-start.14 = (bf16[768,2304]{1,0:T(8,128)(2,1)}, bf16[768,2304]{1,0:T(8,128)(2,1)}, u32[]{:S(2)}, u32[]{:S(2)}) collective-permute-start(bf16[768,2304]{1,0:T(8,128)(2,1)} %slice.66), channel_id=1, source_target_pairs={{0,24},{4,28},{24,0},{28,4},{1,25},{5,29},{25,1},{29,5},{2,26},{6,... | collective-permute-start | bytes 10616840 | tf_op jit(solution)/shard_map/ppermute | solution.py:198
  364.8 80.4 %collective-permute-start.13 = (bf16[768,2304]{1,0:T(8,128)(2,1)}, bf16[768,2304]{1,0:T(8,128)(2,1)}, u32[]{:S(2)}, u32[]{:S(2)}) collective-permute-start(bf16[768,2304]{1,0:T(8,128)(2,1)} %slice.66), channel_id=1, source_target_pairs={{8,16},{12,20},{16,8},{20,12},{9,17},{13,21},{17,9},{21,13},{10,18... | collective-permute-start | bytes 10616840 | tf_op jit(solution)/shard_map/ppermute | solution.py:198
  370.0 7.8 %copy-start.5 = (f32[768,192]{0,1:T(8,128)S(1)}, f32[768,192]{0,1:T(8,128)}, u32[]{:S(2)}) copy-start(f32[768,192]{0,1:T(8,128)} %copy-done.4) | copy-start | bytes 1769476
  375.5 0.8 copy-start.6
  376.3 12.1 %collective-permute-start.12 = (f32[512,256]{1,0:T(8,128)S(1)}, f32[512,256]{1,0:T(8,128)S(1)}, u32[]{:S(2)}, u32[]{:S(2)}) collective-permute-start(f32[512,256]{1,0:T(8,128)S(1)} %maximum_select_fusion.2), channel_id=1, source_target_pairs={{0,2},{1,3},{2,0},{3,1},{4,6},{5,7},{6,4},{7,5},{8,10},{9,11},{10,... | collective-permute-start | bytes 1572872 | tf_op jit(solution)/shard_map/ppermute | solution.py:182
  388.5 0.8 copy-start.7
  389.3 97.9 %collective-permute-start.7 = (bf16[768,512]{1,0:T(8,128)(2,1)}, bf16[768,512]{1,0:T(8,128)(2,1)}, u32[]{:S(2)}, u32[]{:S(2)}) collective-permute-start(bf16[768,512]{1,0:T(8,128)(2,1)} %slice.63), channel_id=1, source_target_pairs={{0,24},{4,28},{24,0},{28,4},{1,25},{5,29},{25,1},{29,5},{2,26},{6,... | collective-permute-start | bytes 2359304 | tf_op jit(solution)/shard_map/ppermute | solution.py:198
  400.2 83.7 %collective-permute-start.8 = (bf16[768,768]{1,0:T(8,128)(2,1)}, bf16[768,768]{1,0:T(8,128)(2,1)}, u32[]{:S(2)}, u32[]{:S(2)}) collective-permute-start(bf16[768,768]{1,0:T(8,128)(2,1)} %slice.64), channel_id=1, source_target_pairs={{0,24},{4,28},{24,0},{28,4},{1,25},{5,29},{25,1},{29,5},{2,26},{6,... | collective-permute-start | bytes 3538952 | tf_op jit(solution)/shard_map/ppermute | solution.py:198
  404.5 79.4 %collective-permute-start.15 = (bf16[768,1280]{1,0:T(8,128)(2,1)}, bf16[768,1280]{1,0:T(8,128)(2,1)}, u32[]{:S(2)}, u32[]{:S(2)}) collective-permute-start(bf16[768,1280]{1,0:T(8,128)(2,1)} %slice.69), channel_id=1, source_target_pairs={{8,16},{12,20},{16,8},{20,12},{9,17},{13,21},{17,9},{21,13},{10,18... | collective-permute-start | bytes 5898248 | tf_op jit(solution)/shard_map/ppermute | solution.py:198
  441.9 47.9 %collective-permute-start.16 = (bf16[768,64]{0,1:T(8,128)(2,1)S(1)}, bf16[768,64]{0,1:T(8,128)(2,1)S(1)}, u32[]{:S(2)}, u32[]{:S(2)}) collective-permute-start(bf16[768,64]{0,1:T(8,128)(2,1)S(1)} %get-tuple-element.23), channel_id=1, source_target_pairs={{0,24},{4,28},{8,16},{12,20},{16,8},{20,12},{24,0},{28,4},{1,25},{... | collective-permute-start | bytes 294920 | tf_op jit(solution)/shard_map/ppermute | solution.py:198
  445.3 88.6 %collective-permute-start.21 = (f32[256,2048]{1,0:T(8,128)S(1)}, f32[256,2048]{1,0:T(8,128)}, u32[]{:S(2)}, u32[]{:S(2)}) collective-permute-start(f32[256,2048]{1,0:T(8,128)S(1)} %fusion.15), channel_id=1, source_target_pairs={{0,4},{4,0},{8,12},{12,8},{16,20},{20,16},{24,28},{28,24},{1,5},{5... | collective-permute-start | bytes 6291464 | tf_op jit(solution)/shard_map/ppermute | solution.py:182
  490.2 40.1 %collective-permute-start.17 = (f32[3,4096]{1,0:T(4,128)S(1)}, f32[3,4096]{1,0:T(4,128)S(1)}, u32[]{:S(2)}, u32[]{:S(2)}) collective-permute-start(f32[3,4096]{1,0:T(4,128)S(1)} %reshape.105), channel_id=1, source_target_pairs={{0,24},{4,28},{8,16},{12,20},{16,8},{20,12},{24,0},{28,4},{1,25},{... | collective-permute-start | bytes 147464 | tf_op jit(solution)/shard_map/ppermute | solution.py:198
  530.3 7.0 collective-permute-start.19
  531.0 6.4 collective-permute-start.20
  532.4 4.9 collective-permute-start.18
  676.0 5.1 collective-permute-start.23
  676.8 6.0 collective-permute-start.24
  678.8 4.1 collective-permute-start.22
  683.7 14.2 %collective-permute-start.26 = (f32[24,256]{1,0:T(8,128)S(1)}, f32[24,256]{1,0:T(8,128)S(1)}, u32[]{:S(2)}, u32[]{:S(2)}) collective-permute-start(f32[24,256]{1,0:T(8,128)S(1)} %add_add_fusion.3), channel_id=1, source_target_pairs={{0,2},{1,3},{2,0},{3,1},{4,6},{5,7},{6,4},{7,5},{8,10},{9,11},{10,... | collective-permute-start | bytes 73736 | tf_op jit(solution)/shard_map/ppermute | solution.py:182
  684.3 13.7 %collective-permute-start.27 = (f32[24,256]{1,0:T(8,128)S(1)}, f32[24,256]{1,0:T(8,128)S(1)}, u32[]{:S(2)}, u32[]{:S(2)}) collective-permute-start(f32[24,256]{1,0:T(8,128)S(1)} %add_add_fusion.3), channel_id=1, source_target_pairs={{0,3},{1,2},{2,1},{3,0},{4,7},{5,6},{6,5},{7,4},{8,11},{9,10},{10,... | collective-permute-start | bytes 73736 | tf_op jit(solution)/shard_map/ppermute | solution.py:182
  686.1 11.9 %collective-permute-start.25 = (f32[24,256]{1,0:T(8,128)S(1)}, f32[24,256]{1,0:T(8,128)S(1)}, u32[]{:S(2)}, u32[]{:S(2)}) collective-permute-start(f32[24,256]{1,0:T(8,128)S(1)} %add_add_fusion.3), channel_id=1, source_target_pairs={{0,1},{1,0},{2,3},{3,2},{4,5},{5,4},{6,7},{7,6},{8,9},{9,8},{10,11... | collective-permute-start | bytes 73736 | tf_op jit(solution)/shard_map/ppermute | solution.py:182
  692.5 6.1 copy-start.1
Sparse Core Ops, SparseCore 0:
  15.6 24.4 all-gather.7
  90.1 100.9 all-gather.9
  193.0 149.0 all-gather.5

commit v8 on v6

--- a/solution.py
+++ b/solution.py
@@ -130,7 +130,7 @@
 
     def part(offset, width, pick):
         at = pl.multiple_of(offset, 128)
-        high, low = split(both[:, pl.ds(at, width)])
+        high, low = split(jnp.concatenate([both[i, :, pl.ds(at, width)] for i in range(both.shape[0])], axis=0))
         return jnp.dot(pick, high, preferred_element_type=f32) + jnp.dot(pick, low, preferred_element_type=f32)
 
     def against(x, side):
@@ -300,10 +300,12 @@
         term = jnp.dot(grad_up, proj_hidden[units, half:], preferred_element_type=f32)
         far = term if far is None else far + term
     up_far = pair(far, in_up_far)
-    query_side = split(query_side + other_side)
+    query_side = query_side + other_side
+    high = lax.reduce_precision(query_side, 8, 7)
+    query_side = (high.astype(jnp.bfloat16), (query_side - high).astype(jnp.bfloat16))
     up = up_own + mirror(up_far)
     up = total(up, "solve", m)
-    both = lax.all_gather(jnp.concatenate([up, down], axis=0), "fsdp", axis=0, tiled=True)
+    both = lax.all_gather(jnp.concatenate([up, down], axis=0), "fsdp", axis=0)
 
     examples = n * local_seqs
     row_width = gram.shape[0]

time: 621 us -> 621 us (level)
  no operation moved by 1% of the time
where the time goes in v8:
time: 621 us; the launch traced here: 620 us
  waiting for transfers between devices  306 us (49%)
  blocking collectives  111 us (18%)
  Pallas kernels  80.4 us (13%)
  starting transfers between devices  45.2 us (7%)
  matrix products  39.1 us (6%)
  between operations  14.1 us (2%)
  local copies, waits for them, and re-layouts  12.7 us (2%)
  other arithmetic  11.4 us (2%)
    all_gather x1, waiting for transfers between devices, local(): cot_full = lax.all_gather(cotangent, 'solve', axis=1, tiled=True)  122 us
    all_gather x1, blocking collectives, local(): both = lax.all_gather(jnp.concatenate([up, down], axis=0), 'fsdp', axis=0)  111 us
    ppermute x20, waiting for transfers between devices, swap(): return lax.ppermute(x, axis, [(i, i ^ bit) for i in range(size)])  106 us
    ppermute x7, waiting for transfers between devices, mirror(): return lax.ppermute(x, 'fsdp', pairs)  77.6 us
    pallas_call x1, Pallas kernels, tokens(): pl.pallas_call(functools.partial(tokens_kernel, count, len(gate_parts), s...  34.7 us
    pallas_call x1, Pallas kernels, gradient(): pl.pallas_call(functools.partial(grad_kernel, count), out_shape=jax.Shape...  31.4 us
    ppermute x20, starting transfers between devices, swap(): return lax.ppermute(x, axis, [(i, i ^ bit) for i in range(size)])  24.5 us
    ppermute x7, starting transfers between devices, mirror(): return lax.ppermute(x, 'fsdp', pairs)  20.6 us
  transfers between devices with their start and end apart: 30, of which 13 were waited for; matrix products, arithmetic and copies ran while one was open for 10% of the time, Pallas kernels for 12%

profile of v8, /device:TPU:0, one launch (start us, length us, event | category | flops | bytes accessed | tf_op | source)
XLA Modules:
  0.0 620.0 jit_solution(17279802978621865718)
XLA Ops:
  8.0 3.1 collective-permute-start.6
  11.1 1.6 convert_element_type.64
  12.8 122.2 %all-gather.8.cloned.1.call-done.refs_0_.refs_1_.refs_2_.refs_3_ = bf16[768,8192]{1,0:T(8,128)(2,1)} async-done(((bf16[768,2048]{1,0:T(8,128)(2,1)}), bf16[768,8192]{1,0:T(8,128)(2,1)}) %all-gather.8.cloned.1.call-update) | async-done | bytes 12582928 | tf_op jit(solution)/shard_map/all_gather | solution.py:210
  135.0 1.5 dynamic_slice.19
  136.5 3.4 collective-permute-start.4
  139.9 38.3 %collective-permute-done.6.refs_6_ = bf16[3584,1024]{1,0:T(8,128)(2,1)} collective-permute-done((bf16[3584,1024]{1,0:T(8,128)(2,1)}, bf16[3584,1024]{1,0:T(8,128)(2,1)}, u32[]{:S(2)}, u32[]{:S(2)}) %collective-permute-start.6) | collective-permute-done | bytes 7340064 | tf_op jit(solution)/shard_map/ppermute | solution.py:182
  178.2 35.6 %collective-permute-done.4 = bf16[192,4096]{1,0:T(8,128)(2,1)} collective-permute-done((bf16[192,4096]{1,0:T(8,128)(2,1)S(1)}, bf16[192,4096]{1,0:T(8,128)(2,1)}, u32[]{:S(2)}, u32[]{:S(2)}) %collective-permute-start.4) | collective-permute-done | bytes 1572896 | tf_op jit(solution)/shard_map/ppermute | solution.py:198
  213.9 8.8 %fusion.6 = f32[768,64]{0,1:T(8,128)} fusion(bf16[768,3584]{1,0:T(8,128)(2,1)} %param.14, bf16[768,3584]{1,0:T(8,128)(2,1)} %refs_8_.1, bf16[3584,128]{1,0:T(8,128)(2,1)} %refs_9_.1), kind=kOutput, calls=%fused_computation.9 | convolution fusion | flops 374341632 | bytes 12124160 | tf_op jit(solution)/shard_map/dot_general | solution.py:233
  222.7 6.6 %fusion.58 = f32[1024,256]{1,0:T(8,128)S(1)} fusion(f32[1024,2048]{1,0:T(8,128)} %param.20, bf16[2048,256]{0,1:T(8,128)(2,1)} %all-gather.6.cloned.1.call-done), kind=kOutput, calls=%fused_computation.97 | convolution fusion | flops 3221225472 | bytes 10485760 | tf_op jit(solution)/shard_map/dot_general | solution.py:242
  230.2 1.6 collective-permute-start
  234.6 2.5 collective-permute-start.10
  237.2 29.8 %collective-permute-done = f32[512,256]{1,0:T(8,128)} collective-permute-done((f32[512,256]{1,0:T(8,128)}, f32[512,256]{1,0:T(8,128)}, u32[]{:S(2)}, u32[]{:S(2)}) %collective-permute-start) | collective-permute-done | bytes 524320 | tf_op jit(solution)/shard_map/ppermute | solution.py:182
  266.9 1.3 dynamic-slice_add_fusion
  268.2 1.5 collective-permute-start.1
  269.8 11.2 %collective-permute-done.1 = f32[256,256]{1,0:T(8,128)S(1)} collective-permute-done((f32[256,256]{1,0:T(8,128)S(1)}, f32[256,256]{1,0:T(8,128)S(1)}, u32[]{:S(2)}, u32[]{:S(2)}) %collective-permute-start.1) | collective-permute-done | bytes 262176 | tf_op jit(solution)/shard_map/ppermute | solution.py:182
  281.1 2.5 collective-permute-start.2
  284.3 11.1 %collective-permute-done.2 = f32[256,256]{1,0:T(8,128)S(1)} collective-permute-done((f32[256,256]{1,0:T(8,128)S(1)}, f32[256,256]{1,0:T(8,128)S(1)}, u32[]{:S(2)}, u32[]{:S(2)}) %collective-permute-start.2) | collective-permute-done | bytes 262176 | tf_op jit(solution)/shard_map/ppermute | solution.py:182
  295.4 2.1 collective-permute-start.8
  298.1 2.1 slice.62
  300.2 2.7 slice.63
  302.9 4.0 slice.66
  307.6 3.1 collective-permute-start.13
  310.7 11.5 %collective-permute-done.8 = f32[768,192]{0,1:T(8,128)} collective-permute-done((f32[768,192]{0,1:T(8,128)S(1)}, f32[768,192]{0,1:T(8,128)}, u32[]{:S(2)}, u32[]{:S(2)}) %collective-permute-start.8) | collective-permute-done | bytes 589856 | tf_op jit(solution)/shard_map/ppermute | solution.py:182
  322.2 1.4 add_add_fusion
  324.1 3.3 collective-permute-start.15
  327.3 7.5 %fusion.15 = f32[256,2048]{1,0:T(8,128)S(1)} fusion(f32[1024,2048]{1,0:T(8,128)} %param.20, f32[512,256]{1,0:T(8,128)} %collective-permute-done.3, f32[512,256]{1,0:T(8,128)S(1)} %maximum_select_fusion.2, pred[]{:T(512)S(6)} %eq.35), kind=kOutput, calls=%fused_computation.21 | convolution fusion | flops 3222011904 | bytes 11534337 | tf_op jit(solution)/shard_map/dot_general | solution.py:262
  334.9 2.5 collective-permute-start.14
  337.5 34.7 %shard_map.130 = f32[768,128]{1,0:T(8,128)} custom-call(s32[4]{0:T(128)} %get-tuple-element.15.idx, bf16[768,8192]{1,0:T(8,128)(2,1)} %all-gather.8.cloned.1.call-done.refs_0_.refs_1_.refs_2_.refs_3_, bf16[768,8192]{1,0:T(8,128)(2,1)} %all-gather.8.cloned.1.call-done.refs_0_.refs_1_.refs_2_.refs_3_, ...), custom_call_target="tpu_custom_call" | custom-call | flops 23957864448 | bytes 46661632 | tf_op jit(solution)/shard_map/pallas_call | solution.py:64
  373.3 5.1 collective-permute-start.12
  378.5 31.4 %shard_map.131 = f32[768,3584]{1,0:T(8,128)} custom-call(s32[4]{0:T(128)} %get-tuple-element.29.idx, bf16[768,4096]{1,0:T(8,128)(2,1)} %all-gather.10.cloned.1.call-done.refs_0_.refs_1_.refs_2_.refs_3_, bf16[768,4096]{1,0:T(8,128)(2,1)} %all-gather.10.cloned.1.call-done.refs_0_.refs_1_.refs_2_.refs_3_, ...), custom_call_target="tpu_custom_call" | custom-call | flops 22548578304 | bytes 46661632 | tf_op jit(solution)/shard_map/pallas_call | solution.py:105
  409.9 2.5 collective-permute-start.11
  412.4 6.1 fusion.9
  418.5 25.2 %collective-permute-done.12 = bf16[768,1024]{1,0:T(8,128)(2,1)} collective-permute-done((bf16[768,1024]{1,0:T(8,128)(2,1)}, bf16[768,1024]{1,0:T(8,128)(2,1)}, u32[]{:S(2)}, u32[]{:S(2)}) %collective-permute-start.12) | collective-permute-done | bytes 1572896 | tf_op jit(solution)/shard_map/ppermute | solution.py:198
  443.7 4.1 fusion.13
  447.8 12.1 %collective-permute-done.11 = bf16[768,512]{1,0:T(8,128)(2,1)S(1)} collective-permute-done((bf16[768,512]{1,0:T(8,128)(2,1)}, bf16[768,512]{1,0:T(8,128)(2,1)S(1)}, u32[]{:S(2)}, u32[]{:S(2)}) %collective-permute-start.11) | collective-permute-done | bytes 786464 | tf_op jit(solution)/shard_map/ppermute | solution.py:198
  460.0 2.4 convolution_add_fusion
  464.3 4.6 collective-permute-done.16
  469.0 3.4 collective-permute-start.19
  472.5 3.4 fusion.11
  476.8 110.9 %all-gather.1.both = f32[8,6,4096]{2,1,0:T(8,128)} all-gather(f32[1,6,4096]{2,1,0:T(8,128)S(1)} %maximum_bitcast_fusion), channel_id=2, replica_groups=mesh['fsdp'=8,'solve'=4] {'fsdp'}, dimensions={0}, use_global_device_ids=true | all-gather | bytes 884736 | tf_op jit(solution)/shard_map/all_gather | solution.py:308
  587.7 3.6 shard_map.132
  592.1 1.5 collective-permute-start.23
  594.8 1.6 collective-permute-done.22
  596.4 1.5 collective-permute-done.23
  598.9 2.0 collective-permute-start.26
  600.9 1.2 collective-permute-start.24
  602.1 5.3 shard_map.133.refs_0_
  607.4 5.4 shard_map.134
  (83 shorter events, 14.9 us)
Async XLA Ops:
  7.2 225.7 %copy-start = (bf16[768,2048]{1,0:T(8,128)(2,1)S(1)}, bf16[768,2048]{1,0:T(8,128)(2,1)}, u32[]{:S(2)}) copy-start(bf16[768,2048]{1,0:T(8,128)(2,1)} %param.11) | copy-start | bytes 9437188
  7.2 127.8 %all-gather.8.cloned.1.call-start = ((), (), s32[]{:S(2)}) async-start(), calls=%async_computation.1 | async-start | bytes 15728640 | tf_op jit(solution)/shard_map/all_gather | solution.py:210
  7.9 214.8 %all-gather.6.cloned.1.call-start = ((), (), s32[]{:S(2)}) async-start(), calls=%async_computation | async-start | bytes 1179648 | tf_op jit(solution)/shard_map/all_gather | solution.py:241
  8.0 170.2 %collective-permute-start.6 = (bf16[3584,1024]{1,0:T(8,128)(2,1)}, bf16[3584,1024]{1,0:T(8,128)(2,1)}, u32[]{:S(2)}, u32[]{:S(2)}) collective-permute-start(bf16[3584,1024]{1,0:T(8,128)(2,1)} %refs_4_.3), channel_id=1, source_target_pairs={{0,8},{4,12},{8,0},{12,4},{16,24},{20,28},{24,16},{28,20},{1,9},{5... | collective-permute-start | bytes 22020104 | tf_op jit(solution)/shard_map/ppermute | solution.py:182
  12.7 365.8 %all-gather.10.cloned.1.call-start = ((), (), s32[]{:S(2)}) async-start(), calls=%async_computation.2 | async-start | bytes 7864320 | tf_op jit(solution)/shard_map/all_gather | solution.py:215
  136.5 77.3 %collective-permute-start.4 = (bf16[192,4096]{1,0:T(8,128)(2,1)S(1)}, bf16[192,4096]{1,0:T(8,128)(2,1)}, u32[]{:S(2)}, u32[]{:S(2)}) collective-permute-start(bf16[192,4096]{1,0:T(8,128)(2,1)S(1)} %dynamic_slice.19), channel_id=1, source_target_pairs={{0,24},{4,28},{8,16},{12,20},{16,8},{20,12},{24,0},{28,4},{1,25},{... | collective-permute-start | bytes 4718600 | tf_op jit(solution)/shard_map/ppermute | solution.py:198
  139.9 195.0 %collective-permute-start.5 = (bf16[3584,1024]{1,0:T(8,128)(2,1)}, bf16[3584,1024]{1,0:T(8,128)(2,1)}, u32[]{:S(2)}, u32[]{:S(2)}) collective-permute-start(bf16[3584,1024]{1,0:T(8,128)(2,1)} %refs_4_.3), channel_id=1, source_target_pairs={{0,4},{4,0},{8,12},{12,8},{16,20},{20,16},{24,28},{28,24},{1,5},{5... | collective-permute-start | bytes 22020104 | tf_op jit(solution)/shard_map/ppermute | solution.py:182
  178.2 159.3 %collective-permute-start.7 = (bf16[3584,1024]{1,0:T(8,128)(2,1)}, bf16[3584,1024]{1,0:T(8,128)(2,1)}, u32[]{:S(2)}, u32[]{:S(2)}) collective-permute-start(bf16[3584,1024]{1,0:T(8,128)(2,1)} %collective-permute-done.6.refs_6_), channel_id=1, source_target_pairs={{0,4},{4,0},{8,12},{12,8},{16,20},{20,16},{24,28},{28,24},{1,5},{5... | collective-permute-start | bytes 22020104 | tf_op jit(solution)/shard_map/ppermute | solution.py:182
  222.7 9.1 %copy-start.2 = (bf16[768,2048]{1,0:T(8,128)(2,1)S(1)}, bf16[768,2048]{1,0:T(8,128)(2,1)}, u32[]{:S(2)}) copy-start(bf16[768,2048]{1,0:T(8,128)(2,1)} %param.12) | copy-start | bytes 9437188
  222.7 9.1 %copy-start.4 = (bf16[2048,128]{1,0:T(8,128)(2,1)S(1)}, bf16[2048,128]{1,0:T(8,128)(2,1)}, u32[]{:S(2)}) copy-start(bf16[2048,128]{1,0:T(8,128)(2,1)} %param.16) | copy-start | bytes 1572868
  229.3 3.6 copy-start.3
  229.4 4.7 copy-start.6
  230.2 54.0 %copy-start.8 = (s32[3]{0:T(128)S(1)}, s32[3]{0:T(128)}, u32[]{:S(2)}) copy-start(s32[3]{0:T(128)} %param.18) | copy-start | bytes 40
  230.2 36.7 %collective-permute-start = (f32[512,256]{1,0:T(8,128)}, f32[512,256]{1,0:T(8,128)}, u32[]{:S(2)}, u32[]{:S(2)}) collective-permute-start(f32[512,256]{1,0:T(8,128)} %constant_dynamic-slice_fusion.1), channel_id=1, source_target_pairs={{0,2},{1,3},{2,0},{3,1},{4,6},{5,7},{6,4},{7,5},{8,10},{9,11},{10,... | collective-permute-start | bytes 1572872 | tf_op jit(solution)/shard_map/ppermute | solution.py:182
  234.1 73.5 %collective-permute-start.9 = (f32[768,192]{0,1:T(8,128)S(1)}, f32[768,192]{0,1:T(8,128)S(1)}, u32[]{:S(2)}, u32[]{:S(2)}) collective-permute-start(f32[768,192]{0,1:T(8,128)S(1)} %pad_maximum_fusion), channel_id=1, source_target_pairs={{0,2},{1,3},{2,0},{3,1},{4,6},{5,7},{6,4},{7,5},{8,10},{9,11},{10,... | collective-permute-start | bytes 1769480 | tf_op jit(solution)/shard_map/ppermute | solution.py:182
  234.6 76.1 %collective-permute-start.10 = (f32[768,192]{0,1:T(8,128)S(1)}, f32[768,192]{0,1:T(8,128)}, u32[]{:S(2)}, u32[]{:S(2)}) collective-permute-start(f32[768,192]{0,1:T(8,128)S(1)} %pad_maximum_fusion), channel_id=1, source_target_pairs={{0,3},{1,2},{2,1},{3,0},{4,7},{5,6},{6,5},{7,4},{8,11},{9,10},{10,... | collective-permute-start | bytes 1769480 | tf_op jit(solution)/shard_map/ppermute | solution.py:182
  268.2 12.8 %collective-permute-start.1 = (f32[256,256]{1,0:T(8,128)S(1)}, f32[256,256]{1,0:T(8,128)S(1)}, u32[]{:S(2)}, u32[]{:S(2)}) collective-permute-start(f32[256,256]{1,0:T(8,128)S(1)} %constant_dynamic-slice_fusion), channel_id=1, source_target_pairs={{0,1},{1,0},{2,3},{3,2},{4,5},{5,4},{6,7},{7,6},{8,9},{9,8},{10,11... | collective-permute-start | bytes 786440 | tf_op jit(solution)/shard_map/ppermute | solution.py:182
  281.1 26.5 %copy-start.5 = (f32[256,256]{1,0:T(8,128)}, f32[256,256]{1,0:T(8,128)S(1)}, u32[]{:S(2)}) copy-start(f32[256,256]{1,0:T(8,128)S(1)} %dynamic-slice_add_fusion.1) | copy-start | bytes 786436
  281.1 14.3 %collective-permute-start.2 = (f32[256,256]{1,0:T(8,128)S(1)}, f32[256,256]{1,0:T(8,128)S(1)}, u32[]{:S(2)}, u32[]{:S(2)}) collective-permute-start(f32[256,256]{1,0:T(8,128)S(1)} %dynamic-slice_add_fusion.1), channel_id=1, source_target_pairs={{0,1},{1,0},{2,3},{3,2},{4,5},{5,4},{6,7},{7,6},{8,9},{9,8},{10,11... | collective-permute-start | bytes 786440 | tf_op jit(solution)/shard_map/ppermute | solution.py:182
  295.4 26.8 %collective-permute-start.8 = (f32[768,192]{0,1:T(8,128)S(1)}, f32[768,192]{0,1:T(8,128)}, u32[]{:S(2)}, u32[]{:S(2)}) collective-permute-start(f32[768,192]{0,1:T(8,128)S(1)} %pad_maximum_fusion), channel_id=1, source_target_pairs={{0,1},{1,0},{2,3},{3,2},{4,5},{5,4},{6,7},{7,6},{8,9},{9,8},{10,11... | collective-permute-start | bytes 1769480 | tf_op jit(solution)/shard_map/ppermute | solution.py:182
  300.2 22.0 %copy-start.7 = (f32[768,64]{0,1:T(8,128)S(1)}, f32[768,64]{0,1:T(8,128)}, u32[]{:S(2)}) copy-start(f32[768,64]{0,1:T(8,128)} %fusion.6) | copy-start | bytes 589828
  307.6 102.3 %collective-permute-start.13 = (bf16[768,3584]{1,0:T(8,128)(2,1)}, bf16[768,3584]{1,0:T(8,128)(2,1)}, u32[]{:S(2)}, u32[]{:S(2)}) collective-permute-start(bf16[768,3584]{1,0:T(8,128)(2,1)} %refs_8_.1), channel_id=1, source_target_pairs={{8,16},{12,20},{16,8},{20,12},{9,17},{13,21},{17,9},{21,13},{10,18... | collective-permute-start | bytes 16515080 | tf_op jit(solution)/shard_map/ppermute | solution.py:198
  310.7 16.6 %collective-permute-start.3 = (f32[512,256]{1,0:T(8,128)S(1)}, f32[512,256]{1,0:T(8,128)}, u32[]{:S(2)}, u32[]{:S(2)}) collective-permute-start(f32[512,256]{1,0:T(8,128)S(1)} %maximum_select_fusion.2), channel_id=1, source_target_pairs={{0,2},{1,3},{2,0},{3,1},{4,6},{5,7},{6,4},{7,5},{8,10},{9,11},{10,... | collective-permute-start | bytes 1572872 | tf_op jit(solution)/shard_map/ppermute | solution.py:182
  324.1 138.3 %collective-permute-start.15 = (bf16[768,64]{0,1:T(8,128)(2,1)S(1)}, bf16[768,64]{0,1:T(8,128)(2,1)S(1)}, u32[]{:S(2)}, u32[]{:S(2)}) collective-permute-start(bf16[768,64]{0,1:T(8,128)(2,1)S(1)} %get-tuple-element.27), channel_id=1, source_target_pairs={{0,24},{4,28},{8,16},{12,20},{16,8},{20,12},{24,0},{28,4},{1,25},{... | collective-permute-start | bytes 294920 | tf_op jit(solution)/shard_map/ppermute | solution.py:198
  334.9 137.7 %collective-permute-start.20 = (f32[256,2048]{1,0:T(8,128)S(1)}, f32[256,2048]{1,0:T(8,128)}, u32[]{:S(2)}, u32[]{:S(2)}) collective-permute-start(f32[256,2048]{1,0:T(8,128)S(1)} %fusion.15), channel_id=1, source_target_pairs={{0,4},{4,0},{8,12},{12,8},{16,20},{20,16},{24,28},{28,24},{1,5},{5... | collective-permute-start | bytes 6291464 | tf_op jit(solution)/shard_map/ppermute | solution.py:182
  334.9 77.5 %collective-permute-start.14 = (bf16[768,2048]{1,0:T(8,128)(2,1)}, bf16[768,2048]{1,0:T(8,128)(2,1)}, u32[]{:S(2)}, u32[]{:S(2)}) collective-permute-start(bf16[768,2048]{1,0:T(8,128)(2,1)} %slice.66), channel_id=1, source_target_pairs={{0,24},{4,28},{24,0},{28,4},{1,25},{5,29},{25,1},{29,5},{2,26},{6,... | collective-permute-start | bytes 9437192 | tf_op jit(solution)/shard_map/ppermute | solution.py:198
  373.3 70.4 %collective-permute-start.12 = (bf16[768,1024]{1,0:T(8,128)(2,1)}, bf16[768,1024]{1,0:T(8,128)(2,1)}, u32[]{:S(2)}, u32[]{:S(2)}) collective-permute-start(bf16[768,1024]{1,0:T(8,128)(2,1)} %slice.63), channel_id=1, source_target_pairs={{0,24},{4,28},{24,0},{28,4},{1,25},{5,29},{25,1},{29,5},{2,26},{6,... | collective-permute-start | bytes 4718600 | tf_op jit(solution)/shard_map/ppermute | solution.py:198
  409.9 50.1 %collective-permute-start.11 = (bf16[768,512]{1,0:T(8,128)(2,1)}, bf16[768,512]{1,0:T(8,128)(2,1)S(1)}, u32[]{:S(2)}, u32[]{:S(2)}) collective-permute-start(bf16[768,512]{1,0:T(8,128)(2,1)} %slice.62), channel_id=1, source_target_pairs={{0,24},{4,28},{24,0},{28,4},{1,25},{5,29},{25,1},{29,5},{2,26},{6,... | collective-permute-start | bytes 2359304 | tf_op jit(solution)/shard_map/ppermute | solution.py:198
  462.7 6.2 %collective-permute-start.16 = (f32[3,4096]{1,0:T(4,128)S(1)}, f32[3,4096]{1,0:T(4,128)S(1)}, u32[]{:S(2)}, u32[]{:S(2)}) collective-permute-start(f32[3,4096]{1,0:T(4,128)S(1)} %reshape.102), channel_id=1, source_target_pairs={{0,24},{4,28},{8,16},{12,20},{16,8},{20,12},{24,0},{28,4},{1,25},{... | collective-permute-start | bytes 147464 | tf_op jit(solution)/shard_map/ppermute | solution.py:198
  469.0 7.0 %collective-permute-start.18 = (f32[3,4096]{1,0:T(4,128)S(1)}, f32[3,4096]{1,0:T(4,128)S(1)}, u32[]{:S(2)}, u32[]{:S(2)}) collective-permute-start(f32[3,4096]{1,0:T(4,128)S(1)} %add.178), channel_id=1, source_target_pairs={{0,2},{1,3},{2,0},{3,1},{4,6},{5,7},{6,4},{7,5},{8,10},{9,11},{10,... | collective-permute-start | bytes 147464 | tf_op jit(solution)/shard_map/ppermute | solution.py:182
  469.0 6.9 %collective-permute-start.19 = (f32[3,4096]{1,0:T(4,128)S(1)}, f32[3,4096]{1,0:T(4,128)S(1)}, u32[]{:S(2)}, u32[]{:S(2)}) collective-permute-start(f32[3,4096]{1,0:T(4,128)S(1)} %add.178), channel_id=1, source_target_pairs={{0,3},{1,2},{2,1},{3,0},{4,7},{5,6},{6,5},{7,4},{8,11},{9,10},{10,... | collective-permute-start | bytes 147464 | tf_op jit(solution)/shard_map/ppermute | solution.py:182
  472.4 4.3 collective-permute-start.17
  591.3 5.1 collective-permute-start.22
  592.1 5.8 collective-permute-start.23
  593.6 4.3 collective-permute-start.21
  598.6 14.2 %collective-permute-start.25 = (f32[24,256]{1,0:T(8,128)S(1)}, f32[24,256]{1,0:T(8,128)S(1)}, u32[]{:S(2)}, u32[]{:S(2)}) collective-permute-start(f32[24,256]{1,0:T(8,128)S(1)} %add_add_fusion.3), channel_id=1, source_target_pairs={{0,2},{1,3},{2,0},{3,1},{4,6},{5,7},{6,4},{7,5},{8,10},{9,11},{10,... | collective-permute-start | bytes 73736 | tf_op jit(solution)/shard_map/ppermute | solution.py:182
  598.9 14.0 %collective-permute-start.26 = (f32[24,256]{1,0:T(8,128)S(1)}, f32[24,256]{1,0:T(8,128)S(1)}, u32[]{:S(2)}, u32[]{:S(2)}) collective-permute-start(f32[24,256]{1,0:T(8,128)S(1)} %add_add_fusion.3), channel_id=1, source_target_pairs={{0,3},{1,2},{2,1},{3,0},{4,7},{5,6},{6,5},{7,4},{8,11},{9,10},{10,... | collective-permute-start | bytes 73736 | tf_op jit(solution)/shard_map/ppermute | solution.py:182
  600.9 12.0 %collective-permute-start.24 = (f32[24,256]{1,0:T(8,128)S(1)}, f32[24,256]{1,0:T(8,128)S(1)}, u32[]{:S(2)}, u32[]{:S(2)}) collective-permute-start(f32[24,256]{1,0:T(8,128)S(1)} %add_add_fusion.3), channel_id=1, source_target_pairs={{0,1},{1,0},{2,3},{3,2},{4,5},{5,4},{6,7},{7,6},{8,9},{9,8},{10,11... | collective-permute-start | bytes 73736 | tf_op jit(solution)/shard_map/ppermute | solution.py:182
  607.4 6.1 copy-start.1
Sparse Core Ops, SparseCore 0:
  9.8 125.0 all-gather.7
  137.1 27.8 all-gather.5
  213.9 113.9 all-gather.9

commit v9 on v8

--- a/solution.py
+++ b/solution.py
@@ -259,6 +259,7 @@
             jnp.concatenate([moved, whitened_rows], axis=0),
         )
         bit *= 2
+    whitened_rows = lax.optimization_barrier(whitened_rows)
     query_side = lax.dot_general(whitened_rows, inverse_factor, (((0,), (0,)), ((), ())), precision=lax.Precision.HIGH)
 
     own_idx = jnp.stack([f ^ k for k in order]).astype(jnp.int32)
@@ -279,7 +280,7 @@
     in_down = early[:, :half]
     out_down = early[:, half : 2 * half] * weight_of
     in_up = early[:, 2 * half :] * weight_of
-    in_up_far = mirror(in_up.astype(jnp.bfloat16)).astype(f32)
+    in_up_far = mirror(lax.dynamic_slice_in_dim(in_up.astype(jnp.bfloat16), s * part, part, 0))
 
     def pair(outs, ins):
         shape = (local_seqs, SEQ_LEN, half)
@@ -299,7 +300,10 @@
         grad_up = (grad[:, units] * (gate * jax.nn.sigmoid(gate))).astype(jnp.bfloat16)
         term = jnp.dot(grad_up, proj_hidden[units, half:], preferred_element_type=f32)
         far = term if far is None else far + term
-    up_far = pair(far, in_up_far)
+        if j == len(chunks) - 2:
+            far, in_up_far = lax.optimization_barrier((far, in_up_far))
+            in_up_far = lax.all_gather(in_up_far, "solve", axis=0, tiled=True)
+    up_far = pair(far, in_up_far.astype(f32))
     query_side = query_side + other_side
     high = lax.reduce_precision(query_side, 8, 7)
     query_side = (high.astype(jnp.bfloat16), (query_side - high).astype(jnp.bfloat16))

time: 621 us -> 616 us (level)
  blocking collectives: 111 us -> 102 us
  starting transfers between devices: 45.2 us -> 51.5 us
    all_gather x1, blocking collectives: 111 us -> 93.5 us  [local(): both = lax.all_gather(jnp.concatenate([up, down], axis=0), 'fsdp', axis=0)]
    all_gather x0 -> x1, blocking collectives: none -> 8.7 us  [local(): in_up_far = lax.all_gather(in_up_far, 'solve', axis=0, tiled=True)]
    ppermute x7, starting transfers between devices: 20.6 us -> 29.2 us  [mirror(): return lax.ppermute(x, 'fsdp', pairs)]
where the time goes in v9:
time: 616 us; the launch traced here: 615 us
  waiting for transfers between devices  303 us (49%)
  blocking collectives  102 us (17%)
  Pallas kernels  80.5 us (13%)
  starting transfers between devices  51.5 us (8%)
  matrix products  39 us (6%)
  between operations  14.2 us (2%)
  other arithmetic  12.5 us (2%)
  local copies, waits for them, and re-layouts  12.2 us (2%)
    all_gather x1, waiting for transfers between devices, local(): cot_full = lax.all_gather(cotangent, 'solve', axis=1, tiled=True)  122 us
    ppermute x20, waiting for transfers between devices, swap(): return lax.ppermute(x, axis, [(i, i ^ bit) for i in range(size)])  109 us
    all_gather x1, blocking collectives, local(): both = lax.all_gather(jnp.concatenate([up, down], axis=0), 'fsdp', axis=0)  93.5 us
    ppermute x7, waiting for transfers between devices, mirror(): return lax.ppermute(x, 'fsdp', pairs)  71.5 us
    pallas_call x1, Pallas kernels, tokens(): pl.pallas_call(functools.partial(tokens_kernel, count, len(gate_parts), s...  34.7 us
    pallas_call x1, Pallas kernels, gradient(): pl.pallas_call(functools.partial(grad_kernel, count), out_shape=jax.Shape...  31.4 us
    ppermute x7, starting transfers between devices, mirror(): return lax.ppermute(x, 'fsdp', pairs)  29.2 us
    ppermute x20, starting transfers between devices, swap(): return lax.ppermute(x, axis, [(i, i ^ bit) for i in range(size)])  22.2 us
  transfers between devices with their start and end apart: 30, of which 13 were waited for; matrix products, arithmetic and copies ran while one was open for 10% of the time, Pallas kernels for 12%

profile of v9, /device:TPU:0, one launch (start us, length us, event | category | flops | bytes accessed | tf_op | source)
XLA Modules:
  0.0 615.4 jit_solution(7395333311519683336)
XLA Ops:
  8.0 3.1 collective-permute-start.6
  11.1 1.6 convert_element_type.64
  12.8 122.2 %all-gather.9.cloned.1.call-done.refs_0_.refs_1_.refs_2_.refs_3_ = bf16[768,8192]{1,0:T(8,128)(2,1)} async-done(((bf16[768,2048]{1,0:T(8,128)(2,1)}), bf16[768,8192]{1,0:T(8,128)(2,1)}) %all-gather.9.cloned.1.call-update) | async-done | bytes 12582928 | tf_op jit(solution)/shard_map/all_gather | solution.py:210
  135.0 1.5 dynamic_slice.22
  136.5 3.4 collective-permute-start.4
  139.9 38.3 %collective-permute-done.6.refs_6_ = bf16[3584,1024]{1,0:T(8,128)(2,1)} collective-permute-done((bf16[3584,1024]{1,0:T(8,128)(2,1)}, bf16[3584,1024]{1,0:T(8,128)(2,1)}, u32[]{:S(2)}, u32[]{:S(2)}) %collective-permute-start.6) | collective-permute-done | bytes 7340064 | tf_op jit(solution)/shard_map/ppermute | solution.py:182
  178.2 35.6 %collective-permute-done.4 = bf16[192,4096]{1,0:T(8,128)(2,1)} collective-permute-done((bf16[192,4096]{1,0:T(8,128)(2,1)S(1)}, bf16[192,4096]{1,0:T(8,128)(2,1)}, u32[]{:S(2)}, u32[]{:S(2)}) %collective-permute-start.4) | collective-permute-done | bytes 1572896 | tf_op jit(solution)/shard_map/ppermute | solution.py:198
  213.9 3.1 fusion.20
  217.0 2.2 fusion.18
  219.2 7.5 %fusion.6 = f32[768,64]{0,1:T(8,128)S(1)} fusion(bf16[768,3584]{1,0:T(8,128)(2,1)} %param.14, bf16[768,3584]{1,0:T(8,128)(2,1)} %refs_8_.1, bf16[3584,128]{1,0:T(8,128)(2,1)S(1)} %copy-done.4), kind=kOutput, calls=%fused_computation.9 | convolution fusion | flops 374341632 | bytes 12124160 | tf_op jit(solution)/shard_map/dot_general | solution.py:233
  226.8 6.0 fusion.48
  235.0 2.2 collective-permute-start.10
  237.4 29.9 %collective-permute-done = f32[512,256]{1,0:T(8,128)} collective-permute-done((f32[512,256]{1,0:T(8,128)S(1)}, f32[512,256]{1,0:T(8,128)}, u32[]{:S(2)}, u32[]{:S(2)}) %collective-permute-start) | collective-permute-done | bytes 524320 | tf_op jit(solution)/shard_map/ppermute | solution.py:182
  268.4 1.5 collective-permute-start.1
  269.9 11.4 %collective-permute-done.1 = f32[256,256]{1,0:T(8,128)S(1)} collective-permute-done((f32[256,256]{1,0:T(8,128)S(1)}, f32[256,256]{1,0:T(8,128)S(1)}, u32[]{:S(2)}, u32[]{:S(2)}) %collective-permute-start.1) | collective-permute-done | bytes 262176 | tf_op jit(solution)/shard_map/ppermute | solution.py:182
  281.3 2.5 collective-permute-start.8
  284.4 2.1 slice.62
  286.5 2.7 slice.63
  289.2 4.0 slice.66
  294.5 3.0 collective-permute-start.13
  297.5 13.2 %collective-permute-done.8 = f32[768,192]{0,1:T(8,128)} collective-permute-done((f32[768,192]{0,1:T(8,128)S(1)}, f32[768,192]{0,1:T(8,128)}, u32[]{:S(2)}, u32[]{:S(2)}) %collective-permute-start.8) | collective-permute-done | bytes 589856 | tf_op jit(solution)/shard_map/ppermute | solution.py:182
  312.1 8.0 %collective-permute-done.2 = f32[256,256]{1,0:T(8,128)S(1)} collective-permute-done((f32[256,256]{1,0:T(8,128)S(1)}, f32[256,256]{1,0:T(8,128)S(1)}, u32[]{:S(2)}, u32[]{:S(2)}) %collective-permute-start.2) | collective-permute-done | bytes 262176 | tf_op jit(solution)/shard_map/ppermute | solution.py:182
  320.8 3.6 collective-permute-start.15
  324.3 5.1 collective-permute-done.3
  330.8 6.1 fusion.49
  337.0 7.9 %collective-permute-start.14 = (bf16[768,2048]{1,0:T(8,128)(2,1)}, bf16[768,2048]{1,0:T(8,128)(2,1)}, u32[]{:S(2)}, u32[]{:S(2)}) collective-permute-start(bf16[768,2048]{1,0:T(8,128)(2,1)} %slice.66), channel_id=1, source_target_pairs={{0,24},{4,28},{24,0},{28,4},{1,25},{5,29},{25,1},{29,5},{2,26},{6,... | collective-permute-start | bytes 9437192 | tf_op jit(solution)/shard_map/ppermute | solution.py:198
  344.9 34.7 %shard_map.130 = f32[768,128]{1,0:T(8,128)} custom-call(s32[4]{0:T(128)} %get-tuple-element.17.idx, bf16[768,8192]{1,0:T(8,128)(2,1)} %all-gather.9.cloned.1.call-done.refs_0_.refs_1_.refs_2_.refs_3_, bf16[768,8192]{1,0:T(8,128)(2,1)} %all-gather.9.cloned.1.call-done.refs_0_.refs_1_.refs_2_.refs_3_, ...), custom_call_target="tpu_custom_call" | custom-call | flops 23957864448 | bytes 46661632 | tf_op jit(solution)/shard_map/pallas_call | solution.py:64
  380.8 1.9 collective-permute-start.12
  382.7 31.4 %shard_map.131 = f32[768,3584]{1,0:T(8,128)} custom-call(s32[4]{0:T(128)} %get-tuple-element.31.idx, bf16[768,4096]{1,0:T(8,128)(2,1)} %all-gather.11.cloned.1.call-done.refs_0_.refs_1_.refs_2_.refs_3_, bf16[768,4096]{1,0:T(8,128)(2,1)} %all-gather.11.cloned.1.call-done.refs_0_.refs_1_.refs_2_.refs_3_, ...), custom_call_target="tpu_custom_call" | custom-call | flops 22548578304 | bytes 46661632 | tf_op jit(solution)/shard_map/pallas_call | solution.py:105
  414.2 5.7 collective-permute-start.11
  419.9 6.1 fusion.9
  426.0 21.8 %collective-permute-done.12 = bf16[768,1024]{1,0:T(8,128)(2,1)} collective-permute-done((bf16[768,1024]{1,0:T(8,128)(2,1)}, bf16[768,1024]{1,0:T(8,128)(2,1)}, u32[]{:S(2)}, u32[]{:S(2)}) %collective-permute-start.12) | collective-permute-done | bytes 1572896 | tf_op jit(solution)/shard_map/ppermute | solution.py:198
  447.8 4.1 fusion.13
  451.9 12.4 %collective-permute-done.11 = bf16[768,512]{1,0:T(8,128)(2,1)S(1)} collective-permute-done((bf16[768,512]{1,0:T(8,128)(2,1)}, bf16[768,512]{1,0:T(8,128)(2,1)S(1)}, u32[]{:S(2)}, u32[]{:S(2)}) %collective-permute-start.11) | collective-permute-done | bytes 786464 | tf_op jit(solution)/shard_map/ppermute | solution.py:198
  464.3 8.7 %all-gather.1 = bf16[4,192,64]{1,2,0:T(8,128)(2,1)S(1)} all-gather(bf16[1,192,64]{1,2,0:T(8,128)(2,1)S(1)} %bitcast.40), channel_id=1, replica_groups=mesh['fsdp'=8,'solve'=4] {'solve'}, dimensions={0}, use_global_device_ids=true | all-gather | bytes 122880 | tf_op jit(solution)/shard_map/all_gather | solution.py:305
  473.3 2.6 convolution_add_fusion
  476.2 3.6 collective-permute-start.16
  480.8 1.7 collective-permute-done.16
  482.8 1.5 collective-permute-start.19
  484.3 1.8 collective-permute-start.17
  486.1 3.4 fusion.11
  489.6 93.5 %all-gather.2.both = f32[8,6,4096]{2,1,0:T(8,128)} all-gather(f32[1,6,4096]{2,1,0:T(8,128)S(1)} %maximum_bitcast_fusion), channel_id=2, replica_groups=mesh['fsdp'=8,'solve'=4] {'fsdp'}, dimensions={0}, use_global_device_ids=true | all-gather | bytes 884736 | tf_op jit(solution)/shard_map/all_gather | solution.py:312
  583.1 3.6 shard_map.132
  588.1 2.1 collective-permute-start.21
  591.6 1.6 collective-permute-done.23
  595.3 1.5 collective-permute-start.26
  597.5 5.3 shard_map.133.refs_0_
  602.8 5.4 shard_map.134
  (82 shorter events, 19.1 us)
Async XLA Ops:
  7.2 209.9 %copy-start = (bf16[768,2048]{1,0:T(8,128)(2,1)S(1)}, bf16[768,2048]{1,0:T(8,128)(2,1)}, u32[]{:S(2)}) copy-start(bf16[768,2048]{1,0:T(8,128)(2,1)} %param.11) | copy-start | bytes 9437188
  7.2 127.8 %all-gather.9.cloned.1.call-start = ((), (), s32[]{:S(2)}) async-start(), calls=%async_computation.1 | async-start | bytes 15728640 | tf_op jit(solution)/shard_map/all_gather | solution.py:210
  7.9 218.8 %all-gather.7.cloned.1.call-start = ((), (), s32[]{:S(2)}) async-start(), calls=%async_computation | async-start | bytes 1179648 | tf_op jit(solution)/shard_map/all_gather | solution.py:241
  8.0 170.2 %collective-permute-start.6 = (bf16[3584,1024]{1,0:T(8,128)(2,1)}, bf16[3584,1024]{1,0:T(8,128)(2,1)}, u32[]{:S(2)}, u32[]{:S(2)}) collective-permute-start(bf16[3584,1024]{1,0:T(8,128)(2,1)} %refs_4_.3), channel_id=1, source_target_pairs={{0,8},{4,12},{8,0},{12,4},{16,24},{20,28},{24,16},{28,20},{1,9},{5... | collective-permute-start | bytes 22020104 | tf_op jit(solution)/shard_map/ppermute | solution.py:182
  12.7 370.0 %all-gather.11.cloned.1.call-start = ((), (), s32[]{:S(2)}) async-start(), calls=%async_computation.2 | async-start | bytes 7864320 | tf_op jit(solution)/shard_map/all_gather | solution.py:215
  136.5 77.3 %collective-permute-start.4 = (bf16[192,4096]{1,0:T(8,128)(2,1)S(1)}, bf16[192,4096]{1,0:T(8,128)(2,1)}, u32[]{:S(2)}, u32[]{:S(2)}) collective-permute-start(bf16[192,4096]{1,0:T(8,128)(2,1)S(1)} %dynamic_slice.22), channel_id=1, source_target_pairs={{0,24},{4,28},{8,16},{12,20},{16,8},{20,12},{24,0},{28,4},{1,25},{... | collective-permute-start | bytes 4718600 | tf_op jit(solution)/shard_map/ppermute | solution.py:198
  139.9 197.1 %collective-permute-start.5 = (bf16[3584,1024]{1,0:T(8,128)(2,1)}, bf16[3584,1024]{1,0:T(8,128)(2,1)}, u32[]{:S(2)}, u32[]{:S(2)}) collective-permute-start(bf16[3584,1024]{1,0:T(8,128)(2,1)} %refs_4_.3), channel_id=1, source_target_pairs={{0,4},{4,0},{8,12},{12,8},{16,20},{20,16},{24,28},{28,24},{1,5},{5... | collective-permute-start | bytes 22020104 | tf_op jit(solution)/shard_map/ppermute | solution.py:182
  178.2 166.7 %collective-permute-start.7 = (bf16[3584,1024]{1,0:T(8,128)(2,1)}, bf16[3584,1024]{1,0:T(8,128)(2,1)}, u32[]{:S(2)}, u32[]{:S(2)}) collective-permute-start(bf16[3584,1024]{1,0:T(8,128)(2,1)} %collective-permute-done.6.refs_6_), channel_id=1, source_target_pairs={{0,4},{4,0},{8,12},{12,8},{16,20},{20,16},{24,28},{28,24},{1,5},{5... | collective-permute-start | bytes 22020104 | tf_op jit(solution)/shard_map/ppermute | solution.py:182
  213.9 5.4 copy-start.4
  226.7 10.6 %copy-start.3 = (s32[3]{0:T(128)S(1)}, s32[3]{0:T(128)}, u32[]{:S(2)}) copy-start(s32[3]{0:T(128)} %param.18) | copy-start | bytes 40
  232.8 34.5 %collective-permute-start = (f32[512,256]{1,0:T(8,128)S(1)}, f32[512,256]{1,0:T(8,128)}, u32[]{:S(2)}, u32[]{:S(2)}) collective-permute-start(f32[512,256]{1,0:T(8,128)S(1)} %constant_dynamic-slice_fusion.1), channel_id=1, source_target_pairs={{0,2},{1,3},{2,0},{3,1},{4,6},{5,7},{6,4},{7,5},{8,10},{9,11},{10,... | collective-permute-start | bytes 1572872 | tf_op jit(solution)/shard_map/ppermute | solution.py:182
  234.2 60.2 %collective-permute-start.9 = (f32[768,192]{0,1:T(8,128)S(1)}, f32[768,192]{0,1:T(8,128)S(1)}, u32[]{:S(2)}, u32[]{:S(2)}) collective-permute-start(f32[768,192]{0,1:T(8,128)S(1)} %pad_maximum_fusion), channel_id=1, source_target_pairs={{0,2},{1,3},{2,0},{3,1},{4,6},{5,7},{6,4},{7,5},{8,10},{9,11},{10,... | collective-permute-start | bytes 1769480 | tf_op jit(solution)/shard_map/ppermute | solution.py:182
  235.0 62.5 %collective-permute-start.10 = (f32[768,192]{0,1:T(8,128)S(1)}, f32[768,192]{0,1:T(8,128)}, u32[]{:S(2)}, u32[]{:S(2)}) collective-permute-start(f32[768,192]{0,1:T(8,128)S(1)} %pad_maximum_fusion), channel_id=1, source_target_pairs={{0,3},{1,2},{2,1},{3,0},{4,7},{5,6},{6,5},{7,4},{8,11},{9,10},{10,... | collective-permute-start | bytes 1769480 | tf_op jit(solution)/shard_map/ppermute | solution.py:182
  268.4 12.9 %collective-permute-start.1 = (f32[256,256]{1,0:T(8,128)S(1)}, f32[256,256]{1,0:T(8,128)S(1)}, u32[]{:S(2)}, u32[]{:S(2)}) collective-permute-start(f32[256,256]{1,0:T(8,128)S(1)} %constant_dynamic-slice_fusion), channel_id=1, source_target_pairs={{0,1},{1,0},{2,3},{3,2},{4,5},{5,4},{6,7},{7,6},{8,9},{9,8},{10,11... | collective-permute-start | bytes 786440 | tf_op jit(solution)/shard_map/ppermute | solution.py:182
  281.3 29.4 %collective-permute-start.8 = (f32[768,192]{0,1:T(8,128)S(1)}, f32[768,192]{0,1:T(8,128)}, u32[]{:S(2)}, u32[]{:S(2)}) collective-permute-start(f32[768,192]{0,1:T(8,128)S(1)} %pad_maximum_fusion), channel_id=1, source_target_pairs={{0,1},{1,0},{2,3},{3,2},{4,5},{5,4},{6,7},{7,6},{8,9},{9,8},{10,11... | collective-permute-start | bytes 1769480 | tf_op jit(solution)/shard_map/ppermute | solution.py:182
  294.4 35.0 %copy-start.2 = (f32[256,256]{1,0:T(8,128)}, f32[256,256]{1,0:T(8,128)S(1)}, u32[]{:S(2)}) copy-start(f32[256,256]{1,0:T(8,128)S(1)} %dynamic-slice_add_fusion.1) | copy-start | bytes 786436
  294.5 119.7 %collective-permute-start.13 = (bf16[768,3584]{1,0:T(8,128)(2,1)}, bf16[768,3584]{1,0:T(8,128)(2,1)}, u32[]{:S(2)}, u32[]{:S(2)}) collective-permute-start(bf16[768,3584]{1,0:T(8,128)(2,1)} %refs_8_.1), channel_id=1, source_target_pairs={{8,16},{12,20},{16,8},{20,12},{9,17},{13,21},{17,9},{21,13},{10,18... | collective-permute-start | bytes 16515080 | tf_op jit(solution)/shard_map/ppermute | solution.py:198
  297.5 22.6 %collective-permute-start.2 = (f32[256,256]{1,0:T(8,128)S(1)}, f32[256,256]{1,0:T(8,128)S(1)}, u32[]{:S(2)}, u32[]{:S(2)}) collective-permute-start(f32[256,256]{1,0:T(8,128)S(1)} %dynamic-slice_add_fusion.1), channel_id=1, source_target_pairs={{0,1},{1,0},{2,3},{3,2},{4,5},{5,4},{6,7},{7,6},{8,9},{9,8},{10,11... | collective-permute-start | bytes 786440 | tf_op jit(solution)/shard_map/ppermute | solution.py:182
  320.1 9.4 %collective-permute-start.3 = (f32[512,256]{1,0:T(8,128)S(1)}, f32[512,256]{1,0:T(8,128)}, u32[]{:S(2)}, u32[]{:S(2)}) collective-permute-start(f32[512,256]{1,0:T(8,128)S(1)} %maximum_select_fusion.1), channel_id=1, source_target_pairs={{0,2},{1,3},{2,0},{3,1},{4,6},{5,7},{6,4},{7,5},{8,10},{9,11},{10,... | collective-permute-start | bytes 1572872 | tf_op jit(solution)/shard_map/ppermute | solution.py:182
  320.8 131.1 %collective-permute-start.15 = (bf16[192,64]{0,1:T(8,128)(2,1)S(1)}, bf16[192,64]{0,1:T(8,128)(2,1)S(1)}, u32[]{:S(2)}, u32[]{:S(2)}) collective-permute-start(bf16[192,64]{0,1:T(8,128)(2,1)S(1)} %dynamic-slice_convert_fusion), channel_id=1, source_target_pairs={{0,24},{4,28},{8,16},{12,20},{16,8},{20,12},{24,0},{28,4},{1,25},{... | collective-permute-start | bytes 73736 | tf_op jit(solution)/shard_map/ppermute | solution.py:198
  336.9 149.2 %collective-permute-start.20 = (f32[256,2048]{1,0:T(8,128)S(1)}, f32[256,2048]{1,0:T(8,128)}, u32[]{:S(2)}, u32[]{:S(2)}) collective-permute-start(f32[256,2048]{1,0:T(8,128)S(1)} %fusion.49), channel_id=1, source_target_pairs={{0,4},{4,0},{8,12},{12,8},{16,20},{20,16},{24,28},{28,24},{1,5},{5... | collective-permute-start | bytes 6291464 | tf_op jit(solution)/shard_map/ppermute | solution.py:182
  337.0 82.9 %collective-permute-start.14 = (bf16[768,2048]{1,0:T(8,128)(2,1)}, bf16[768,2048]{1,0:T(8,128)(2,1)}, u32[]{:S(2)}, u32[]{:S(2)}) collective-permute-start(bf16[768,2048]{1,0:T(8,128)(2,1)} %slice.66), channel_id=1, source_target_pairs={{0,24},{4,28},{24,0},{28,4},{1,25},{5,29},{25,1},{29,5},{2,26},{6,... | collective-permute-start | bytes 9437192 | tf_op jit(solution)/shard_map/ppermute | solution.py:198
  380.8 67.0 %collective-permute-start.12 = (bf16[768,1024]{1,0:T(8,128)(2,1)}, bf16[768,1024]{1,0:T(8,128)(2,1)}, u32[]{:S(2)}, u32[]{:S(2)}) collective-permute-start(bf16[768,1024]{1,0:T(8,128)(2,1)} %slice.63), channel_id=1, source_target_pairs={{0,24},{4,28},{24,0},{28,4},{1,25},{5,29},{25,1},{29,5},{2,26},{6,... | collective-permute-start | bytes 4718600 | tf_op jit(solution)/shard_map/ppermute | solution.py:198
  414.2 50.2 %collective-permute-start.11 = (bf16[768,512]{1,0:T(8,128)(2,1)}, bf16[768,512]{1,0:T(8,128)(2,1)S(1)}, u32[]{:S(2)}, u32[]{:S(2)}) collective-permute-start(bf16[768,512]{1,0:T(8,128)(2,1)} %slice.62), channel_id=1, source_target_pairs={{0,24},{4,28},{24,0},{28,4},{1,25},{5,29},{25,1},{29,5},{2,26},{6,... | collective-permute-start | bytes 2359304 | tf_op jit(solution)/shard_map/ppermute | solution.py:198
  464.3 8.7 %copy-start.5 = (bf16[768,512]{1,0:T(8,128)(2,1)}, bf16[768,512]{1,0:T(8,128)(2,1)S(1)}, u32[]{:S(2)}) copy-start(bf16[768,512]{1,0:T(8,128)(2,1)S(1)} %collective-permute-done.11) | copy-start | bytes 2359300
  476.2 6.2 %collective-permute-start.16 = (f32[3,4096]{1,0:T(4,128)S(1)}, f32[3,4096]{1,0:T(4,128)S(1)}, u32[]{:S(2)}, u32[]{:S(2)}) collective-permute-start(f32[3,4096]{1,0:T(4,128)S(1)} %reshape.102), channel_id=1, source_target_pairs={{0,24},{4,28},{8,16},{12,20},{16,8},{20,12},{24,0},{28,4},{1,25},{... | collective-permute-start | bytes 147464 | tf_op jit(solution)/shard_map/ppermute | solution.py:198
  482.5 7.0 %collective-permute-start.18 = (f32[3,4096]{1,0:T(4,128)S(1)}, f32[3,4096]{1,0:T(4,128)S(1)}, u32[]{:S(2)}, u32[]{:S(2)}) collective-permute-start(f32[3,4096]{1,0:T(4,128)S(1)} %add.179), channel_id=1, source_target_pairs={{0,2},{1,3},{2,0},{3,1},{4,6},{5,7},{6,4},{7,5},{8,10},{9,11},{10,... | collective-permute-start | bytes 147464 | tf_op jit(solution)/shard_map/ppermute | solution.py:182
  482.8 6.7 %collective-permute-start.19 = (f32[3,4096]{1,0:T(4,128)S(1)}, f32[3,4096]{1,0:T(4,128)S(1)}, u32[]{:S(2)}, u32[]{:S(2)}) collective-permute-start(f32[3,4096]{1,0:T(4,128)S(1)} %add.179), channel_id=1, source_target_pairs={{0,3},{1,2},{2,1},{3,0},{4,7},{5,6},{6,5},{7,4},{8,11},{9,10},{10,... | collective-permute-start | bytes 147464 | tf_op jit(solution)/shard_map/ppermute | solution.py:182
  484.3 5.2 collective-permute-start.17
  586.7 4.9 collective-permute-start.22
  587.4 5.8 collective-permute-start.23
  588.1 5.2 collective-permute-start.21
  594.0 14.2 %collective-permute-start.25 = (f32[24,256]{1,0:T(8,128)S(1)}, f32[24,256]{1,0:T(8,128)S(1)}, u32[]{:S(2)}, u32[]{:S(2)}) collective-permute-start(f32[24,256]{1,0:T(8,128)S(1)} %add_add_fusion.3), channel_id=1, source_target_pairs={{0,2},{1,3},{2,0},{3,1},{4,6},{5,7},{6,4},{7,5},{8,10},{9,11},{10,... | collective-permute-start | bytes 73736 | tf_op jit(solution)/shard_map/ppermute | solution.py:182
  595.3 13.0 %collective-permute-start.26 = (f32[24,256]{1,0:T(8,128)S(1)}, f32[24,256]{1,0:T(8,128)S(1)}, u32[]{:S(2)}, u32[]{:S(2)}) collective-permute-start(f32[24,256]{1,0:T(8,128)S(1)} %add_add_fusion.3), channel_id=1, source_target_pairs={{0,3},{1,2},{2,1},{3,0},{4,7},{5,6},{6,5},{7,4},{8,11},{9,10},{10,... | collective-permute-start | bytes 73736 | tf_op jit(solution)/shard_map/ppermute | solution.py:182
  596.7 11.6 %collective-permute-start.24 = (f32[24,256]{1,0:T(8,128)S(1)}, f32[24,256]{1,0:T(8,128)S(1)}, u32[]{:S(2)}, u32[]{:S(2)}) collective-permute-start(f32[24,256]{1,0:T(8,128)S(1)} %add_add_fusion.3), channel_id=1, source_target_pairs={{0,1},{1,0},{2,3},{3,2},{4,5},{5,4},{6,7},{7,6},{8,9},{9,8},{10,11... | collective-permute-start | bytes 73736 | tf_op jit(solution)/shard_map/ppermute | solution.py:182
  602.8 6.1 copy-start.1
Sparse Core Ops, SparseCore 0:
  9.8 125.0 all-gather.8
  137.1 27.8 all-gather.6
  213.9 113.4 all-gather.10

commit v10 on v9

--- a/solution.py
+++ b/solution.py
@@ -288,8 +288,10 @@
         return feat.reshape(local_seqs, half * half)
 
     down = pair(out_down, in_down)
-    up_own = pair(own[:, half:], in_up)
-
+    up_own = total(pair(own[:, half:], in_up), "solve", m)
+
+    own, in_up_far = lax.optimization_barrier((own, in_up_far))
+    in_up_far = lax.all_gather(in_up_far, "solve", axis=0, tiled=True)
     grad = gradient(far_idx, cot_far, weights)
     far = None
     for j, a, b, gate_outer in chunks:
@@ -300,15 +302,21 @@
         grad_up = (grad[:, units] * (gate * jax.nn.sigmoid(gate))).astype(jnp.bfloat16)
         term = jnp.dot(grad_up, proj_hidden[units, half:], preferred_element_type=f32)
         far = term if far is None else far + term
-        if j == len(chunks) - 2:
-            far, in_up_far = lax.optimization_barrier((far, in_up_far))
-            in_up_far = lax.all_gather(in_up_far, "solve", axis=0, tiled=True)
     up_far = pair(far, in_up_far.astype(f32))
     query_side = query_side + other_side
     high = lax.reduce_precision(query_side, 8, 7)
     query_side = (high.astype(jnp.bfloat16), (query_side - high).astype(jnp.bfloat16))
-    up = up_own + mirror(up_far)
-    up = total(up, "solve", m)
+    moved = [
+        lax.ppermute(
+            up_far,
+            ("fsdp", "solve"),
+            [(i * m + j, mirror_of[i] * m + (j ^ k)) for i in range(n) for j in range(m)],
+        )
+        for k in range(min(m, 4))
+    ]
+    while len(moved) > 1:
+        moved = [one + two for one, two in zip(moved[::2], moved[1::2])]
+    up = up_own + total(moved[0], "solve", m, 4)
     both = lax.all_gather(jnp.concatenate([up, down], axis=0), "fsdp", axis=0)
 
     examples = n * local_seqs

time: 616 us -> 658 us (1.068)
  blocking collectives: 102 us -> 149 us
  waiting for transfers between devices: 303 us -> 293 us
    all_gather x1, blocking collectives: 93.5 us -> 141 us  [local(): both = lax.all_gather(jnp.concatenate([up, down], axis=0), 'fsdp', axis=0)]
    ppermute x7 -> x6, waiting for transfers between devices: 71.5 us -> 56.7 us  [mirror(): return lax.ppermute(x, 'fsdp', pairs)]
    ppermute x0 -> x4, starting transfers between devices: none -> 9.51 us  [local(): lax.ppermute(up_far, ('fsdp', 'solve'), [(i * m + j, mirror_of[i] * m + (...]
    ppermute x7 -> x6, starting transfers between devices: 29.2 us -> 23.8 us  [mirror(): return lax.ppermute(x, 'fsdp', pairs)]
  transfers between devices with their start and end apart: 30 -> 33, of which waited for: 13 -> 12; matrix products, arithmetic and copies ran while one was open for 10% -> 9% of each run, Pallas kernels for 12% -> 12%
where the time goes in v10:
time: 658 us; the launch traced here: 657 us
  waiting for transfers between devices  293 us (45%)
  blocking collectives  149 us (23%)
  Pallas kernels  80.6 us (12%)
  starting transfers between devices  57.1 us (9%)
  matrix products  38.8 us (6%)
  between operations  14.2 us (2%)
  other arithmetic  12.5 us (2%)
  local copies, waits for them, and re-layouts  12.2 us (2%)
    all_gather x1, blocking collectives, local(): both = lax.all_gather(jnp.concatenate([up, down], axis=0), 'fsdp', axis=0)  141 us
    all_gather x1, waiting for transfers between devices, local(): cot_full = lax.all_gather(cotangent, 'solve', axis=1, tiled=True)  122 us
    ppermute x20, waiting for transfers between devices, swap(): return lax.ppermute(x, axis, [(i, i ^ bit) for i in range(size)])  110 us
    ppermute x6, waiting for transfers between devices, mirror(): return lax.ppermute(x, 'fsdp', pairs)  56.7 us
    pallas_call x1, Pallas kernels, tokens(): pl.pallas_call(functools.partial(tokens_kernel, count, len(gate_parts), s...  34.7 us
    pallas_call x1, Pallas kernels, gradient(): pl.pallas_call(functools.partial(grad_kernel, count), out_shape=jax.Shape...  31.5 us
    ppermute x6, starting transfers between devices, mirror(): return lax.ppermute(x, 'fsdp', pairs)  23.8 us
    ppermute x20, starting transfers between devices, swap(): return lax.ppermute(x, axis, [(i, i ^ bit) for i in range(size)])  23.6 us
  transfers between devices with their start and end apart: 33, of which 12 were waited for; matrix products, arithmetic and copies ran while one was open for 9% of the time, Pallas kernels for 12%

profile of v10, /device:TPU:0, one launch (start us, length us, event | category | flops | bytes accessed | tf_op | source)
XLA Modules:
  0.0 656.8 jit_solution(911846916419700898)
XLA Ops:
  8.0 3.1 collective-permute-start.6
  11.1 1.6 convert_element_type.64
  12.8 122.2 %all-gather.9.cloned.1.call-done.refs_0_.refs_1_.refs_2_.refs_3_ = bf16[768,8192]{1,0:T(8,128)(2,1)} async-done(((bf16[768,2048]{1,0:T(8,128)(2,1)}), bf16[768,8192]{1,0:T(8,128)(2,1)}) %all-gather.9.cloned.1.call-update) | async-done | bytes 12582928 | tf_op jit(solution)/shard_map/all_gather | solution.py:210
  135.0 1.5 dynamic_slice.22
  136.5 3.4 collective-permute-start.4
  139.9 38.3 %collective-permute-done.6.refs_6_ = bf16[3584,1024]{1,0:T(8,128)(2,1)} collective-permute-done((bf16[3584,1024]{1,0:T(8,128)(2,1)}, bf16[3584,1024]{1,0:T(8,128)(2,1)}, u32[]{:S(2)}, u32[]{:S(2)}) %collective-permute-start.6) | collective-permute-done | bytes 7340064 | tf_op jit(solution)/shard_map/ppermute | solution.py:182
  178.2 35.6 %collective-permute-done.4 = bf16[192,4096]{1,0:T(8,128)(2,1)} collective-permute-done((bf16[192,4096]{1,0:T(8,128)(2,1)S(1)}, bf16[192,4096]{1,0:T(8,128)(2,1)}, u32[]{:S(2)}, u32[]{:S(2)}) %collective-permute-start.4) | collective-permute-done | bytes 1572896 | tf_op jit(solution)/shard_map/ppermute | solution.py:198
  213.9 3.1 fusion.20
  217.0 2.2 fusion.18
  219.2 7.5 %fusion.6 = f32[768,64]{0,1:T(8,128)S(1)} fusion(bf16[768,3584]{1,0:T(8,128)(2,1)} %param.14, bf16[768,3584]{1,0:T(8,128)(2,1)} %refs_8_.1, bf16[3584,128]{1,0:T(8,128)(2,1)S(1)} %copy-done.5), kind=kOutput, calls=%fused_computation.9 | convolution fusion | flops 374341632 | bytes 12124160 | tf_op jit(solution)/shard_map/dot_general | solution.py:233
  226.8 6.0 fusion.48
  234.2 1.5 collective-permute-start.10
  236.6 29.9 %collective-permute-done = f32[512,256]{1,0:T(8,128)} collective-permute-done((f32[512,256]{1,0:T(8,128)S(1)}, f32[512,256]{1,0:T(8,128)}, u32[]{:S(2)}, u32[]{:S(2)}) %collective-permute-start) | collective-permute-done | bytes 524320 | tf_op jit(solution)/shard_map/ppermute | solution.py:182
  267.6 1.5 collective-permute-start.1
  269.1 11.1 %collective-permute-done.1 = f32[256,256]{1,0:T(8,128)S(1)} collective-permute-done((f32[256,256]{1,0:T(8,128)S(1)}, f32[256,256]{1,0:T(8,128)S(1)}, u32[]{:S(2)}, u32[]{:S(2)}) %collective-permute-start.1) | collective-permute-done | bytes 262176 | tf_op jit(solution)/shard_map/ppermute | solution.py:182
  280.8 4.0 slice.66
  284.8 2.7 slice.63
  287.5 2.1 slice.62
  290.9 3.0 collective-permute-start.16
  294.0 2.3 collective-permute-start.2
  296.2 11.5 %collective-permute-done.9 = f32[768,192]{0,1:T(8,128)} collective-permute-done((f32[768,192]{0,1:T(8,128)S(1)}, f32[768,192]{0,1:T(8,128)}, u32[]{:S(2)}, u32[]{:S(2)}) %collective-permute-start.9) | collective-permute-done | bytes 589856 | tf_op jit(solution)/shard_map/ppermute | solution.py:182
  309.9 4.4 collective-permute-start.18
  314.7 14.7 %collective-permute-done.3 = f32[512,256]{1,0:T(8,128)} collective-permute-done((f32[512,256]{1,0:T(8,128)S(1)}, f32[512,256]{1,0:T(8,128)}, u32[]{:S(2)}, u32[]{:S(2)}) %collective-permute-start.3) | collective-permute-done | bytes 524320 | tf_op jit(solution)/shard_map/ppermute | solution.py:182
  330.8 6.1 fusion.49
  337.0 5.4 collective-permute-start.17
  342.4 34.7 %shard_map.130 = f32[768,128]{1,0:T(8,128)} custom-call(s32[4]{0:T(128)} %get-tuple-element.16.idx, bf16[768,8192]{1,0:T(8,128)(2,1)} %all-gather.9.cloned.1.call-done.refs_0_.refs_1_.refs_2_.refs_3_, bf16[768,8192]{1,0:T(8,128)(2,1)} %all-gather.9.cloned.1.call-done.refs_0_.refs_1_.refs_2_.refs_3_, ...), custom_call_target="tpu_custom_call" | custom-call | flops 23957864448 | bytes 46661632 | tf_op jit(solution)/shard_map/pallas_call | solution.py:64
  379.1 1.5 collective-permute-start.11
  380.7 7.5 %all-gather.1 = bf16[4,192,64]{1,2,0:T(8,128)(2,1)S(1)} all-gather(bf16[1,192,64]{1,2,0:T(8,128)(2,1)S(1)} %bitcast.40), channel_id=1, replica_groups=mesh['fsdp'=8,'solve'=4] {'solve'}, dimensions={0}, use_global_device_ids=true | all-gather | bytes 122880 | tf_op jit(solution)/shard_map/all_gather | solution.py:294
  388.5 2.4 collective-permute-start.15
  390.9 31.5 %shard_map.131 = f32[768,3584]{1,0:T(8,128)} custom-call(s32[4]{0:T(128)} %get-tuple-element.29.idx, bf16[768,4096]{1,0:T(8,128)(2,1)} %all-gather.11.cloned.1.call-done.refs_0_.refs_1_.refs_2_.refs_3_, bf16[768,4096]{1,0:T(8,128)(2,1)} %all-gather.11.cloned.1.call-done.refs_0_.refs_1_.refs_2_.refs_3_, ...), custom_call_target="tpu_custom_call" | custom-call | flops 22548578304 | bytes 46661632 | tf_op jit(solution)/shard_map/pallas_call | solution.py:105
  422.4 1.5 collective-permute-start.12
  424.0 5.2 collective-permute-start.14
  429.2 6.1 fusion.9
  435.3 10.4 %collective-permute-done.15 = bf16[768,1024]{1,0:T(8,128)(2,1)} collective-permute-done((bf16[768,1024]{1,0:T(8,128)(2,1)}, bf16[768,1024]{1,0:T(8,128)(2,1)}, u32[]{:S(2)}, u32[]{:S(2)}) %collective-permute-start.15) | collective-permute-done | bytes 1572896 | tf_op jit(solution)/shard_map/ppermute | solution.py:198
  447.2 4.1 fusion.13
  451.3 10.7 %collective-permute-done.14 = bf16[768,512]{1,0:T(8,128)(2,1)S(1)} collective-permute-done((bf16[768,512]{1,0:T(8,128)(2,1)S(1)}, bf16[768,512]{1,0:T(8,128)(2,1)S(1)}, u32[]{:S(2)}, u32[]{:S(2)}) %collective-permute-start.14) | collective-permute-done | bytes 786464 | tf_op jit(solution)/shard_map/ppermute | solution.py:198
  462.0 2.4 convolution_add_fusion
  464.7 3.4 collective-permute-start.19
  469.5 3.3 collective-permute-start.21
  474.2 3.4 fusion.11
  477.7 3.1 collective-permute-done.22
  480.9 141.3 %all-gather.2.both = f32[8,6,4096]{2,1,0:T(8,128)} all-gather(f32[1,6,4096]{2,1,0:T(8,128)S(1)} %maximum_bitcast_fusion), channel_id=2, replica_groups=mesh['fsdp'=8,'solve'=4] {'fsdp'}, dimensions={0}, use_global_device_ids=true | all-gather | bytes 884736 | tf_op jit(solution)/shard_map/all_gather | solution.py:320
  622.2 3.6 shard_map.132
  626.3 2.5 collective-permute-start.25
  631.6 3.1 collective-permute-done.26
  635.7 1.7 collective-permute-start.28
  638.9 5.3 shard_map.133.refs_0_
  644.2 5.4 shard_map.134
  (87 shorter events, 23.6 us)
Async XLA Ops:
  7.2 209.9 %copy-start = (bf16[768,2048]{1,0:T(8,128)(2,1)S(1)}, bf16[768,2048]{1,0:T(8,128)(2,1)}, u32[]{:S(2)}) copy-start(bf16[768,2048]{1,0:T(8,128)(2,1)} %param.11) | copy-start | bytes 9437188
  7.2 127.8 %all-gather.9.cloned.1.call-start = ((), (), s32[]{:S(2)}) async-start(), calls=%async_computation.1 | async-start | bytes 15728640 | tf_op jit(solution)/shard_map/all_gather | solution.py:210
  7.9 218.8 %all-gather.7.cloned.1.call-start = ((), (), s32[]{:S(2)}) async-start(), calls=%async_computation | async-start | bytes 1179648 | tf_op jit(solution)/shard_map/all_gather | solution.py:241
  8.0 170.2 %collective-permute-start.6 = (bf16[3584,1024]{1,0:T(8,128)(2,1)}, bf16[3584,1024]{1,0:T(8,128)(2,1)}, u32[]{:S(2)}, u32[]{:S(2)}) collective-permute-start(bf16[3584,1024]{1,0:T(8,128)(2,1)} %refs_4_.3), channel_id=1, source_target_pairs={{0,8},{4,12},{8,0},{12,4},{16,24},{20,28},{24,16},{28,20},{1,9},{5... | collective-permute-start | bytes 22020104 | tf_op jit(solution)/shard_map/ppermute | solution.py:182
  12.7 378.2 %all-gather.11.cloned.1.call-start = ((), (), s32[]{:S(2)}) async-start(), calls=%async_computation.2 | async-start | bytes 7864320 | tf_op jit(solution)/shard_map/all_gather | solution.py:215
  136.5 77.3 %collective-permute-start.4 = (bf16[192,4096]{1,0:T(8,128)(2,1)S(1)}, bf16[192,4096]{1,0:T(8,128)(2,1)}, u32[]{:S(2)}, u32[]{:S(2)}) collective-permute-start(bf16[192,4096]{1,0:T(8,128)(2,1)S(1)} %dynamic_slice.22), channel_id=1, source_target_pairs={{0,24},{4,28},{8,16},{12,20},{16,8},{20,12},{24,0},{28,4},{1,25},{... | collective-permute-start | bytes 4718600 | tf_op jit(solution)/shard_map/ppermute | solution.py:198
  139.9 197.1 %collective-permute-start.5 = (bf16[3584,1024]{1,0:T(8,128)(2,1)}, bf16[3584,1024]{1,0:T(8,128)(2,1)}, u32[]{:S(2)}, u32[]{:S(2)}) collective-permute-start(bf16[3584,1024]{1,0:T(8,128)(2,1)} %refs_4_.3), channel_id=1, source_target_pairs={{0,4},{4,0},{8,12},{12,8},{16,20},{20,16},{24,28},{28,24},{1,5},{5... | collective-permute-start | bytes 22020104 | tf_op jit(solution)/shard_map/ppermute | solution.py:182
  178.2 164.2 %collective-permute-start.7 = (bf16[3584,1024]{1,0:T(8,128)(2,1)}, bf16[3584,1024]{1,0:T(8,128)(2,1)}, u32[]{:S(2)}, u32[]{:S(2)}) collective-permute-start(bf16[3584,1024]{1,0:T(8,128)(2,1)} %collective-permute-done.6.refs_6_), channel_id=1, source_target_pairs={{0,4},{4,0},{8,12},{12,8},{16,20},{20,16},{24,28},{28,24},{1,5},{5... | collective-permute-start | bytes 22020104 | tf_op jit(solution)/shard_map/ppermute | solution.py:182
  213.9 5.4 copy-start.5
  226.7 9.8 %copy-start.4 = (s32[3]{0:T(128)S(1)}, s32[3]{0:T(128)}, u32[]{:S(2)}) copy-start(s32[3]{0:T(128)} %param.18) | copy-start | bytes 40
  232.8 33.6 %collective-permute-start = (f32[512,256]{1,0:T(8,128)S(1)}, f32[512,256]{1,0:T(8,128)}, u32[]{:S(2)}, u32[]{:S(2)}) collective-permute-start(f32[512,256]{1,0:T(8,128)S(1)} %constant_dynamic-slice_fusion.1), channel_id=1, source_target_pairs={{0,2},{1,3},{2,0},{3,1},{4,6},{5,7},{6,4},{7,5},{8,10},{9,11},{10,... | collective-permute-start | bytes 1572872 | tf_op jit(solution)/shard_map/ppermute | solution.py:182
  234.2 56.7 %collective-permute-start.10 = (f32[768,192]{0,1:T(8,128)S(1)}, f32[768,192]{0,1:T(8,128)S(1)}, u32[]{:S(2)}, u32[]{:S(2)}) collective-permute-start(f32[768,192]{0,1:T(8,128)S(1)} %pad_maximum_fusion), channel_id=1, source_target_pairs={{0,3},{1,2},{2,1},{3,0},{4,7},{5,6},{6,5},{7,4},{8,11},{9,10},{10,... | collective-permute-start | bytes 1769480 | tf_op jit(solution)/shard_map/ppermute | solution.py:182
  235.7 58.2 %collective-permute-start.8 = (f32[768,192]{0,1:T(8,128)S(1)}, f32[768,192]{0,1:T(8,128)}, u32[]{:S(2)}, u32[]{:S(2)}) collective-permute-start(f32[768,192]{0,1:T(8,128)S(1)} %pad_maximum_fusion), channel_id=1, source_target_pairs={{0,1},{1,0},{2,3},{3,2},{4,5},{5,4},{6,7},{7,6},{8,9},{9,8},{10,11... | collective-permute-start | bytes 1769480 | tf_op jit(solution)/shard_map/ppermute | solution.py:182
  267.6 12.6 %collective-permute-start.1 = (f32[256,256]{1,0:T(8,128)S(1)}, f32[256,256]{1,0:T(8,128)S(1)}, u32[]{:S(2)}, u32[]{:S(2)}) collective-permute-start(f32[256,256]{1,0:T(8,128)S(1)} %constant_dynamic-slice_fusion), channel_id=1, source_target_pairs={{0,1},{1,0},{2,3},{3,2},{4,5},{5,4},{6,7},{7,6},{8,9},{9,8},{10,11... | collective-permute-start | bytes 786440 | tf_op jit(solution)/shard_map/ppermute | solution.py:182
  280.2 27.5 %collective-permute-start.9 = (f32[768,192]{0,1:T(8,128)S(1)}, f32[768,192]{0,1:T(8,128)}, u32[]{:S(2)}, u32[]{:S(2)}) collective-permute-start(f32[768,192]{0,1:T(8,128)S(1)} %pad_maximum_fusion), channel_id=1, source_target_pairs={{0,2},{1,3},{2,0},{3,1},{4,6},{5,7},{6,4},{7,5},{8,10},{9,11},{10,... | collective-permute-start | bytes 1769480 | tf_op jit(solution)/shard_map/ppermute | solution.py:182
  290.9 38.5 %copy-start.2 = (f32[256,256]{1,0:T(8,128)}, f32[256,256]{1,0:T(8,128)S(1)}, u32[]{:S(2)}) copy-start(f32[256,256]{1,0:T(8,128)S(1)} %dynamic-slice_add_fusion.1) | copy-start | bytes 786436
  290.9 131.5 %collective-permute-start.16 = (bf16[768,3584]{1,0:T(8,128)(2,1)}, bf16[768,3584]{1,0:T(8,128)(2,1)}, u32[]{:S(2)}, u32[]{:S(2)}) collective-permute-start(bf16[768,3584]{1,0:T(8,128)(2,1)} %refs_8_.1), channel_id=1, source_target_pairs={{8,16},{12,20},{16,8},{20,12},{9,17},{13,21},{17,9},{21,13},{10,18... | collective-permute-start | bytes 16515080 | tf_op jit(solution)/shard_map/ppermute | solution.py:198
  294.0 15.2 %collective-permute-start.2 = (f32[256,256]{1,0:T(8,128)S(1)}, f32[256,256]{1,0:T(8,128)S(1)}, u32[]{:S(2)}, u32[]{:S(2)}) collective-permute-start(f32[256,256]{1,0:T(8,128)S(1)} %dynamic-slice_add_fusion.1), channel_id=1, source_target_pairs={{0,1},{1,0},{2,3},{3,2},{4,5},{5,4},{6,7},{7,6},{8,9},{9,8},{10,11... | collective-permute-start | bytes 786440 | tf_op jit(solution)/shard_map/ppermute | solution.py:182
  309.2 20.3 %collective-permute-start.3 = (f32[512,256]{1,0:T(8,128)S(1)}, f32[512,256]{1,0:T(8,128)}, u32[]{:S(2)}, u32[]{:S(2)}) collective-permute-start(f32[512,256]{1,0:T(8,128)S(1)} %maximum_select_fusion.1), channel_id=1, source_target_pairs={{0,2},{1,3},{2,0},{3,1},{4,6},{5,7},{6,4},{7,5},{8,10},{9,11},{10,... | collective-permute-start | bytes 1572872 | tf_op jit(solution)/shard_map/ppermute | solution.py:182
  309.9 70.8 %collective-permute-start.18 = (bf16[192,64]{0,1:T(8,128)(2,1)S(1)}, bf16[192,64]{0,1:T(8,128)(2,1)S(1)}, u32[]{:S(2)}, u32[]{:S(2)}) collective-permute-start(bf16[192,64]{0,1:T(8,128)(2,1)S(1)} %dynamic-slice_convert_fusion), channel_id=1, source_target_pairs={{0,24},{4,28},{8,16},{12,20},{16,8},{20,12},{24,0},{28,4},{1,25},{... | collective-permute-start | bytes 73736 | tf_op jit(solution)/shard_map/ppermute | solution.py:198
  336.9 131.3 %collective-permute-start.23 = (f32[256,2048]{1,0:T(8,128)S(1)}, f32[256,2048]{1,0:T(8,128)}, u32[]{:S(2)}, u32[]{:S(2)}) collective-permute-start(f32[256,2048]{1,0:T(8,128)S(1)} %fusion.49), channel_id=1, source_target_pairs={{0,4},{4,0},{8,12},{12,8},{16,20},{20,16},{24,28},{28,24},{1,5},{5... | collective-permute-start | bytes 6291464 | tf_op jit(solution)/shard_map/ppermute | solution.py:182
  337.0 87.0 %collective-permute-start.17 = (bf16[768,2048]{1,0:T(8,128)(2,1)}, bf16[768,2048]{1,0:T(8,128)(2,1)}, u32[]{:S(2)}, u32[]{:S(2)}) collective-permute-start(bf16[768,2048]{1,0:T(8,128)(2,1)} %slice.66), channel_id=1, source_target_pairs={{0,24},{4,28},{24,0},{28,4},{1,25},{5,29},{25,1},{29,5},{2,26},{6,... | collective-permute-start | bytes 9437192 | tf_op jit(solution)/shard_map/ppermute | solution.py:198
  379.1 90.4 %collective-permute-start.11 = (f32[3,4096]{1,0:T(4,128)S(1)}, f32[3,4096]{1,0:T(4,128)S(1)}, u32[]{:S(2)}, u32[]{:S(2)}) collective-permute-start(f32[3,4096]{1,0:T(4,128)S(1)} %reshape.99), channel_id=1, source_target_pairs={{0,1},{1,0},{2,3},{3,2},{4,5},{5,4},{6,7},{7,6},{8,9},{9,8},{10,11... | collective-permute-start | bytes 147464 | tf_op jit(solution)/shard_map/ppermute | solution.py:182
  388.5 57.3 %collective-permute-start.15 = (bf16[768,1024]{1,0:T(8,128)(2,1)}, bf16[768,1024]{1,0:T(8,128)(2,1)}, u32[]{:S(2)}, u32[]{:S(2)}) collective-permute-start(bf16[768,1024]{1,0:T(8,128)(2,1)} %slice.63), channel_id=1, source_target_pairs={{0,24},{4,28},{24,0},{28,4},{1,25},{5,29},{25,1},{29,5},{2,26},{6,... | collective-permute-start | bytes 4718600 | tf_op jit(solution)/shard_map/ppermute | solution.py:198
  390.9 33.1 %copy-start.3 = (bf16[768,512]{1,0:T(8,128)(2,1)S(1)}, bf16[768,512]{1,0:T(8,128)(2,1)}, u32[]{:S(2)}) copy-start(bf16[768,512]{1,0:T(8,128)(2,1)} %slice.62) | copy-start | bytes 2359300
  422.4 50.4 %collective-permute-start.12 = (f32[3,4096]{1,0:T(4,128)S(1)}, f32[3,4096]{1,0:T(4,128)S(1)}, u32[]{:S(2)}, u32[]{:S(2)}) collective-permute-start(f32[3,4096]{1,0:T(4,128)S(1)} %reshape.99), channel_id=1, source_target_pairs={{0,2},{1,3},{2,0},{3,1},{4,6},{5,7},{6,4},{7,5},{8,10},{9,11},{10,... | collective-permute-start | bytes 147464 | tf_op jit(solution)/shard_map/ppermute | solution.py:182
  424.0 38.0 %collective-permute-start.14 = (bf16[768,512]{1,0:T(8,128)(2,1)S(1)}, bf16[768,512]{1,0:T(8,128)(2,1)S(1)}, u32[]{:S(2)}, u32[]{:S(2)}) collective-permute-start(bf16[768,512]{1,0:T(8,128)(2,1)S(1)} %copy-done.3), channel_id=1, source_target_pairs={{0,24},{4,28},{24,0},{28,4},{1,25},{5,29},{25,1},{29,5},{2,26},{6,... | collective-permute-start | bytes 2359304 | tf_op jit(solution)/shard_map/ppermute | solution.py:198
  445.8 31.9 %collective-permute-start.13 = (f32[3,4096]{1,0:T(4,128)S(1)}, f32[3,4096]{1,0:T(4,128)S(1)}, u32[]{:S(2)}, u32[]{:S(2)}) collective-permute-start(f32[3,4096]{1,0:T(4,128)S(1)} %reshape.99), channel_id=1, source_target_pairs={{0,3},{1,2},{2,1},{3,0},{4,7},{5,6},{6,5},{7,4},{8,11},{9,10},{10,... | collective-permute-start | bytes 147464 | tf_op jit(solution)/shard_map/ppermute | solution.py:182
  464.7 13.0 %collective-permute-start.19 = (f32[3,4096]{1,0:T(4,128)S(1)}, f32[3,4096]{1,0:T(4,128)S(1)}, u32[]{:S(2)}, u32[]{:S(2)}) collective-permute-start(f32[3,4096]{1,0:T(4,128)S(1)} %reshape.102), channel_id=1, source_target_pairs={{0,24},{1,25},{2,26},{3,27},{4,28},{5,29},{6,30},{7,31},{8,16},{9,... | collective-permute-start | bytes 147464 | tf_op jit(solution)/shard_map/ppermute | solution.py:310
  468.1 9.6 %collective-permute-start.20 = (f32[3,4096]{1,0:T(4,128)S(1)}, f32[3,4096]{1,0:T(4,128)S(1)}, u32[]{:S(2)}, u32[]{:S(2)}) collective-permute-start(f32[3,4096]{1,0:T(4,128)S(1)} %reshape.102), channel_id=1, source_target_pairs={{0,25},{1,24},{2,27},{3,26},{4,29},{5,28},{6,31},{7,30},{8,17},{9,... | collective-permute-start | bytes 147464 | tf_op jit(solution)/shard_map/ppermute | solution.py:310
  469.5 8.2 %collective-permute-start.21 = (f32[3,4096]{1,0:T(4,128)S(1)}, f32[3,4096]{1,0:T(4,128)S(1)}, u32[]{:S(2)}, u32[]{:S(2)}) collective-permute-start(f32[3,4096]{1,0:T(4,128)S(1)} %reshape.102), channel_id=1, source_target_pairs={{0,26},{1,27},{2,24},{3,25},{4,30},{5,31},{6,28},{7,29},{8,18},{9,... | collective-permute-start | bytes 147464 | tf_op jit(solution)/shard_map/ppermute | solution.py:310
  472.8 8.0 %collective-permute-start.22 = (f32[3,4096]{1,0:T(4,128)S(1)}, f32[3,4096]{1,0:T(4,128)S(1)}, u32[]{:S(2)}, u32[]{:S(2)}) collective-permute-start(f32[3,4096]{1,0:T(4,128)S(1)} %reshape.102), channel_id=1, source_target_pairs={{0,27},{1,26},{2,25},{3,24},{4,31},{5,30},{6,29},{7,28},{8,19},{9,... | collective-permute-start | bytes 147464 | tf_op jit(solution)/shard_map/ppermute | solution.py:310
  625.9 4.4 collective-permute-start.24
  626.3 5.3 collective-permute-start.25
  628.8 5.8 collective-permute-start.26
  635.4 14.2 %collective-permute-start.27 = (f32[24,256]{1,0:T(8,128)S(1)}, f32[24,256]{1,0:T(8,128)S(1)}, u32[]{:S(2)}, u32[]{:S(2)}) collective-permute-start(f32[24,256]{1,0:T(8,128)S(1)} %add_add_fusion.3), channel_id=1, source_target_pairs={{0,1},{1,0},{2,3},{3,2},{4,5},{5,4},{6,7},{7,6},{8,9},{9,8},{10,11... | collective-permute-start | bytes 73736 | tf_op jit(solution)/shard_map/ppermute | solution.py:182
  635.7 14.0 %collective-permute-start.28 = (f32[24,256]{1,0:T(8,128)S(1)}, f32[24,256]{1,0:T(8,128)S(1)}, u32[]{:S(2)}, u32[]{:S(2)}) collective-permute-start(f32[24,256]{1,0:T(8,128)S(1)} %add_add_fusion.3), channel_id=1, source_target_pairs={{0,2},{1,3},{2,0},{3,1},{4,6},{5,7},{6,4},{7,5},{8,10},{9,11},{10,... | collective-permute-start | bytes 73736 | tf_op jit(solution)/shard_map/ppermute | solution.py:182
  637.4 12.2 %collective-permute-start.29 = (f32[24,256]{1,0:T(8,128)S(1)}, f32[24,256]{1,0:T(8,128)S(1)}, u32[]{:S(2)}, u32[]{:S(2)}) collective-permute-start(f32[24,256]{1,0:T(8,128)S(1)} %add_add_fusion.3), channel_id=1, source_target_pairs={{0,3},{1,2},{2,1},{3,0},{4,7},{5,6},{6,5},{7,4},{8,11},{9,10},{10,... | collective-permute-start | bytes 73736 | tf_op jit(solution)/shard_map/ppermute | solution.py:182
  644.2 6.1 copy-start.1
Sparse Core Ops, SparseCore 0:
  9.8 125.0 all-gather.8
  137.1 27.8 all-gather.6
  213.9 113.5 all-gather.10

commit v11 on v9

--- a/solution.py
+++ b/solution.py
@@ -290,6 +290,8 @@
     down = pair(out_down, in_down)
     up_own = pair(own[:, half:], in_up)
 
+    own, in_up_far = lax.optimization_barrier((own, in_up_far))
+    in_up_far = lax.all_gather(in_up_far, "solve", axis=0, tiled=True)
     grad = gradient(far_idx, cot_far, weights)
     far = None
     for j, a, b, gate_outer in chunks:
@@ -300,9 +302,6 @@
         grad_up = (grad[:, units] * (gate * jax.nn.sigmoid(gate))).astype(jnp.bfloat16)
         term = jnp.dot(grad_up, proj_hidden[units, half:], preferred_element_type=f32)
         far = term if far is None else far + term
-        if j == len(chunks) - 2:
-            far, in_up_far = lax.optimization_barrier((far, in_up_far))
-            in_up_far = lax.all_gather(in_up_far, "solve", axis=0, tiled=True)
     up_far = pair(far, in_up_far.astype(f32))
     query_side = query_side + other_side
     high = lax.reduce_precision(query_side, 8, 7)
@@ -339,7 +338,7 @@
     )(at, both, pick_left, pick_right, *query_side)
     scores = total(scores, "fsdp", n, 2)
     scores = total(scores, "solve", m)
-    block = 128
+    block = 256
     steps = row_width // block
     ends = [0, steps // 2, steps]
     new_gram = None

time: 616 us -> 646 us (1.049)
  blocking collectives: 102 us -> 139 us
    all_gather x1, blocking collectives: 93.5 us -> 130 us  [local(): both = lax.all_gather(jnp.concatenate([up, down], axis=0), 'fsdp', axis=0)]
where the time goes in v11:
time: 646 us; the launch traced here: 645 us
  waiting for transfers between devices  299 us (46%)
  blocking collectives  139 us (22%)
  Pallas kernels  78.1 us (12%)
  starting transfers between devices  51.5 us (8%)
  matrix products  39 us (6%)
  between operations  14.2 us (2%)
  other arithmetic  12.5 us (2%)
  local copies, waits for them, and re-layouts  12.2 us (2%)
    all_gather x1, blocking collectives, local(): both = lax.all_gather(jnp.concatenate([up, down], axis=0), 'fsdp', axis=0)  130 us
    all_gather x1, waiting for transfers between devices, local(): cot_full = lax.all_gather(cotangent, 'solve', axis=1, tiled=True)  122 us
    ppermute x20, waiting for transfers between devices, swap(): return lax.ppermute(x, axis, [(i, i ^ bit) for i in range(size)])  109 us
    ppermute x7, waiting for transfers between devices, mirror(): return lax.ppermute(x, 'fsdp', pairs)  66.8 us
    pallas_call x1, Pallas kernels, tokens(): pl.pallas_call(functools.partial(tokens_kernel, count, len(gate_parts), s...  34.7 us
    pallas_call x1, Pallas kernels, gradient(): pl.pallas_call(functools.partial(grad_kernel, count), out_shape=jax.Shape...  31.4 us
    ppermute x7, starting transfers between devices, mirror(): return lax.ppermute(x, 'fsdp', pairs)  29.2 us
    ppermute x20, starting transfers between devices, swap(): return lax.ppermute(x, axis, [(i, i ^ bit) for i in range(size)])  22.2 us
  transfers between devices with their start and end apart: 30, of which 13 were waited for; matrix products, arithmetic and copies ran while one was open for 10% of the time, Pallas kernels for 12%

profile of v11, /device:TPU:0, one launch (start us, length us, event | category | flops | bytes accessed | tf_op | source)
XLA Modules:
  0.0 645.3 jit_solution(3164208677563224766)
XLA Ops:
  8.0 3.1 collective-permute-start.6
  11.1 1.6 convert_element_type.64
  12.8 122.2 %all-gather.9.cloned.1.call-done.refs_0_.refs_1_.refs_2_.refs_3_ = bf16[768,8192]{1,0:T(8,128)(2,1)} async-done(((bf16[768,2048]{1,0:T(8,128)(2,1)}), bf16[768,8192]{1,0:T(8,128)(2,1)}) %all-gather.9.cloned.1.call-update) | async-done | bytes 12582928 | tf_op jit(solution)/shard_map/all_gather | solution.py:210
  135.0 1.5 dynamic_slice.22
  136.5 3.4 collective-permute-start.4
  139.9 38.3 %collective-permute-done.6.refs_6_ = bf16[3584,1024]{1,0:T(8,128)(2,1)} collective-permute-done((bf16[3584,1024]{1,0:T(8,128)(2,1)}, bf16[3584,1024]{1,0:T(8,128)(2,1)}, u32[]{:S(2)}, u32[]{:S(2)}) %collective-permute-start.6) | collective-permute-done | bytes 7340064 | tf_op jit(solution)/shard_map/ppermute | solution.py:182
  178.2 35.6 %collective-permute-done.4 = bf16[192,4096]{1,0:T(8,128)(2,1)} collective-permute-done((bf16[192,4096]{1,0:T(8,128)(2,1)S(1)}, bf16[192,4096]{1,0:T(8,128)(2,1)}, u32[]{:S(2)}, u32[]{:S(2)}) %collective-permute-start.4) | collective-permute-done | bytes 1572896 | tf_op jit(solution)/shard_map/ppermute | solution.py:198
  213.9 3.1 fusion.20
  217.0 2.2 fusion.18
  219.2 7.5 %fusion.6 = f32[768,64]{0,1:T(8,128)S(1)} fusion(bf16[768,3584]{1,0:T(8,128)(2,1)} %param.14, bf16[768,3584]{1,0:T(8,128)(2,1)} %refs_8_.1, bf16[3584,128]{1,0:T(8,128)(2,1)S(1)} %copy-done.4), kind=kOutput, calls=%fused_computation.9 | convolution fusion | flops 374341632 | bytes 12124160 | tf_op jit(solution)/shard_map/dot_general | solution.py:233
  226.8 6.0 fusion.48
  235.0 2.2 collective-permute-start.10
  237.4 29.9 %collective-permute-done = f32[512,256]{1,0:T(8,128)} collective-permute-done((f32[512,256]{1,0:T(8,128)S(1)}, f32[512,256]{1,0:T(8,128)}, u32[]{:S(2)}, u32[]{:S(2)}) %collective-permute-start) | collective-permute-done | bytes 524320 | tf_op jit(solution)/shard_map/ppermute | solution.py:182
  268.4 1.5 collective-permute-start.1
  269.9 11.4 %collective-permute-done.1 = f32[256,256]{1,0:T(8,128)S(1)} collective-permute-done((f32[256,256]{1,0:T(8,128)S(1)}, f32[256,256]{1,0:T(8,128)S(1)}, u32[]{:S(2)}, u32[]{:S(2)}) %collective-permute-start.1) | collective-permute-done | bytes 262176 | tf_op jit(solution)/shard_map/ppermute | solution.py:182
  281.3 2.5 collective-permute-start.8
  284.4 2.1 slice.62
  286.4 2.7 slice.63
  289.1 4.0 slice.66
  294.5 3.0 collective-permute-start.13
  297.6 13.1 %collective-permute-done.8 = f32[768,192]{0,1:T(8,128)} collective-permute-done((f32[768,192]{0,1:T(8,128)S(1)}, f32[768,192]{0,1:T(8,128)}, u32[]{:S(2)}, u32[]{:S(2)}) %collective-permute-start.8) | collective-permute-done | bytes 589856 | tf_op jit(solution)/shard_map/ppermute | solution.py:182
  310.7 1.4 add_add_fusion
  312.1 8.0 %collective-permute-done.2 = f32[256,256]{1,0:T(8,128)S(1)} collective-permute-done((f32[256,256]{1,0:T(8,128)S(1)}, f32[256,256]{1,0:T(8,128)S(1)}, u32[]{:S(2)}, u32[]{:S(2)}) %collective-permute-start.2) | collective-permute-done | bytes 262176 | tf_op jit(solution)/shard_map/ppermute | solution.py:182
  320.8 3.6 collective-permute-start.15
  324.3 5.1 collective-permute-done.3
  330.8 6.1 fusion.49
  337.0 7.9 %collective-permute-start.14 = (bf16[768,2048]{1,0:T(8,128)(2,1)}, bf16[768,2048]{1,0:T(8,128)(2,1)}, u32[]{:S(2)}, u32[]{:S(2)}) collective-permute-start(bf16[768,2048]{1,0:T(8,128)(2,1)} %slice.66), channel_id=1, source_target_pairs={{0,24},{4,28},{24,0},{28,4},{1,25},{5,29},{25,1},{29,5},{2,26},{6,... | collective-permute-start | bytes 9437192 | tf_op jit(solution)/shard_map/ppermute | solution.py:198
  344.9 34.7 %shard_map.130 = f32[768,128]{1,0:T(8,128)} custom-call(s32[4]{0:T(128)} %get-tuple-element.16.idx, bf16[768,8192]{1,0:T(8,128)(2,1)} %all-gather.9.cloned.1.call-done.refs_0_.refs_1_.refs_2_.refs_3_, bf16[768,8192]{1,0:T(8,128)(2,1)} %all-gather.9.cloned.1.call-done.refs_0_.refs_1_.refs_2_.refs_3_, ...), custom_call_target="tpu_custom_call" | custom-call | flops 23957864448 | bytes 46661632 | tf_op jit(solution)/shard_map/pallas_call | solution.py:64
  380.8 1.9 collective-permute-start.11
  382.7 5.7 collective-permute-start.12
  388.4 8.6 %all-gather.1 = bf16[4,192,64]{1,2,0:T(8,128)(2,1)S(1)} all-gather(bf16[1,192,64]{1,2,0:T(8,128)(2,1)S(1)} %bitcast.40), channel_id=1, replica_groups=mesh['fsdp'=8,'solve'=4] {'solve'}, dimensions={0}, use_global_device_ids=true | all-gather | bytes 122880 | tf_op jit(solution)/shard_map/all_gather | solution.py:294
  397.4 31.4 %shard_map.131 = f32[768,3584]{1,0:T(8,128)} custom-call(s32[4]{0:T(128)} %get-tuple-element.29.idx, bf16[768,4096]{1,0:T(8,128)(2,1)} %all-gather.11.cloned.1.call-done.refs_0_.refs_1_.refs_2_.refs_3_, bf16[768,4096]{1,0:T(8,128)(2,1)} %all-gather.11.cloned.1.call-done.refs_0_.refs_1_.refs_2_.refs_3_, ...), custom_call_target="tpu_custom_call" | custom-call | flops 22548578304 | bytes 46661632 | tf_op jit(solution)/shard_map/pallas_call | solution.py:105
  428.8 6.1 fusion.9
  434.9 29.6 %collective-permute-done.12 = bf16[768,1024]{1,0:T(8,128)(2,1)} collective-permute-done((bf16[768,1024]{1,0:T(8,128)(2,1)}, bf16[768,1024]{1,0:T(8,128)(2,1)}, u32[]{:S(2)}, u32[]{:S(2)}) %collective-permute-start.12) | collective-permute-done | bytes 1572896 | tf_op jit(solution)/shard_map/ppermute | solution.py:198
  464.4 4.1 fusion.13
  468.6 2.6 convolution_add_fusion
  471.5 3.6 collective-permute-start.16
  476.0 1.6 collective-permute-done.16
  478.0 2.8 collective-permute-start.19
  481.2 3.4 fusion.11
  485.2 130.1 %all-gather.2.both = f32[8,6,4096]{2,1,0:T(8,128)} all-gather(f32[1,6,4096]{2,1,0:T(8,128)S(1)} %maximum_bitcast_fusion), channel_id=2, replica_groups=mesh['fsdp'=8,'solve'=4] {'fsdp'}, dimensions={0}, use_global_device_ids=true | all-gather | bytes 884736 | tf_op jit(solution)/shard_map/all_gather | solution.py:311
  615.2 3.6 shard_map.132
  620.9 1.4 collective-permute-start.21
  622.4 1.7 collective-permute-done.22
  624.0 1.4 collective-permute-done.23
  627.4 1.5 collective-permute-start.26
  629.7 4.1 shard_map.133.refs_0_
  633.8 4.3 shard_map.134
  (80 shorter events, 17.8 us)
Async XLA Ops:
  7.2 209.9 %copy-start = (bf16[768,2048]{1,0:T(8,128)(2,1)S(1)}, bf16[768,2048]{1,0:T(8,128)(2,1)}, u32[]{:S(2)}) copy-start(bf16[768,2048]{1,0:T(8,128)(2,1)} %param.11) | copy-start | bytes 9437188
  7.2 127.8 %all-gather.9.cloned.1.call-start = ((), (), s32[]{:S(2)}) async-start(), calls=%async_computation.1 | async-start | bytes 15728640 | tf_op jit(solution)/shard_map/all_gather | solution.py:210
  7.9 218.8 %all-gather.7.cloned.1.call-start = ((), (), s32[]{:S(2)}) async-start(), calls=%async_computation | async-start | bytes 1179648 | tf_op jit(solution)/shard_map/all_gather | solution.py:241
  8.0 170.2 %collective-permute-start.6 = (bf16[3584,1024]{1,0:T(8,128)(2,1)}, bf16[3584,1024]{1,0:T(8,128)(2,1)}, u32[]{:S(2)}, u32[]{:S(2)}) collective-permute-start(bf16[3584,1024]{1,0:T(8,128)(2,1)} %refs_4_.3), channel_id=1, source_target_pairs={{0,8},{4,12},{8,0},{12,4},{16,24},{20,28},{24,16},{28,20},{1,9},{5... | collective-permute-start | bytes 22020104 | tf_op jit(solution)/shard_map/ppermute | solution.py:182
  12.7 384.6 %all-gather.11.cloned.1.call-start = ((), (), s32[]{:S(2)}) async-start(), calls=%async_computation.2 | async-start | bytes 7864320 | tf_op jit(solution)/shard_map/all_gather | solution.py:215
  136.5 77.3 %collective-permute-start.4 = (bf16[192,4096]{1,0:T(8,128)(2,1)S(1)}, bf16[192,4096]{1,0:T(8,128)(2,1)}, u32[]{:S(2)}, u32[]{:S(2)}) collective-permute-start(bf16[192,4096]{1,0:T(8,128)(2,1)S(1)} %dynamic_slice.22), channel_id=1, source_target_pairs={{0,24},{4,28},{8,16},{12,20},{16,8},{20,12},{24,0},{28,4},{1,25},{... | collective-permute-start | bytes 4718600 | tf_op jit(solution)/shard_map/ppermute | solution.py:198
  139.9 197.1 %collective-permute-start.5 = (bf16[3584,1024]{1,0:T(8,128)(2,1)}, bf16[3584,1024]{1,0:T(8,128)(2,1)}, u32[]{:S(2)}, u32[]{:S(2)}) collective-permute-start(bf16[3584,1024]{1,0:T(8,128)(2,1)} %refs_4_.3), channel_id=1, source_target_pairs={{0,4},{4,0},{8,12},{12,8},{16,20},{20,16},{24,28},{28,24},{1,5},{5... | collective-permute-start | bytes 22020104 | tf_op jit(solution)/shard_map/ppermute | solution.py:182
  178.2 166.7 %collective-permute-start.7 = (bf16[3584,1024]{1,0:T(8,128)(2,1)}, bf16[3584,1024]{1,0:T(8,128)(2,1)}, u32[]{:S(2)}, u32[]{:S(2)}) collective-permute-start(bf16[3584,1024]{1,0:T(8,128)(2,1)} %collective-permute-done.6.refs_6_), channel_id=1, source_target_pairs={{0,4},{4,0},{8,12},{12,8},{16,20},{20,16},{24,28},{28,24},{1,5},{5... | collective-permute-start | bytes 22020104 | tf_op jit(solution)/shard_map/ppermute | solution.py:182
  213.9 5.4 copy-start.4
  226.7 10.6 %copy-start.3 = (s32[3]{0:T(128)S(1)}, s32[3]{0:T(128)}, u32[]{:S(2)}) copy-start(s32[3]{0:T(128)} %param.18) | copy-start | bytes 40
  232.8 34.5 %collective-permute-start = (f32[512,256]{1,0:T(8,128)S(1)}, f32[512,256]{1,0:T(8,128)}, u32[]{:S(2)}, u32[]{:S(2)}) collective-permute-start(f32[512,256]{1,0:T(8,128)S(1)} %constant_dynamic-slice_fusion.1), channel_id=1, source_target_pairs={{0,2},{1,3},{2,0},{3,1},{4,6},{5,7},{6,4},{7,5},{8,10},{9,11},{10,... | collective-permute-start | bytes 1572872 | tf_op jit(solution)/shard_map/ppermute | solution.py:182
  234.2 60.3 %collective-permute-start.9 = (f32[768,192]{0,1:T(8,128)S(1)}, f32[768,192]{0,1:T(8,128)S(1)}, u32[]{:S(2)}, u32[]{:S(2)}) collective-permute-start(f32[768,192]{0,1:T(8,128)S(1)} %pad_maximum_fusion), channel_id=1, source_target_pairs={{0,2},{1,3},{2,0},{3,1},{4,6},{5,7},{6,4},{7,5},{8,10},{9,11},{10,... | collective-permute-start | bytes 1769480 | tf_op jit(solution)/shard_map/ppermute | solution.py:182
  235.0 62.5 %collective-permute-start.10 = (f32[768,192]{0,1:T(8,128)S(1)}, f32[768,192]{0,1:T(8,128)}, u32[]{:S(2)}, u32[]{:S(2)}) collective-permute-start(f32[768,192]{0,1:T(8,128)S(1)} %pad_maximum_fusion), channel_id=1, source_target_pairs={{0,3},{1,2},{2,1},{3,0},{4,7},{5,6},{6,5},{7,4},{8,11},{9,10},{10,... | collective-permute-start | bytes 1769480 | tf_op jit(solution)/shard_map/ppermute | solution.py:182
  268.4 12.9 %collective-permute-start.1 = (f32[256,256]{1,0:T(8,128)S(1)}, f32[256,256]{1,0:T(8,128)S(1)}, u32[]{:S(2)}, u32[]{:S(2)}) collective-permute-start(f32[256,256]{1,0:T(8,128)S(1)} %constant_dynamic-slice_fusion), channel_id=1, source_target_pairs={{0,1},{1,0},{2,3},{3,2},{4,5},{5,4},{6,7},{7,6},{8,9},{9,8},{10,11... | collective-permute-start | bytes 786440 | tf_op jit(solution)/shard_map/ppermute | solution.py:182
  281.3 29.4 %collective-permute-start.8 = (f32[768,192]{0,1:T(8,128)S(1)}, f32[768,192]{0,1:T(8,128)}, u32[]{:S(2)}, u32[]{:S(2)}) collective-permute-start(f32[768,192]{0,1:T(8,128)S(1)} %pad_maximum_fusion), channel_id=1, source_target_pairs={{0,1},{1,0},{2,3},{3,2},{4,5},{5,4},{6,7},{7,6},{8,9},{9,8},{10,11... | collective-permute-start | bytes 1769480 | tf_op jit(solution)/shard_map/ppermute | solution.py:182
  294.5 35.0 %copy-start.2 = (f32[256,256]{1,0:T(8,128)}, f32[256,256]{1,0:T(8,128)S(1)}, u32[]{:S(2)}) copy-start(f32[256,256]{1,0:T(8,128)S(1)} %dynamic-slice_add_fusion.1) | copy-start | bytes 786436
  294.5 134.3 %collective-permute-start.13 = (bf16[768,3584]{1,0:T(8,128)(2,1)}, bf16[768,3584]{1,0:T(8,128)(2,1)}, u32[]{:S(2)}, u32[]{:S(2)}) collective-permute-start(bf16[768,3584]{1,0:T(8,128)(2,1)} %refs_8_.1), channel_id=1, source_target_pairs={{8,16},{12,20},{16,8},{20,12},{9,17},{13,21},{17,9},{21,13},{10,18... | collective-permute-start | bytes 16515080 | tf_op jit(solution)/shard_map/ppermute | solution.py:198
  297.6 22.5 %collective-permute-start.2 = (f32[256,256]{1,0:T(8,128)S(1)}, f32[256,256]{1,0:T(8,128)S(1)}, u32[]{:S(2)}, u32[]{:S(2)}) collective-permute-start(f32[256,256]{1,0:T(8,128)S(1)} %dynamic-slice_add_fusion.1), channel_id=1, source_target_pairs={{0,1},{1,0},{2,3},{3,2},{4,5},{5,4},{6,7},{7,6},{8,9},{9,8},{10,11... | collective-permute-start | bytes 786440 | tf_op jit(solution)/shard_map/ppermute | solution.py:182
  320.1 9.4 %collective-permute-start.3 = (f32[512,256]{1,0:T(8,128)S(1)}, f32[512,256]{1,0:T(8,128)}, u32[]{:S(2)}, u32[]{:S(2)}) collective-permute-start(f32[512,256]{1,0:T(8,128)S(1)} %maximum_select_fusion.1), channel_id=1, source_target_pairs={{0,2},{1,3},{2,0},{3,1},{4,6},{5,7},{6,4},{7,5},{8,10},{9,11},{10,... | collective-permute-start | bytes 1572872 | tf_op jit(solution)/shard_map/ppermute | solution.py:182
  320.8 61.9 %collective-permute-start.15 = (bf16[192,64]{0,1:T(8,128)(2,1)S(1)}, bf16[192,64]{0,1:T(8,128)(2,1)S(1)}, u32[]{:S(2)}, u32[]{:S(2)}) collective-permute-start(bf16[192,64]{0,1:T(8,128)(2,1)S(1)} %dynamic-slice_convert_fusion), channel_id=1, source_target_pairs={{0,24},{4,28},{8,16},{12,20},{16,8},{20,12},{24,0},{28,4},{1,25},{... | collective-permute-start | bytes 73736 | tf_op jit(solution)/shard_map/ppermute | solution.py:198
  336.9 144.3 %collective-permute-start.20 = (f32[256,2048]{1,0:T(8,128)S(1)}, f32[256,2048]{1,0:T(8,128)}, u32[]{:S(2)}, u32[]{:S(2)}) collective-permute-start(f32[256,2048]{1,0:T(8,128)S(1)} %fusion.49), channel_id=1, source_target_pairs={{0,4},{4,0},{8,12},{12,8},{16,20},{20,16},{24,28},{28,24},{1,5},{5... | collective-permute-start | bytes 6291464 | tf_op jit(solution)/shard_map/ppermute | solution.py:182
  337.0 91.8 %collective-permute-start.14 = (bf16[768,2048]{1,0:T(8,128)(2,1)}, bf16[768,2048]{1,0:T(8,128)(2,1)}, u32[]{:S(2)}, u32[]{:S(2)}) collective-permute-start(bf16[768,2048]{1,0:T(8,128)(2,1)} %slice.66), channel_id=1, source_target_pairs={{0,24},{4,28},{24,0},{28,4},{1,25},{5,29},{25,1},{29,5},{2,26},{6,... | collective-permute-start | bytes 9437192 | tf_op jit(solution)/shard_map/ppermute | solution.py:198
  380.8 87.8 %collective-permute-start.11 = (bf16[768,512]{1,0:T(8,128)(2,1)}, bf16[768,512]{1,0:T(8,128)(2,1)}, u32[]{:S(2)}, u32[]{:S(2)}) collective-permute-start(bf16[768,512]{1,0:T(8,128)(2,1)} %slice.62), channel_id=1, source_target_pairs={{0,24},{4,28},{24,0},{28,4},{1,25},{5,29},{25,1},{29,5},{2,26},{6,... | collective-permute-start | bytes 2359304 | tf_op jit(solution)/shard_map/ppermute | solution.py:198
  382.7 81.7 %collective-permute-start.12 = (bf16[768,1024]{1,0:T(8,128)(2,1)}, bf16[768,1024]{1,0:T(8,128)(2,1)}, u32[]{:S(2)}, u32[]{:S(2)}) collective-permute-start(bf16[768,1024]{1,0:T(8,128)(2,1)} %slice.63), channel_id=1, source_target_pairs={{0,24},{4,28},{24,0},{28,4},{1,25},{5,29},{25,1},{29,5},{2,26},{6,... | collective-permute-start | bytes 4718600 | tf_op jit(solution)/shard_map/ppermute | solution.py:198
  471.5 6.1 collective-permute-start.16
  477.6 7.0 %collective-permute-start.18 = (f32[3,4096]{1,0:T(4,128)S(1)}, f32[3,4096]{1,0:T(4,128)S(1)}, u32[]{:S(2)}, u32[]{:S(2)}) collective-permute-start(f32[3,4096]{1,0:T(4,128)S(1)} %add.179), channel_id=1, source_target_pairs={{0,2},{1,3},{2,0},{3,1},{4,6},{5,7},{6,4},{7,5},{8,10},{9,11},{10,... | collective-permute-start | bytes 147464 | tf_op jit(solution)/shard_map/ppermute | solution.py:182
  478.0 6.7 %collective-permute-start.19 = (f32[3,4096]{1,0:T(4,128)S(1)}, f32[3,4096]{1,0:T(4,128)S(1)}, u32[]{:S(2)}, u32[]{:S(2)}) collective-permute-start(f32[3,4096]{1,0:T(4,128)S(1)} %add.179), channel_id=1, source_target_pairs={{0,3},{1,2},{2,1},{3,0},{4,7},{5,6},{6,5},{7,4},{8,11},{9,10},{10,... | collective-permute-start | bytes 147464 | tf_op jit(solution)/shard_map/ppermute | solution.py:182
  480.8 4.3 collective-permute-start.17
  618.9 5.1 collective-permute-start.22
  619.6 5.8 collective-permute-start.23
  620.9 4.5 collective-permute-start.21
  626.2 11.9 %collective-permute-start.25 = (f32[24,256]{1,0:T(8,128)S(1)}, f32[24,256]{1,0:T(8,128)S(1)}, u32[]{:S(2)}, u32[]{:S(2)}) collective-permute-start(f32[24,256]{1,0:T(8,128)S(1)} %add_add_fusion.3), channel_id=1, source_target_pairs={{0,2},{1,3},{2,0},{3,1},{4,6},{5,7},{6,4},{7,5},{8,10},{9,11},{10,... | collective-permute-start | bytes 73736 | tf_op jit(solution)/shard_map/ppermute | solution.py:182
  627.4 10.6 %collective-permute-start.26 = (f32[24,256]{1,0:T(8,128)S(1)}, f32[24,256]{1,0:T(8,128)S(1)}, u32[]{:S(2)}, u32[]{:S(2)}) collective-permute-start(f32[24,256]{1,0:T(8,128)S(1)} %add_add_fusion.3), channel_id=1, source_target_pairs={{0,3},{1,2},{2,1},{3,0},{4,7},{5,6},{6,5},{7,4},{8,11},{9,10},{10,... | collective-permute-start | bytes 73736 | tf_op jit(solution)/shard_map/ppermute | solution.py:182
  628.9 9.2 %collective-permute-start.24 = (f32[24,256]{1,0:T(8,128)S(1)}, f32[24,256]{1,0:T(8,128)S(1)}, u32[]{:S(2)}, u32[]{:S(2)}) collective-permute-start(f32[24,256]{1,0:T(8,128)S(1)} %add_add_fusion.3), channel_id=1, source_target_pairs={{0,1},{1,0},{2,3},{3,2},{4,5},{5,4},{6,7},{7,6},{8,9},{9,8},{10,11... | collective-permute-start | bytes 73736 | tf_op jit(solution)/shard_map/ppermute | solution.py:182
  633.8 4.9 copy-start.1
Sparse Core Ops, SparseCore 0:
  9.8 125.0 all-gather.8
  137.1 27.8 all-gather.6
  213.9 113.4 all-gather.10
